TPU v7x, 128 devices: a whole 4x4x4 slice. The times are simulated.
128 devices in a mesh: grp: 4 (over z), list: 32 (over y, x, core).
Axes of the slice: x: 4, y: 4, z: 4, core: 2. Of those that a mesh axis runs over, the one named last changes fastest.
Arguments:
- vectors: bfloat16 [3, 65536, 1024], P(None, ('grp', 'list')), may hold values from -6 to 6
- owner_route: int32 [3, 65536, 1], P(None, ('grp', 'list')), may hold values from 0 to 31; in each aligned block of 512 rows (0 to 511, 512 to 1023, ..., all dimensions but the last counted through in order) at most 32 rows name the same one
- list_slot: int32 [3, 65536], P(None, ('grp', 'list')), may hold values from 0 to 1023
- centroids: float32 [32768, 1024], P('list'), may hold values from -6 to 6
- counts: int32 [32768], P('list'), may hold values from 1 to 8
Outputs:
- residuals: bfloat16 [3, 65536, 1024], P(None, ('grp', 'list'))
- new_centroids: float32 [32768, 1024], P('list')
Inputs may be any that keep to these rules, and one draw needn't show every extreme that they name: `owner_route`: within the rows of one device for one step, at most 32 vectors name the same owner; some owner is named exactly 32 times.
All inputs are finite; a program needn't handle non-finite values.
Results may differ from a plain program's by a relative error of at most 0.0035.
Values may be sent and summed in bfloat16 or wider, within the bound.
No kernel may reach another device: no remote copies, remote signals or barrier semaphores. Data moves between devices by JAX's collectives and lax.ppermute only.
A program may use at most 128 MiB of HBM per device.

v0:
```python
import jax
import jax.numpy as jnp
from jax import lax
from jax.sharding import PartitionSpec as P

STEPS = 3


def list_sums(slots, rows, list_dev):
    one_hot = (jnp.arange(list_dev, dtype=jnp.int32)[:, None] == slots[None, :]).astype(
        jnp.bfloat16
    )
    sums = jnp.dot(one_hot, rows, preferred_element_type=jnp.float32)
    return (sums, jnp.sum(one_hot, axis=1, dtype=jnp.float32))


def local(vectors, owner_route, list_slot, centroids, counts):
    owner_count = lax.axis_size("list")
    row_count = vectors.shape[1]
    width = vectors.shape[2]
    capacity = 2 * row_count // owner_count
    list_dev = centroids.shape[0]
    current = centroids
    weights = counts.astype(jnp.float32)
    outputs = []
    for step_index in range(STEPS):
        owner_ids = owner_route[step_index, :, 0]
        slot_ids = list_slot[step_index]
        owner_hits = (
            owner_ids[:, None] == jnp.arange(owner_count, dtype=jnp.int32)[None, :]
        ).astype(jnp.int32)
        rank_rows = jnp.sum((jnp.cumsum(owner_hits, axis=0) - owner_hits) * owner_hits, axis=1)
        dest_rows = owner_ids * capacity + rank_rows
        send_rows = (
            jnp.zeros((owner_count * capacity, width), jnp.bfloat16)
            .at[dest_rows]
            .set(vectors[step_index])
        )
        send_rows = send_rows.reshape(owner_count, capacity, width)
        send_slots = jnp.full((owner_count * capacity,), -1, jnp.int32).at[dest_rows].set(slot_ids)
        send_slots = send_slots.reshape(owner_count, capacity)
        table = current

        def route_fn(pieces, table=table):
            vec_rows, list_ids = pieces
            chosen = table[jnp.clip(list_ids, 0, list_dev - 1)]
            residual_rows = (vec_rows.astype(jnp.float32) - chosen).astype(jnp.bfloat16)
            back_rows = lax.all_to_all(
                residual_rows, "list", split_axis=0, concat_axis=0, tiled=True
            )
            return (back_rows, vec_rows, list_ids)

        back_rows, recv_rows, recv_slots = route_fn(
            (
                lax.all_to_all(send_rows, "list", split_axis=0, concat_axis=0, tiled=True),
                lax.all_to_all(send_slots, "list", split_axis=0, concat_axis=0, tiled=True),
            )
        )
        outputs.append(back_rows.reshape(owner_count * capacity, width)[dest_rows])
        flat_rows = recv_rows.reshape(-1, width)
        flat_slots = recv_slots.reshape(-1)
        sums, batch_count = list_sums(flat_slots, flat_rows, list_dev)
        total_sums, total_count = (
            lax.psum(sums.astype(jnp.bfloat16), "grp").astype(jnp.float32),
            lax.psum(batch_count.astype(jnp.bfloat16), "grp").astype(jnp.float32),
        )
        current = (weights[:, None] * current + total_sums) / (weights + total_count)[:, None]
        weights = weights + total_count
    return (jnp.stack(outputs, axis=0), current)


def solution(mesh):
    in_specs = (
        P(None, ("grp", "list"), None),
        P(None, ("grp", "list"), None),
        P(None, ("grp", "list")),
        P("list", None),
        P("list"),
    )
    out_specs = (P(None, ("grp", "list"), None), P("list", None))
    return jax.shard_map(local, mesh=mesh, in_specs=in_specs, out_specs=out_specs, check_vma=False)
```

profile of v0, /device:TPU:2, one launch (start us, length us, event | category | flops | bytes accessed | tf_op | source)
XLA Modules:
  0.0 395.2 jit_solution(9526469417952136260)
XLA Ops:
  17.2 7.6 %all-to-all-start.4 = ((s32[32,1,32]{2,1,0:T(1,128)}), s32[32,1,32]{2,1,0:T(1,128)S(1)}, u32[]{:S(2)}, u32[]{:S(2)}) async-start(s32[32,1,32]{2,1,0:T(1,128)} %all_to_all.41), calls=%async_computation.4 | async-start | bytes 32768 | tf_op jit(solution)/shard_map/all_to_all | solution.py:56
  30.9 5.0 %all-to-all-start.7 = ((s32[32,1,32]{2,1,0:T(1,128)}), s32[32,1,32]{2,1,0:T(1,128)S(1)}, u32[]{:S(2)}, u32[]{:S(2)}) async-start(s32[32,1,32]{2,1,0:T(1,128)} %all_to_all.45), calls=%async_computation.7 | async-start | bytes 32768 | tf_op jit(solution)/shard_map/all_to_all | solution.py:56
  53.3 6.1 %all-to-all-start.3 = ((bf16[32,32,1024]{2,1,0:T(8,128)(2,1)}), bf16[32,32,1024]{2,1,0:T(8,128)(2,1)S(1)}, u32[]{:S(2)}, u32[]{:S(2)}) async-start(bf16[32,32,1024]{2,1,0:T(8,128)(2,1)} %bitcast.22), calls=%async_computation.3 | async-start | bytes 4194304 | tf_op jit(solution)/shard_map/all_to_all | solution.py:55
  64.2 23.0 %all-to-all-done.3 = bf16[32,32,1024]{2,1,0:T(8,128)(2,1)S(1)} async-done(((bf16[32,32,1024]{2,1,0:T(8,128)(2,1)}), bf16[32,32,1024]{2,1,0:T(8,128)(2,1)S(1)}, u32[]{:S(2)}, u32[]{:S(2)}) %all-to-all-start.3) | async-done | bytes 2097184 | tf_op jit(solution)/shard_map/all_to_all | solution.py:55
  87.3 6.7 %all-to-all-start.6 = ((bf16[32,32,1024]{2,1,0:T(8,128)(2,1)}), bf16[32,32,1024]{2,1,0:T(8,128)(2,1)}, u32[]{:S(2)}, u32[]{:S(2)}) async-start(bf16[32,32,1024]{2,1,0:T(8,128)(2,1)} %bitcast.37), calls=%async_computation.6 | async-start | bytes 4194304 | tf_op jit(solution)/shard_map/all_to_all | solution.py:55
  98.7 23.2 %all-to-all-done.6 = bf16[32,32,1024]{2,1,0:T(8,128)(2,1)} async-done(((bf16[32,32,1024]{2,1,0:T(8,128)(2,1)}), bf16[32,32,1024]{2,1,0:T(8,128)(2,1)}, u32[]{:S(2)}, u32[]{:S(2)}) %all-to-all-start.6) | async-done | bytes 2097184 | tf_op jit(solution)/shard_map/all_to_all | solution.py:55
  122.0 6.7 %all-to-all-start = ((bf16[32,32,1024]{2,1,0:T(8,128)(2,1)}), bf16[32,32,1024]{2,1,0:T(8,128)(2,1)}, u32[]{:S(2)}, u32[]{:S(2)}) async-start(bf16[32,32,1024]{2,1,0:T(8,128)(2,1)} %bitcast.7), calls=%async_computation | async-start | bytes 4194304 | tf_op jit(solution)/shard_map/all_to_all | solution.py:55
  135.2 5.3 %fusion.14 = bf16[1024,1024]{1,0:T(8,128)(2,1)} fusion(bf16[1024,1024]{1,0:T(8,128)(2,1)} %bitcast.45, s32[1024]{0:T(1024)S(1)} %eq.153), kind=kOutput, calls=%fused_computation.36 | convolution fusion | flops 2149580800 | bytes 4198400 | tf_op jit(solution)/shard_map/dot_general | solution.py:13
  140.5 16.2 %all-to-all-done = bf16[32,32,1024]{2,1,0:T(8,128)(2,1)} async-done(((bf16[32,32,1024]{2,1,0:T(8,128)(2,1)}), bf16[32,32,1024]{2,1,0:T(8,128)(2,1)}, u32[]{:S(2)}, u32[]{:S(2)}) %all-to-all-start) | async-done | bytes 2097184 | tf_op jit(solution)/shard_map/all_to_all | solution.py:55
  156.7 5.2 %fusion.12 = bf16[1024,1024]{1,0:T(8,128)(2,1)} fusion(bf16[1024,1024]{1,0:T(8,128)(2,1)} %bitcast.23, s32[1024]{0:T(1024)S(1)} %eq.137), kind=kOutput, calls=%fused_computation.34 | convolution fusion | flops 2149580800 | bytes 4198400 | tf_op jit(solution)/shard_map/dot_general | solution.py:13
  162.8 8.5 %gather_fusion = f32[1024,1024]{1,0:T(8,128)} fusion(f32[1024,1024]{1,0:T(8,128)} %param.8, s32[1024]{0:T(1024)S(1)} %broadcast_clamp_fusion.2), kind=kCustom, calls=%fused_computation | custom fusion | bytes 8392704 | tf_op jit(solution)/shard_map/gather | solution.py:46
  172.8 12.2 %all-reduce = (bf16[1024]{0:T(1024)(128)(2,1)S(1)}, bf16[1024]{0:T(1024)(128)(2,1)S(1)}, bf16[1024]{0:T(1024)(128)(2,1)S(1)}) all-reduce(bf16[1024]{0:T(1024)(128)(2,1)S(1)} %get-tuple-element.25, bf16[1024]{0:T(1024)(128)(2,1)S(1)} %get-tuple-element.26, bf16[1024]{0:T(1024)(128)(2,1)S(1)} %fusion.8), channel_id=1, replica_groups=mesh['grp'=4,'list'=32] {'grp'}, use_global_device_ids=true, to_apply=%region_11.12 | all-reduce | flops 3072 | bytes 12288 | tf_op jit(solution)/shard_map/psum | solution.py:65
  185.0 5.0 %subtract_convert_fusion.2 = bf16[32,32,1024]{2,1,0:T(8,128)(2,1)} fusion(f32[32,32,1024]{2,1,0:T(8,128)} %bitcast.133, bf16[32,32,1024]{2,1,0:T(8,128)(2,1)} %all-to-all-done), kind=kLoop, calls=%fused_computation.26 | loop fusion | flops 3145728 | bytes 8388608 | tf_op jit(solution)/shard_map/convert_element_type | solution.py:47
  190.0 6.2 %all-to-all-start.2 = ((bf16[32,32,1024]{2,1,0:T(8,128)(2,1)}), bf16[32,32,1024]{2,1,0:T(8,128)(2,1)S(1)}, u32[]{:S(2)}, u32[]{:S(2)}) async-start(bf16[32,32,1024]{2,1,0:T(8,128)(2,1)} %subtract_convert_fusion.2), calls=%async_computation.2 | async-start | bytes 4194304 | tf_op jit(solution)/shard_map/all_to_all | solution.py:48
  196.2 93.4 %all-reduce.4.cloned.1.call-done = (bf16[1024,1024]{1,0:T(8,128)(2,1)}, bf16[1024,1024]{1,0:T(8,128)(2,1)}, bf16[1024,1024]{1,0:T(8,128)(2,1)}) async-done(((bf16[1024,1024]{1,0:T(8,128)(2,1)}, bf16[1024,1024]{1,0:T(8,128)(2,1)}, bf16[1024,1024]{1,0:T(8,128)(2,1)}), (bf16[1024,1024]{1,0:T(8,128)(2,1)}, bf16[1024,1024]{1,0:T(8,128)(2,1)}, bf16[1024,1024]{1,0:T(8,128)(2,1)})) %all-reduce.4.cloned.1.call-update) | async-done | bytes 6291472 | tf_op jit(solution)/shard_map/psum | solution.py:64
  289.6 8.4 %add_divide_fusion = (f32[1024,1024]{1,0:T(8,128)}, f32[1024,1024]{1,0:T(8,128)}, f32[1024,1024]{1,0:T(8,128)}) fusion(bf16[1024,1024]{1,0:T(8,128)(2,1)} %get-tuple-element.7, f32[1024]{0:T(1024)S(1)} %get-tuple-element.11, f32[1024]{0:T(1024)S(1)} %get-tuple-element.12, bf16[1024,1024]{1,0:T(8,128)(2,1)} %get-tuple-element.5, ...), kind=kLoop, calls=%fused_computation.12 | loop fusion | flops 12582912 | bytes 23085056 | tf_op jit(solution)/shard_map/div | solution.py:67
  298.0 8.6 %gather_fusion.4 = f32[1024,1024]{1,0:T(8,128)} fusion(f32[1024,1024]{1,0:T(8,128)} %get-tuple-element.9, s32[1024]{0:T(1024)S(1)} %broadcast_clamp_fusion), kind=kCustom, calls=%fused_computation.4 | custom fusion | bytes 8392704 | tf_op jit(solution)/shard_map/gather | solution.py:46
  306.6 5.0 %subtract_convert_fusion = bf16[32,32,1024]{2,1,0:T(8,128)(2,1)} fusion(f32[32,32,1024]{2,1,0:T(8,128)} %bitcast.134, bf16[32,32,1024]{2,1,0:T(8,128)(2,1)} %all-to-all-done.6), kind=kLoop, calls=%fused_computation.16 | loop fusion | flops 3145728 | bytes 8388608 | tf_op jit(solution)/shard_map/convert_element_type | solution.py:47
  311.6 7.5 %all-to-all-start.8 = ((bf16[32,32,1024]{2,1,0:T(8,128)(2,1)}), bf16[32,32,1024]{2,1,0:T(8,128)(2,1)}, u32[]{:S(2)}, u32[]{:S(2)}) async-start(bf16[32,32,1024]{2,1,0:T(8,128)(2,1)} %subtract_convert_fusion), calls=%async_computation.8 | async-start | bytes 4194304 | tf_op jit(solution)/shard_map/all_to_all | solution.py:48
  319.2 8.6 %gather_fusion.2 = f32[1024,1024]{1,0:T(8,128)} fusion(f32[1024,1024]{1,0:T(8,128)} %get-tuple-element.10, s32[1024]{0:T(1024)S(1)} %broadcast_clamp_fusion.1), kind=kCustom, calls=%fused_computation.2 | custom fusion | bytes 8392704 | tf_op jit(solution)/shard_map/gather | solution.py:46
  327.8 5.0 %subtract_convert_fusion.1 = bf16[32,32,1024]{2,1,0:T(8,128)(2,1)} fusion(f32[32,32,1024]{2,1,0:T(8,128)} %bitcast.135, bf16[32,32,1024]{2,1,0:T(8,128)(2,1)} %copy-done), kind=kLoop, calls=%fused_computation.21 | loop fusion | flops 3145728 | bytes 8388608 | tf_op jit(solution)/shard_map/convert_element_type | solution.py:47
  332.7 14.3 %all-to-all-done.8 = bf16[32,32,1024]{2,1,0:T(8,128)(2,1)} async-done(((bf16[32,32,1024]{2,1,0:T(8,128)(2,1)}), bf16[32,32,1024]{2,1,0:T(8,128)(2,1)}, u32[]{:S(2)}, u32[]{:S(2)}) %all-to-all-start.8) | async-done | bytes 2097184 | tf_op jit(solution)/shard_map/all_to_all | solution.py:48
  347.0 6.7 %all-to-all-start.5 = ((bf16[32,32,1024]{2,1,0:T(8,128)(2,1)}), bf16[32,32,1024]{2,1,0:T(8,128)(2,1)}, u32[]{:S(2)}, u32[]{:S(2)}) async-start(bf16[32,32,1024]{2,1,0:T(8,128)(2,1)} %subtract_convert_fusion.1), calls=%async_computation.5 | async-start | bytes 4194304 | tf_op jit(solution)/shard_map/all_to_all | solution.py:48
  360.4 21.3 %all-to-all-done.5 = bf16[32,32,1024]{2,1,0:T(8,128)(2,1)} async-done(((bf16[32,32,1024]{2,1,0:T(8,128)(2,1)}), bf16[32,32,1024]{2,1,0:T(8,128)(2,1)}, u32[]{:S(2)}, u32[]{:S(2)}) %all-to-all-start.5) | async-done | bytes 2097184 | tf_op jit(solution)/shard_map/all_to_all | solution.py:48
  (71 shorter events, 65.3 us)
Async XLA Ops:
  17.2 13.7 %all-to-all-start.4 = ((s32[32,1,32]{2,1,0:T(1,128)}), s32[32,1,32]{2,1,0:T(1,128)S(1)}, u32[]{:S(2)}, u32[]{:S(2)}) async-start(s32[32,1,32]{2,1,0:T(1,128)} %all_to_all.41), calls=%async_computation.4 | async-start | bytes 32768 | tf_op jit(solution)/shard_map/all_to_all | solution.py:56
  30.9 11.2 %all-to-all-start.7 = ((s32[32,1,32]{2,1,0:T(1,128)}), s32[32,1,32]{2,1,0:T(1,128)S(1)}, u32[]{:S(2)}, u32[]{:S(2)}) async-start(s32[32,1,32]{2,1,0:T(1,128)} %all_to_all.45), calls=%async_computation.7 | async-start | bytes 32768 | tf_op jit(solution)/shard_map/all_to_all | solution.py:56
  42.1 11.1 %all-to-all-start.1 = ((s32[32,1,32]{2,1,0:T(1,128)}), s32[32,1,32]{2,1,0:T(1,128)S(1)}, u32[]{:S(2)}, u32[]{:S(2)}) async-start(s32[32,1,32]{2,1,0:T(1,128)} %all_to_all.37), calls=%async_computation.1 | async-start | bytes 32768 | tf_op jit(solution)/shard_map/all_to_all | solution.py:56
  53.3 34.0 %all-to-all-start.3 = ((bf16[32,32,1024]{2,1,0:T(8,128)(2,1)}), bf16[32,32,1024]{2,1,0:T(8,128)(2,1)S(1)}, u32[]{:S(2)}, u32[]{:S(2)}) async-start(bf16[32,32,1024]{2,1,0:T(8,128)(2,1)} %bitcast.22), calls=%async_computation.3 | async-start | bytes 4194304 | tf_op jit(solution)/shard_map/all_to_all | solution.py:55
  87.2 44.3 %copy-start = (bf16[32,32,1024]{2,1,0:T(8,128)(2,1)}, bf16[32,32,1024]{2,1,0:T(8,128)(2,1)S(1)}, u32[]{:S(2)}) copy-start(bf16[32,32,1024]{2,1,0:T(8,128)(2,1)S(1)} %all-to-all-done.3) | copy-start | bytes 6291460
  87.3 34.7 %all-to-all-start.6 = ((bf16[32,32,1024]{2,1,0:T(8,128)(2,1)}), bf16[32,32,1024]{2,1,0:T(8,128)(2,1)}, u32[]{:S(2)}, u32[]{:S(2)}) async-start(bf16[32,32,1024]{2,1,0:T(8,128)(2,1)} %bitcast.37), calls=%async_computation.6 | async-start | bytes 4194304 | tf_op jit(solution)/shard_map/all_to_all | solution.py:55
  122.0 34.7 %all-to-all-start = ((bf16[32,32,1024]{2,1,0:T(8,128)(2,1)}), bf16[32,32,1024]{2,1,0:T(8,128)(2,1)}, u32[]{:S(2)}, u32[]{:S(2)}) async-start(bf16[32,32,1024]{2,1,0:T(8,128)(2,1)} %bitcast.7), calls=%async_computation | async-start | bytes 4194304 | tf_op jit(solution)/shard_map/all_to_all | solution.py:55
  128.7 160.9 %all-reduce.4.cloned.1.call-start = ((), (), s32[]{:S(2)}) async-start(), calls=%async_computation.9 | async-start | bytes 12582912 | tf_op jit(solution)/shard_map/psum | solution.py:64
  161.9 0.7 copy-start.1
  190.0 121.6 %all-to-all-start.2 = ((bf16[32,32,1024]{2,1,0:T(8,128)(2,1)}), bf16[32,32,1024]{2,1,0:T(8,128)(2,1)S(1)}, u32[]{:S(2)}, u32[]{:S(2)}) async-start(bf16[32,32,1024]{2,1,0:T(8,128)(2,1)} %subtract_convert_fusion.2), calls=%async_computation.2 | async-start | bytes 4194304 | tf_op jit(solution)/shard_map/all_to_all | solution.py:48
  311.6 35.4 %all-to-all-start.8 = ((bf16[32,32,1024]{2,1,0:T(8,128)(2,1)}), bf16[32,32,1024]{2,1,0:T(8,128)(2,1)}, u32[]{:S(2)}, u32[]{:S(2)}) async-start(bf16[32,32,1024]{2,1,0:T(8,128)(2,1)} %subtract_convert_fusion), calls=%async_computation.8 | async-start | bytes 4194304 | tf_op jit(solution)/shard_map/all_to_all | solution.py:48
  347.0 34.7 %all-to-all-start.5 = ((bf16[32,32,1024]{2,1,0:T(8,128)(2,1)}), bf16[32,32,1024]{2,1,0:T(8,128)(2,1)}, u32[]{:S(2)}, u32[]{:S(2)}) async-start(bf16[32,32,1024]{2,1,0:T(8,128)(2,1)} %subtract_convert_fusion.1), calls=%async_computation.5 | async-start | bytes 4194304 | tf_op jit(solution)/shard_map/all_to_all | solution.py:48
Sparse Core Ops, SparseCore 0:
  162.1 127.5 all-reduce.3
where the time goes:
time: 398 us; the launch traced here: 395 us
  waiting for transfers between devices  199 us (50%)
  local copies, waits for them, and re-layouts  64.6 us (16%)
  starting transfers between devices  57.4 us (14%)
  other arithmetic  33.6 us (8%)
  between operations  14.3 us (4%)
  matrix products  14.1 us (4%)
  blocking collectives  12.2 us (3%)
    psum x1, waiting for transfers between devices, local(): lax.psum(sums.astype(jnp.bfloat16), 'grp').astype(jnp.float32)  93.4 us
    all_to_all x3, waiting for transfers between devices, local(): lax.all_to_all(send_rows, 'list', split_axis=0, concat_axis=0, tiled=True)  62.5 us
    all_to_all x3, waiting for transfers between devices, route_fn(): lax.all_to_all(residual_rows, 'list', split_axis=0, concat_axis=0, tiled=...  35.6 us
    gather x3, local copies, waits for them, and re-layouts, route_fn(): chosen = table[jnp.clip(list_ids, 0, list_dev - 1)]  25.8 us
    all_to_all x3, starting transfers between devices, route_fn(): lax.all_to_all(residual_rows, 'list', split_axis=0, concat_axis=0, tiled=...  20.3 us
    all_to_all x3, starting transfers between devices, local(): lax.all_to_all(send_rows, 'list', split_axis=0, concat_axis=0, tiled=True)  19.5 us
    all_to_all x3, starting transfers between devices, local(): lax.all_to_all(send_slots, 'list', split_axis=0, concat_axis=0, tiled=True)  17.5 us
    convert_element_type x3, other arithmetic, route_fn(): residual_rows = (vec_rows.astype(jnp.float32) - chosen).astype(jnp.bfloat16)  14.9 us
  transfers between devices with their start and end apart: 10, of which 9 were waited for; matrix products, arithmetic and copies ran while one was open for 22% of the time, Pallas kernels for 0%

commit v1 on v0

v1 whole, which is shorter than its diff:
```python
import jax
import jax.numpy as jnp
from jax import lax
from jax.sharding import PartitionSpec as P

STEPS = 3


def tie(value, *others):
    return lax.optimization_barrier((value,) + others)[0]


def split_table(table):
    hi = lax.reduce_precision(table, 8, 7)
    lo = table - hi
    return jnp.concatenate([hi.astype(jnp.bfloat16), lo.astype(jnp.bfloat16)], axis=0)


def local(vectors, owner_route, list_slot, centroids, counts):
    owner_count = lax.axis_size("list")
    grp_count = lax.axis_size("grp")
    row_count = vectors.shape[1]
    width = vectors.shape[2]
    capacity = 2 * row_count // owner_count
    list_dev = centroids.shape[0]
    total_rows = owner_count * capacity

    owner_ids = owner_route[:, :, 0]
    hits = owner_ids[:, :, None] == jnp.arange(owner_count, dtype=jnp.int32)
    earlier = jnp.arange(row_count)[:, None] > jnp.arange(row_count)[None, :]
    before = jnp.einsum(
        "ij,sjo->sio",
        earlier.astype(jnp.bfloat16),
        hits.astype(jnp.bfloat16),
        preferred_element_type=jnp.float32,
    )
    rank = jnp.sum(jnp.where(hits, before, 0.0), axis=2).astype(jnp.int32)
    dest = owner_ids * capacity + rank

    row_iota = jnp.arange(total_rows, dtype=jnp.int32)
    place = dest[:, None, :] == row_iota[None, :, None]
    slots = jnp.sum(jnp.where(place, list_slot[:, None, :] + 1, 0), axis=2) - 1
    slots = slots.reshape(STEPS, owner_count, capacity).transpose(1, 0, 2)
    slots = slots.reshape(owner_count, 1, STEPS * capacity)
    slots = lax.all_to_all(slots, "list", split_axis=0, concat_axis=0, tiled=True)
    slots = slots.reshape(owner_count, STEPS, capacity).transpose(1, 0, 2)
    slots = slots.reshape(STEPS, total_rows)

    list_iota = jnp.arange(list_dev, dtype=jnp.int32)
    batch = jnp.sum((slots[:, None, :] == list_iota[None, :, None]).astype(jnp.int32), axis=2)
    parts = [batch]
    for offset in range(1, grp_count):
        parts.append(
            lax.ppermute(batch, "grp", [(i, (i + offset) % grp_count) for i in range(grp_count)])
        )
    batch = sum(parts).astype(jnp.float32)

    def exchange(rows):
        rows = rows.reshape(owner_count, capacity, width)
        rows = lax.all_to_all(rows, "list", split_axis=0, concat_axis=0, tiled=True)
        return rows.reshape(total_rows, width)

    received = []
    for step in range(STEPS):
        send = jnp.dot(
            (dest[step][None, :] == row_iota[:, None]).astype(jnp.bfloat16),
            vectors[step],
            preferred_element_type=jnp.float32,
        ).astype(jnp.bfloat16)
        if received:
            send = tie(send, received[-1])
        received.append(exchange(send))

    totals = []
    for step in range(STEPS):
        one_hot = (list_iota[:, None] == slots[step][None, :]).astype(jnp.bfloat16)
        sums = jnp.dot(one_hot, received[step], preferred_element_type=jnp.float32)
        sums = sums.astype(jnp.bfloat16)
        if totals:
            sums = tie(sums, totals[-1])
        totals.append(lax.psum(sums, "grp"))

    weights = counts.astype(jnp.float32)
    mass = weights[:, None] * centroids
    current = centroids
    outputs = []
    last = received[-1]
    backs = []
    for step in range(STEPS):
        one_hot = slots[step][:, None] == (jnp.arange(2 * list_dev, dtype=jnp.int32) % list_dev)[None, :]
        chosen = jnp.dot(
            one_hot.astype(jnp.bfloat16), split_table(current), preferred_element_type=jnp.float32
        )
        residual = (received[step].astype(jnp.float32) - chosen).astype(jnp.bfloat16)
        back = exchange(tie(residual, last))
        last = back
        backs.append(back)
        pick = (dest[step][:, None] == row_iota[None, :]).astype(jnp.bfloat16)
        outputs.append(jnp.dot(pick, back, preferred_element_type=jnp.float32).astype(jnp.bfloat16))
        total = tie(totals[step], received[-1] if step == 0 else backs[-2])
        mass = mass + total.astype(jnp.float32)
        weights = weights + batch[step]
        current = mass / weights[:, None]
    return (jnp.stack(outputs, axis=0), current)


def solution(mesh):
    in_specs = (
        P(None, ("grp", "list"), None),
        P(None, ("grp", "list"), None),
        P(None, ("grp", "list")),
        P("list", None),
        P("list"),
    )
    out_specs = (P(None, ("grp", "list"), None), P("list", None))
    return jax.shard_map(local, mesh=mesh, in_specs=in_specs, out_specs=out_specs, check_vma=False)
```

time: 398 us -> 317 us (0.80)
  local copies, waits for them, and re-layouts: 64.6 us -> 2.58 us
  matrix products: 14.1 us -> 54.7 us
  waiting for transfers between devices: 199 us -> 168 us
  blocking collectives: 12.2 us -> 0 us
  other arithmetic: 33.6 us -> 21.5 us
    dot_general x3 -> x13, matrix products: 14.1 us -> 54.7 us  [the longest x3 21.6 us: local(): jnp.dot(one_hot.astype(jnp.bfloat16), split_table(current), preferred_ele...]
    gather x6 -> x0, local copies, waits for them, and re-layouts: 37 us -> none  [the longest x3 25.8 us: route_fn(): chosen = table[jnp.clip(list_ids, 0, list_dev - 1)]]
    all_to_all x9 -> x7, waiting for transfers between devices: 105 us -> 71.3 us  [the longest x6 68.9 us: exchange(): rows = lax.all_to_all(rows, 'list', split_axis=0, concat_axis=0, tiled=True)]
    scatter x6 -> x0, local copies, waits for them, and re-layouts: 21.7 us -> none  [the longest x3 14.4 us: local(): send_rows = jnp.zeros((owner_count * capacity, width), jnp.bfloat16).at[d...]
    psum x1 -> x0, blocking collectives: 12.2 us -> none  [local(): lax.psum(batch_count.astype(jnp.bfloat16), 'grp').astype(jnp.float32)]
    all_to_all x9 -> x7, starting transfers between devices: 57.3 us -> 48.3 us  [the longest x6 42.5 us: exchange(): rows = lax.all_to_all(rows, 'list', split_axis=0, concat_axis=0, tiled=True)]
    div x1 -> x0, other arithmetic: 8.36 us -> none  [local(): (weights[:, None] * current + total_sums) / (weights + total_count)[:, None]]
    ppermute x0 -> x3, starting transfers between devices: none -> 5.37 us  [local(): lax.ppermute(batch, 'grp', [(i, (i + offset) % grp_count) for i in range(...]
  transfers between devices with their start and end apart: 10 -> 13, of which waited for: 9 -> 8; matrix products, arithmetic and copies ran while one was open for 22% -> 18% of each run, Pallas kernels for 0% -> 0%
where the time goes in v1:
time: 317 us; the launch traced here: 315 us
  waiting for transfers between devices  168 us (53%)
  matrix products  54.7 us (17%)
  starting transfers between devices  54 us (17%)
  other arithmetic  21.5 us (7%)
  between operations  13.9 us (4%)
    psum x3, waiting for transfers between devices, local(): totals.append(lax.psum(sums, 'grp'))  92.7 us
    all_to_all x6, waiting for transfers between devices, exchange(): rows = lax.all_to_all(rows, 'list', split_axis=0, concat_axis=0, tiled=True)  68.9 us
    all_to_all x6, starting transfers between devices, exchange(): rows = lax.all_to_all(rows, 'list', split_axis=0, concat_axis=0, tiled=True)  42.5 us
    dot_general x3, matrix products, local(): jnp.dot(one_hot.astype(jnp.bfloat16), split_table(current), preferred_ele...  21.6 us
    dot_general x3, matrix products, local(): sums = jnp.dot(one_hot, received[step], preferred_element_type=jnp.float32)  14.3 us
    dot_general x3, matrix products, local(): jnp.dot((dest[step][None, :] == row_iota[:, None]).astype(jnp.bfloat16),...  11.4 us
    convert_element_type x2, other arithmetic, split_table(): hi.astype(jnp.bfloat16)  11.3 us
    dot_general x3, matrix products, local(): jnp.dot(pick, back, preferred_element_type=jnp.float32).astype(jnp.bfloat16)  7.06 us
  transfers between devices with their start and end apart: 13, of which 8 were waited for; matrix products, arithmetic and copies ran while one was open for 18% of the time, Pallas kernels for 0%

profile of v1, /device:TPU:2, one launch (start us, length us, event | category | flops | bytes accessed | tf_op | source)
XLA Modules:
  0.0 314.5 jit_solution(11587762332282311893)
XLA Ops:
  12.7 7.6 %all-to-all-start = ((bf16[32,32,1024]{2,1,0:T(8,128)(2,1)}), bf16[32,32,1024]{2,1,0:T(8,128)(2,1)S(1)}, u32[]{:S(2)}, u32[]{:S(2)}) async-start(bf16[32,32,1024]{2,1,0:T(8,128)(2,1)} %bitcast.63), calls=%async_computation | async-start | bytes 4194304 | tf_op jit(solution)/shard_map/all_to_all | solution.py:60
  22.0 26.2 %all-to-all-done = bf16[32,32,1024]{2,1,0:T(8,128)(2,1)S(1)} async-done(((bf16[32,32,1024]{2,1,0:T(8,128)(2,1)}), bf16[32,32,1024]{2,1,0:T(8,128)(2,1)S(1)}, u32[]{:S(2)}, u32[]{:S(2)}) %all-to-all-start) | async-done | bytes 2097184 | tf_op jit(solution)/shard_map/all_to_all | solution.py:60
  48.2 5.8 %all-to-all-start.1 = ((s32[32,1,96]{2,1,0:T(1,128)}), s32[32,1,96]{2,1,0:T(1,128)S(1)}, u32[]{:S(2)}, u32[]{:S(2)}) async-start(s32[32,1,96]{2,1,0:T(1,128)} %bitcast.7), calls=%async_computation.1 | async-start | bytes 32768 | tf_op jit(solution)/shard_map/all_to_all | solution.py:45
  54.0 3.8 %fusion.37 = bf16[1024,1024]{1,0:T(8,128)(2,1)} fusion(bf16[3,512,1024]{2,1,0:T(8,128)(2,1)} %param.5, s32[512]{0:T(512)S(1)} %bitcast.74), kind=kOutput, calls=%fused_computation.64 | convolution fusion | flops 1075314688 | bytes 3147776 | tf_op jit(solution)/shard_map/dot_general | solution.py:65
  60.2 5.8 %all-to-all-start.2 = ((bf16[32,32,1024]{2,1,0:T(8,128)(2,1)}), bf16[32,32,1024]{2,1,0:T(8,128)(2,1)}, u32[]{:S(2)}, u32[]{:S(2)}) async-start(bf16[32,32,1024]{2,1,0:T(8,128)(2,1)} %bitcast.60), calls=%async_computation.2 | async-start | bytes 4194304 | tf_op jit(solution)/shard_map/all_to_all | solution.py:60
  71.3 3.8 %fusion.38 = bf16[1024,1024]{1,0:T(8,128)(2,1)} fusion(bf16[3,512,1024]{2,1,0:T(8,128)(2,1)} %param.5, s32[512]{0:T(512)S(1)} %bitcast.72), kind=kOutput, calls=%fused_computation.65 | convolution fusion | flops 1075314688 | bytes 3147776 | tf_op jit(solution)/shard_map/dot_general | solution.py:65
  75.1 19.0 %all-to-all-done.2 = bf16[32,32,1024]{2,1,0:T(8,128)(2,1)} async-done(((bf16[32,32,1024]{2,1,0:T(8,128)(2,1)}), bf16[32,32,1024]{2,1,0:T(8,128)(2,1)}, u32[]{:S(2)}, u32[]{:S(2)}) %all-to-all-start.2) | async-done | bytes 2097184 | tf_op jit(solution)/shard_map/all_to_all | solution.py:60
  94.0 6.7 %all-to-all-start.3 = ((bf16[32,32,1024]{2,1,0:T(8,128)(2,1)}), bf16[32,32,1024]{2,1,0:T(8,128)(2,1)}, u32[]{:S(2)}, u32[]{:S(2)}) async-start(bf16[32,32,1024]{2,1,0:T(8,128)(2,1)} %bitcast.58), calls=%async_computation.3 | async-start | bytes 4194304 | tf_op jit(solution)/shard_map/all_to_all | solution.py:60
  102.4 4.1 %collective-permute-start.2 = (s32[3,1024]{1,0:T(4,128)S(1)}, s32[3,1024]{1,0:T(4,128)S(1)}, u32[]{:S(2)}, u32[]{:S(2)}) collective-permute-start(s32[3,1024]{1,0:T(4,128)S(1)} %convert_reduce_fusion), channel_id=1, source_target_pairs={{0,96},{32,0},{64,32},{96,64},{1,97},{33,1},{65,33},{97,65},{2,98}... | collective-permute-start | bytes 36872 | tf_op jit(solution)/shard_map/ppermute | solution.py:54
  111.8 5.4 %fusion.41 = bf16[1024,1024]{1,0:T(8,128)(2,1)} fusion(bf16[1024,1024]{1,0:T(8,128)(2,1)} %bitcast.14, s32[1024]{0:T(1024)S(1)} %eq.241), kind=kOutput, calls=%fused_computation.68 | convolution fusion | flops 2149580800 | bytes 4198400 | tf_op jit(solution)/shard_map/dot_general | solution.py:77
  117.2 15.4 %all-reduce.4.cloned.1.call-done = bf16[1024,1024]{1,0:T(8,128)(2,1)} async-done(((bf16[1024,1024]{1,0:T(8,128)(2,1)}), bf16[1024,1024]{1,0:T(8,128)(2,1)}) %all-reduce.4.cloned.1.call-update) | async-done | bytes 2097168 | tf_op jit(solution)/shard_map/psum | solution.py:81
  132.7 5.3 %reduce-precision_convert_fusion.1 = (bf16[1024,1024]{1,0:T(8,128)(2,1)}, f32[1024,1024]{1,0:T(8,128)}, bf16[1024,1024]{1,0:T(8,128)(2,1)S(1)}, bf16[1024,1024]{1,0:T(8,128)(2,1)S(1)}) fusion(f32[1024]{0:T(1024)S(1)} %get-tuple-element.27, bf16[1024,1024]{1,0:T(8,128)(2,1)} %all-reduce.4.cloned.1.call-done, f32[1024,1024]{1,0:T(8,128)} %param.8, ...), kind=kLoop, calls=%fused_computation.13 | loop fusion | flops 10485760 | bytes 16785408 | tf_op jit(solution)/shard_map/convert_element_type | solution.py:16
  138.0 5.9 %subtract_convert_fusion.2 = bf16[1024,1024]{1,0:T(8,128)(2,1)} fusion(bf16[1024,1024]{1,0:T(8,128)(2,1)S(1)} %bitcast.57, bf16[1024,1024]{1,0:T(8,128)(2,1)S(1)} %get-tuple-element.34, bf16[1024,1024]{1,0:T(8,128)(2,1)S(1)} %get-tuple-element.33, s32[2048]{0:T(1024)S(1)} %add_select_fusion, s32[1024]{0:T(1024)S(1)} %eq.226), kind=kOutput, calls=%fused_computation.36 | convolution fusion | flops 4308598784 | bytes 8400896 | tf_op jit(solution)/shard_map/dot_general | solution.py:91
  143.9 7.4 %all-to-all-start.4 = ((bf16[32,32,1024]{2,1,0:T(8,128)(2,1)}), bf16[32,32,1024]{2,1,0:T(8,128)(2,1)S(1)}, u32[]{:S(2)}, u32[]{:S(2)}) async-start(bf16[32,32,1024]{2,1,0:T(8,128)(2,1)} %bitcast.61), calls=%async_computation.4 | async-start | bytes 4194304 | tf_op jit(solution)/shard_map/all_to_all | solution.py:60
  151.6 5.3 %fusion.40 = bf16[1024,1024]{1,0:T(8,128)(2,1)} fusion(bf16[1024,1024]{1,0:T(8,128)(2,1)} %bitcast.16, s32[1024]{0:T(1024)S(1)} %eq.254), kind=kOutput, calls=%fused_computation.67 | convolution fusion | flops 2149580800 | bytes 4198400 | tf_op jit(solution)/shard_map/dot_general | solution.py:77
  156.9 4.4 %fusion.7 = bf16[1024,1024]{1,0:T(8,128)(2,1)} fusion(f32[1024,1024]{1,0:T(8,128)} %get-tuple-element.29, f32[1024]{0:T(1024)S(1)} %get-tuple-element.27), kind=kLoop, calls=%fused_computation.17 | loop fusion | flops 4194304 | bytes 6295552 | tf_op jit(solution)/shard_map/convert_element_type | solution.py:16
  161.3 32.5 %all-reduce.6.cloned.1.call-done = bf16[1024,1024]{1,0:T(8,128)(2,1)} async-done(((bf16[1024,1024]{1,0:T(8,128)(2,1)}), bf16[1024,1024]{1,0:T(8,128)(2,1)}) %all-reduce.6.cloned.1.call-update) | async-done | bytes 2097168 | tf_op jit(solution)/shard_map/psum | solution.py:81
  193.8 8.7 %subtract_convert_fusion.1 = bf16[1024,1024]{1,0:T(8,128)(2,1)} fusion(bf16[1024,1024]{1,0:T(8,128)(2,1)} %bitcast.14, bf16[1024,1024]{1,0:T(8,128)(2,1)} %fusion.7, bf16[1024,1024]{1,0:T(8,128)(2,1)} %get-tuple-element.28, s32[2048]{0:T(1024)S(1)} %add_select_fusion, s32[1024]{0:T(1024)S(1)} %eq.241), kind=kOutput, calls=%fused_computation.33 | convolution fusion | flops 4308598784 | bytes 8400896 | tf_op jit(solution)/shard_map/dot_general | solution.py:91
  202.5 7.5 %all-to-all-start.5 = ((bf16[32,32,1024]{2,1,0:T(8,128)(2,1)}), bf16[32,32,1024]{2,1,0:T(8,128)(2,1)}, u32[]{:S(2)}, u32[]{:S(2)}) async-start(bf16[32,32,1024]{2,1,0:T(8,128)(2,1)} %bitcast.62), calls=%async_computation.5 | async-start | bytes 4194304 | tf_op jit(solution)/shard_map/all_to_all | solution.py:60
  210.0 44.8 %all-reduce.8.cloned.1.call-done = bf16[1024,1024]{1,0:T(8,128)(2,1)} async-done(((bf16[1024,1024]{1,0:T(8,128)(2,1)}), bf16[1024,1024]{1,0:T(8,128)(2,1)}) %all-reduce.8.cloned.1.call-update) | async-done | bytes 2097168 | tf_op jit(solution)/shard_map/psum | solution.py:81
  254.8 5.9 %reduce-precision_convert_fusion = (bf16[1024,1024]{1,0:T(8,128)(2,1)S(1)}, bf16[1024,1024]{1,0:T(8,128)(2,1)S(1)}, f32[1024,1024]{1,0:T(8,128)}) fusion(f32[1024]{0:T(1024)S(1)} %get-tuple-element.26, f32[1024,1024]{1,0:T(8,128)} %get-tuple-element.29, bf16[1024,1024]{1,0:T(8,128)(2,1)} %all-reduce.6.cloned.1.call-done, f32[1024]{0:T(1024)S(1)} %get-tuple-element.25, ...), kind=kLoop, calls=%fused_computation.11 | loop fusion | flops 10485760 | bytes 16785408 | tf_op jit(solution)/shard_map/convert_element_type | solution.py:16
  260.7 7.0 %subtract_convert_fusion = bf16[1024,1024]{1,0:T(8,128)(2,1)} fusion(bf16[1024,1024]{1,0:T(8,128)(2,1)} %bitcast.16, bf16[1024,1024]{1,0:T(8,128)(2,1)S(1)} %get-tuple-element.31, bf16[1024,1024]{1,0:T(8,128)(2,1)S(1)} %get-tuple-element.30, s32[2048]{0:T(1024)S(1)} %add_select_fusion, s32[1024]{0:T(1024)S(1)} %eq.254), kind=kOutput, calls=%fused_computation.30 | convolution fusion | flops 4308598784 | bytes 8400896 | tf_op jit(solution)/shard_map/dot_general | solution.py:91
  267.7 7.5 %all-to-all-start.6 = ((bf16[32,32,1024]{2,1,0:T(8,128)(2,1)}), bf16[32,32,1024]{2,1,0:T(8,128)(2,1)}, u32[]{:S(2)}, u32[]{:S(2)}) async-start(bf16[32,32,1024]{2,1,0:T(8,128)(2,1)} %bitcast.64), calls=%async_computation.6 | async-start | bytes 4194304 | tf_op jit(solution)/shard_map/all_to_all | solution.py:60
  279.4 23.7 %all-to-all-done.6 = bf16[32,32,1024]{2,1,0:T(8,128)(2,1)} async-done(((bf16[32,32,1024]{2,1,0:T(8,128)(2,1)}), bf16[32,32,1024]{2,1,0:T(8,128)(2,1)}, u32[]{:S(2)}, u32[]{:S(2)}) %all-to-all-start.6) | async-done | bytes 2097184 | tf_op jit(solution)/shard_map/all_to_all | solution.py:60
  (47 shorter events, 31.1 us)
Async XLA Ops:
  12.7 35.5 %all-to-all-start = ((bf16[32,32,1024]{2,1,0:T(8,128)(2,1)}), bf16[32,32,1024]{2,1,0:T(8,128)(2,1)S(1)}, u32[]{:S(2)}, u32[]{:S(2)}) async-start(bf16[32,32,1024]{2,1,0:T(8,128)(2,1)} %bitcast.63), calls=%async_computation | async-start | bytes 4194304 | tf_op jit(solution)/shard_map/all_to_all | solution.py:60
  48.2 12.0 %all-to-all-start.1 = ((s32[32,1,96]{2,1,0:T(1,128)}), s32[32,1,96]{2,1,0:T(1,128)S(1)}, u32[]{:S(2)}, u32[]{:S(2)}) async-start(s32[32,1,96]{2,1,0:T(1,128)} %bitcast.7), calls=%async_computation.1 | async-start | bytes 32768 | tf_op jit(solution)/shard_map/all_to_all | solution.py:45
  60.2 33.8 %all-to-all-start.2 = ((bf16[32,32,1024]{2,1,0:T(8,128)(2,1)}), bf16[32,32,1024]{2,1,0:T(8,128)(2,1)}, u32[]{:S(2)}, u32[]{:S(2)}) async-start(bf16[32,32,1024]{2,1,0:T(8,128)(2,1)} %bitcast.60), calls=%async_computation.2 | async-start | bytes 4194304 | tf_op jit(solution)/shard_map/all_to_all | solution.py:60
  66.0 66.6 %all-reduce.4.cloned.1.call-start = ((), (), s32[]{:S(2)}) async-start(), calls=%async_computation.7 | async-start | bytes 4194304 | tf_op jit(solution)/shard_map/psum | solution.py:81
  75.1 32.8 %copy-start = (s32[1024]{0:T(1024)S(1)}, s32[1024]{0:T(1024)}, u32[]{:S(2)}) copy-start(s32[1024]{0:T(1024)} %param.9) | copy-start | bytes 12292
  94.0 38.6 %all-to-all-start.3 = ((bf16[32,32,1024]{2,1,0:T(8,128)(2,1)}), bf16[32,32,1024]{2,1,0:T(8,128)(2,1)}, u32[]{:S(2)}, u32[]{:S(2)}) async-start(bf16[32,32,1024]{2,1,0:T(8,128)(2,1)} %bitcast.58), calls=%async_computation.3 | async-start | bytes 4194304 | tf_op jit(solution)/shard_map/all_to_all | solution.py:60
  100.7 93.0 %all-reduce.6.cloned.1.call-start = ((), (), s32[]{:S(2)}) async-start(), calls=%async_computation.8 | async-start | bytes 4194304 | tf_op jit(solution)/shard_map/psum | solution.py:81
  102.4 5.6 %collective-permute-start.2 = (s32[3,1024]{1,0:T(4,128)S(1)}, s32[3,1024]{1,0:T(4,128)S(1)}, u32[]{:S(2)}, u32[]{:S(2)}) collective-permute-start(s32[3,1024]{1,0:T(4,128)S(1)} %convert_reduce_fusion), channel_id=1, source_target_pairs={{0,96},{32,0},{64,32},{96,64},{1,97},{33,1},{65,33},{97,65},{2,98}... | collective-permute-start | bytes 36872 | tf_op jit(solution)/shard_map/ppermute | solution.py:54
  106.5 5.2 %collective-permute-start.1 = (s32[3,1024]{1,0:T(4,128)S(1)}, s32[3,1024]{1,0:T(4,128)S(1)}, u32[]{:S(2)}, u32[]{:S(2)}) collective-permute-start(s32[3,1024]{1,0:T(4,128)S(1)} %convert_reduce_fusion), channel_id=1, source_target_pairs={{0,64},{32,96},{64,0},{96,32},{1,65},{33,97},{65,1},{97,33},{2,66}... | collective-permute-start | bytes 36872 | tf_op jit(solution)/shard_map/ppermute | solution.py:54
  106.6 5.2 %collective-permute-start = (s32[3,1024]{1,0:T(4,128)S(1)}, s32[3,1024]{1,0:T(4,128)S(1)}, u32[]{:S(2)}, u32[]{:S(2)}) collective-permute-start(s32[3,1024]{1,0:T(4,128)S(1)} %convert_reduce_fusion), channel_id=1, source_target_pairs={{0,32},{32,64},{64,96},{96,0},{1,33},{33,65},{65,97},{97,1},{2,34}... | collective-permute-start | bytes 36872 | tf_op jit(solution)/shard_map/ppermute | solution.py:54
  143.9 58.6 %all-to-all-start.4 = ((bf16[32,32,1024]{2,1,0:T(8,128)(2,1)}), bf16[32,32,1024]{2,1,0:T(8,128)(2,1)S(1)}, u32[]{:S(2)}, u32[]{:S(2)}) async-start(bf16[32,32,1024]{2,1,0:T(8,128)(2,1)} %bitcast.61), calls=%async_computation.4 | async-start | bytes 4194304 | tf_op jit(solution)/shard_map/all_to_all | solution.py:60
  151.3 103.5 %all-reduce.8.cloned.1.call-start = ((), (), s32[]{:S(2)}) async-start(), calls=%async_computation.9 | async-start | bytes 4194304 | tf_op jit(solution)/shard_map/psum | solution.py:81
  202.5 52.3 %all-to-all-start.5 = ((bf16[32,32,1024]{2,1,0:T(8,128)(2,1)}), bf16[32,32,1024]{2,1,0:T(8,128)(2,1)}, u32[]{:S(2)}, u32[]{:S(2)}) async-start(bf16[32,32,1024]{2,1,0:T(8,128)(2,1)} %bitcast.62), calls=%async_computation.5 | async-start | bytes 4194304 | tf_op jit(solution)/shard_map/all_to_all | solution.py:60
  267.7 35.4 %all-to-all-start.6 = ((bf16[32,32,1024]{2,1,0:T(8,128)(2,1)}), bf16[32,32,1024]{2,1,0:T(8,128)(2,1)}, u32[]{:S(2)}, u32[]{:S(2)}) async-start(bf16[32,32,1024]{2,1,0:T(8,128)(2,1)} %bitcast.64), calls=%async_computation.6 | async-start | bytes 4194304 | tf_op jit(solution)/shard_map/all_to_all | solution.py:60
Sparse Core Ops, SparseCore 0:
  71.4 61.1 all-reduce.3
  135.1 58.6 all-reduce.5
  196.1 58.5 all-reduce.7

commit v2 on v0

v2 whole, which is shorter than its diff:
```python
import jax
import jax.numpy as jnp
from jax import lax
from jax.experimental import pallas as pl
from jax.experimental.pallas import tpu as pltpu
from jax.sharding import PartitionSpec as P

STEPS = 3
BLOCK = 512
CHEAP = pl.CostEstimate(flops=1, bytes_accessed=1, transcendentals=0)


def gate(*values):
    return lax.optimization_barrier(values)


def swap(rows, axis, offset):
    count = lax.axis_size(axis)
    return lax.ppermute(rows, axis, [(i, i ^ offset) for i in range(count)])


def select(hit):
    return jnp.where(hit, 1.0, 0.0).astype(jnp.bfloat16)


def mix(left, right):
    return jnp.dot(left, right, preferred_element_type=jnp.float32)


def pack_rows(vectors, dest, step, owners, capacity, count):
    row_count, width = vectors.shape[1:]
    group = BLOCK // capacity

    def body(dest_ref, vec_ref, out_ref):
        rows = lax.broadcasted_iota(jnp.int32, (BLOCK, row_count), 0) + pl.program_id(0) * BLOCK
        picked = mix(select(rows == dest_ref[0]), vec_ref[0]).astype(jnp.bfloat16)
        out_ref[...] = picked.reshape(group, 1, capacity, width)

    return pl.pallas_call(
        body,
        grid=(owners // group,),
        in_specs=[
            pl.BlockSpec((1, 1, row_count), lambda b: (step, 0, 0)),
            pl.BlockSpec((1, row_count, width), lambda b: (step, 0, 0)),
        ],
        out_specs=pl.BlockSpec((group, 1, capacity, width), lambda b: (b, 0, 0, 0)),
        out_shape=jax.ShapeDtypeStruct((owners, count, capacity, width), jnp.bfloat16),
        name="pack_rows",
        cost_estimate=CHEAP,
    )(dest, vectors)


def list_sums(received, at, slots, step, list_dev):
    owners, _, capacity, width = received.shape
    rows = owners * capacity
    sizes = [list_dev // 8, list_dev // 8, list_dev // 4] * 2

    def body(slot_ref, row_ref, *outs):
        data = row_ref[...].reshape(rows, width)
        first = 0
        for half in range(2):
            lists = lax.broadcasted_iota(jnp.int32, (list_dev // 2, rows), 0) + first
            sums = mix(select(lists == slot_ref[0]), data).astype(jnp.bfloat16)
            at = 0
            for out_ref in outs[3 * half : 3 * half + 3]:
                out_ref[...] = sums[at : at + out_ref.shape[0]]
                at += out_ref.shape[0]
            first += list_dev // 2

    return pl.pallas_call(
        body,
        grid=(1,),
        in_specs=[
            pl.BlockSpec((1, 1, rows), lambda i: (step, 0, 0)),
            pl.BlockSpec((owners, 1, capacity, width), lambda i: (0, at, 0, 0)),
        ],
        out_specs=[pl.BlockSpec((size, width), lambda i: (0, 0)) for size in sizes],
        out_shape=[jax.ShapeDtypeStruct((size, width), jnp.bfloat16) for size in sizes],
        name="list_sums",
        cost_estimate=CHEAP,
    )(slots, received)


def update(step, index, place_ref, weight_ref, table_ref, parts, store):
    chunk = table_ref.shape[0]
    slab = 16

    def run(piece, base):
        def one(k, carry):
            at = pl.ds(pl.multiple_of(k * slab, slab), slab)
            table = table_ref[at, :]
            if parts:
                away = pl.ds(pl.multiple_of(base + k * slab, slab), slab)
                total = parts[0][piece][away, :].astype(jnp.float32)
                for four in parts[1:]:
                    total = total + four[piece][away, :].astype(jnp.float32)
                weights = weight_ref[at, :]
                share = 1.0 / weights[:, step : step + 1]
                table = (weights[:, :1] * table + total) * share
            store(index * chunk + k * slab, at, table)
            return carry

        lax.fori_loop(0, chunk // slab, one, 0, unroll=4)

    if not parts:
        run(0, 0)
        return
    half = index // 4
    relative = (index % 4) ^ place_ref[half]
    mine = 2 * half + relative // 2
    for piece in range(4):
        pl.when(mine == piece)(lambda piece=piece: run(piece, (relative % 2) * chunk))


def part_specs(parts):
    return [pl.BlockSpec(p.shape, lambda i, group: (0, 0)) for four in parts for p in four]


def fours(refs):
    return [refs[k : k + 4] for k in range(0, len(refs), 4)]


def residual_rows(received, at, slots, step, centroids, weights, parts, places, into, place, count):
    owners, _, capacity, width = received.shape
    list_dev = centroids.shape[0]
    group = BLOCK // capacity
    blocks = owners // group
    chunks = 8
    chunk = list_dev // chunks
    part_count = 4 * len(parts)

    def body(place_ref, slot_ref, row_ref, table_ref, weight_ref, *rest):
        out_ref, pair_ref = rest[-2:]
        index = pl.program_id(0)

        def store(first, at, table):
            hi = table.astype(jnp.bfloat16)
            lo = (table - hi.astype(jnp.float32)).astype(jnp.bfloat16)
            pair_ref[pl.ds(pl.multiple_of(first, 16), 16), :] = hi
            pair_ref[pl.ds(pl.multiple_of(list_dev + first, 16), 16), :] = lo

        @pl.when(index < chunks)
        def _():
            update(step, index, place_ref, weight_ref, table_ref, fours(rest[:part_count]), store)

        @pl.when(index >= chunks)
        def _():
            lists = lax.broadcasted_iota(jnp.int32, (BLOCK, list_dev), 1)
            hit = select(lists == slot_ref[:, step : step + 1])
            chosen = mix(jnp.concatenate([hit, hit], axis=1), pair_ref[...])
            data = row_ref[...].reshape(BLOCK, width).astype(jnp.float32)
            out_ref[...] = (data - chosen).astype(jnp.bfloat16).reshape(group, 1, capacity, width)

    def late(i):
        return jnp.maximum(i - chunks, 0)

    def early(i):
        return jnp.minimum(i, chunks - 1)

    in_specs = [
        pl.BlockSpec((BLOCK, STEPS), lambda i, places: (late(i), 0)),
        pl.BlockSpec((group, 1, capacity, width), lambda i, places: (late(i), at, 0, 0)),
        pl.BlockSpec((chunk, width), lambda i, places: (early(i), 0)),
        pl.BlockSpec((chunk, STEPS + 1), lambda i, places: (early(i), 0)),
    ] + part_specs(parts)
    args = [slots, received, centroids, weights] + [p for four in parts for p in four]
    aliases = {}
    if into is not None:
        in_specs.append(pl.BlockSpec(memory_space=pl.ANY))
        aliases = {1 + len(args): 0}
        args.append(into)
    return pl.pallas_call(
        body,
        grid_spec=pltpu.PrefetchScalarGridSpec(
            num_scalar_prefetch=1,
            grid=(chunks + blocks,),
            in_specs=in_specs,
            out_specs=pl.BlockSpec(
                (group, 1, capacity, width), lambda i, places: (late(i), place, 0, 0)
            ),
            scratch_shapes=[pltpu.VMEM((2 * list_dev, width), jnp.bfloat16)],
        ),
        out_shape=jax.ShapeDtypeStruct((owners, count, capacity, width), jnp.bfloat16),
        input_output_aliases=aliases,
        name="residual_rows",
        cost_estimate=CHEAP,
    )(places, *args)


def new_rows(centroids, weights, parts, places):
    list_dev, width = centroids.shape
    chunk = list_dev // 8

    def body(place_ref, table_ref, weight_ref, *rest):
        def store(first, at, table):
            rest[-1][at, :] = table

        update(STEPS, pl.program_id(0), place_ref, weight_ref, table_ref, fours(rest[:-1]), store)

    return pl.pallas_call(
        body,
        grid_spec=pltpu.PrefetchScalarGridSpec(
            num_scalar_prefetch=1,
            grid=(8,),
            in_specs=[
                pl.BlockSpec((chunk, width), lambda i, places: (i, 0)),
                pl.BlockSpec((chunk, STEPS + 1), lambda i, places: (i, 0)),
            ]
            + part_specs(parts),
            out_specs=pl.BlockSpec((chunk, width), lambda i, places: (i, 0)),
        ),
        out_shape=jax.ShapeDtypeStruct((list_dev, width), jnp.float32),
        name="new_rows",
        cost_estimate=CHEAP,
    )(places, centroids, weights, *[p for four in parts for p in four])


def unpack_rows(back, at, dest, step, into, row_count):
    owners, _, capacity, width = back.shape
    rows = owners * capacity

    def body(dest_ref, row_ref, *rest):
        places = lax.broadcasted_iota(jnp.int32, (row_count, rows), 1)
        data = row_ref[...].reshape(rows, width)
        hit = select(places == dest_ref[:, step : step + 1])
        rest[-1][0] = mix(hit, data).astype(jnp.bfloat16)

    in_specs = [
        pl.BlockSpec((row_count, STEPS), lambda b: (0, 0)),
        pl.BlockSpec((owners, 1, capacity, width), lambda b: (0, at, 0, 0)),
    ]
    args = [dest, back]
    aliases = {}
    if into is not None:
        in_specs.append(pl.BlockSpec(memory_space=pl.ANY))
        args.append(into)
        aliases = {2: 0}
    return pl.pallas_call(
        body,
        grid=(1,),
        in_specs=in_specs,
        out_specs=pl.BlockSpec((1, row_count, width), lambda b: (step, 0, 0)),
        out_shape=jax.ShapeDtypeStruct((STEPS, row_count, width), jnp.bfloat16),
        input_output_aliases=aliases,
        name="unpack_rows",
        cost_estimate=CHEAP,
    )(*args)


def add(*values):
    total = values[0].astype(jnp.float32)
    for value in values[1:]:
        total = total + value.astype(jnp.float32)
    return total.astype(jnp.bfloat16)


def scatter_sum(parts):
    got = [swap(parts[2], "grp", 1), swap(parts[5], "grp", 3)]
    block = parts[0].shape[0]
    over = [swap(add(parts[3 * h + 1], got[h][block:]), "grp", 3 - 2 * h) for h in range(2)]
    return [add(parts[3 * h], got[h][:block], over[h]) for h in range(2)]


def gather_sum(done):
    own = [jnp.concatenate([done[h], swap(done[h], "grp", 3 - 2 * h)]) for h in range(2)]
    near = [swap(own[h], "grp", 1 + 2 * h) for h in range(2)]
    return [own[0], near[0], own[1], near[1]]


def exchange(rows):
    return lax.all_to_all(rows, "list", split_axis=0, concat_axis=0, tiled=True)


def local(vectors, owner_route, list_slot, centroids, counts):
    owners = lax.axis_size("list")
    grp_count = lax.axis_size("grp")
    row_count = vectors.shape[1]
    capacity = 2 * row_count // owners
    list_dev = centroids.shape[0]
    group = lax.axis_index("grp")
    assert grp_count == 4

    owner_ids = owner_route[:, :, 0]
    hits = owner_ids[:, None, :] == jnp.arange(owners, dtype=jnp.int32)[None, :, None]
    earlier = jnp.arange(row_count)[:, None] < jnp.arange(row_count)[None, :]
    rank = mix(
        hits.reshape(STEPS * owners, row_count).astype(jnp.bfloat16), earlier.astype(jnp.bfloat16)
    )
    rank = jnp.sum(jnp.where(hits, rank.reshape(hits.shape), 0.0), axis=1).astype(jnp.int32)
    dest = owner_ids * capacity + rank
    dest_lanes = dest.reshape(STEPS, 1, row_count)

    places = jnp.arange(owners * capacity, dtype=jnp.int32)
    found = dest[:, None, :] == places[None, :, None]
    slots = jnp.sum(jnp.where(found, list_slot[:, None, :] + 1, 0), axis=2) - 1
    slots = slots.reshape(STEPS, owners, capacity).transpose(1, 0, 2)
    slots = exchange(slots.reshape(owners, 1, STEPS * capacity))

    first = pack_rows(vectors, dest_lanes, 0, owners, capacity, 1)
    first, slots = gate(first, slots)
    received0 = exchange(first)
    second = pack_rows(vectors, dest_lanes, 1, owners, capacity, 1)
    third = pack_rows(vectors, dest_lanes, 2, owners, capacity, 2)

    slots = slots.reshape(owners, STEPS, capacity).transpose(1, 0, 2)
    slots = slots.reshape(STEPS, owners * capacity)
    slot_cols = slots.T
    dest_cols = dest.T

    list_iota = jnp.arange(list_dev, dtype=jnp.int32)
    batch = jnp.sum((slots[:, None, :] == list_iota[None, :, None]).astype(jnp.int32), axis=2)
    batch = sum([batch] + [swap(batch, "grp", offset) for offset in range(1, grp_count)])
    weights = [counts]
    for step in range(STEPS):
        weights.append(weights[-1] + batch[step])
    weights = jnp.stack(weights).astype(jnp.float32).T

    high = group // 2
    low = (group ^ high) % 2
    places = jnp.stack([2 * low + high, 2 * high + low]).astype(jnp.int32)
    order = jnp.where(slots < list_dev // 2, places[0], places[1]) * (list_dev // 8)
    relative_slots = jnp.where(slots < 0, -1, slots ^ order).reshape(STEPS, 1, owners * capacity)

    def sums_of(rows, step):
        return list_sums(rows, 0, relative_slots, step, list_dev)

    def residual(rows, step, parts, into=None, place=0, count=1):
        return residual_rows(
            rows, 0, slot_cols, step, centroids, weights, parts, places, into, place, count
        )

    second, third, slot_cols, weights, received0 = gate(second, third, slot_cols, weights, received0)
    received1 = exchange(second)

    done = scatter_sum(sums_of(received0, 0))
    buffer = residual(received0, 0, [], third, 1, 2)
    buffer, done, received1 = gate(buffer, done, received1)
    mixed = exchange(buffer)

    whole = gather_sum(done)
    parts = [whole]
    done = scatter_sum(sums_of(received1, 1))
    buffer = residual(received1, 1, parts)
    whole = gather_sum(done)
    buffer, whole, mixed = gate(buffer, whole, mixed)
    back1 = exchange(buffer)

    parts = parts + [whole]
    done = scatter_sum(sums_of(mixed, 2))
    buffer = residual(mixed, 2, parts)
    buffer, done, back1 = gate(buffer, done, back1)
    back2 = exchange(buffer)

    parts = parts + [gather_sum(done)]
    current = new_rows(centroids, weights, parts, places)
    output = unpack_rows(mixed, 1, dest_cols, 0, None, row_count)
    output = unpack_rows(back1, 0, dest_cols, 1, output, row_count)
    output = unpack_rows(back2, 0, dest_cols, 2, output, row_count)
    return (output, current)


def solution(mesh):
    in_specs = (
        P(None, ("grp", "list"), None),
        P(None, ("grp", "list"), None),
        P(None, ("grp", "list")),
        P("list", None),
        P("list"),
    )
    out_specs = (P(None, ("grp", "list"), None), P("list", None))
    return jax.shard_map(local, mesh=mesh, in_specs=in_specs, out_specs=out_specs, check_vma=False)
```

time: 398 us -> 273 us (0.69)
  waiting for transfers between devices: 199 us -> 78 us
  Pallas kernels: 0 us -> 87 us
  local copies, waits for them, and re-layouts: 64.6 us -> 6.99 us
  starting transfers between devices: 57.4 us -> 81.9 us
  other arithmetic: 33.6 us -> 16.4 us
  matrix products: 14.1 us -> 0.24 us
  between operations: 14.3 us -> 1.18 us
  blocking collectives: 12.2 us -> 0 us
    psum x1 -> x0, waiting for transfers between devices: 93.4 us -> none  [local(): lax.psum(sums.astype(jnp.bfloat16), 'grp').astype(jnp.float32)]
    all_to_all x9 -> x6, waiting for transfers between devices: 105 us -> 12.7 us  [exchange(): return lax.all_to_all(rows, 'list', split_axis=0, concat_axis=0, tiled=True)]
    pallas_call x0 -> x13, Pallas kernels: none -> 87 us  [the longest x3 39.8 us: residual_rows(): pl.pallas_call(body, grid_spec=pltpu.PrefetchScalarGridSpec(num_scalar_pr...]
    ppermute x0 -> x27, waiting for transfers between devices: none -> 65.4 us  [swap(): return lax.ppermute(rows, axis, [(i, i ^ offset) for i in range(count)])]
    ppermute x0 -> x27, starting transfers between devices: none -> 39.5 us  [swap(): return lax.ppermute(rows, axis, [(i, i ^ offset) for i in range(count)])]
    gather x6 -> x0, local copies, waits for them, and re-layouts: 37 us -> none  [the longest x3 25.8 us: route_fn(): chosen = table[jnp.clip(list_ids, 0, list_dev - 1)]]
    scatter x6 -> x0, local copies, waits for them, and re-layouts: 21.7 us -> none  [the longest x3 14.4 us: local(): send_rows = jnp.zeros((owner_count * capacity, width), jnp.bfloat16).at[d...]
    all_to_all x9 -> x6, starting transfers between devices: 57.3 us -> 42.4 us  [exchange(): return lax.all_to_all(rows, 'list', split_axis=0, concat_axis=0, tiled=True)]
  transfers between devices with their start and end apart: 10 -> 33, of which waited for: 9 -> 13; matrix products, arithmetic and copies ran while one was open for 22% -> 7% of each run, Pallas kernels for 0% -> 31%
where the time goes in v2:
time: 273 us; the launch traced here: 272 us
  Pallas kernels  87 us (32%)
  starting transfers between devices  81.9 us (30%)
  waiting for transfers between devices  78 us (29%)
  other arithmetic  16.4 us (6%)
  local copies, waits for them, and re-layouts  6.99 us (3%)
    ppermute x27, waiting for transfers between devices, swap(): return lax.ppermute(rows, axis, [(i, i ^ offset) for i in range(count)])  65.4 us
    all_to_all x6, starting transfers between devices, exchange(): return lax.all_to_all(rows, 'list', split_axis=0, concat_axis=0, tiled=True)  42.4 us
    pallas_call x3, Pallas kernels, residual_rows(): pl.pallas_call(body, grid_spec=pltpu.PrefetchScalarGridSpec(num_scalar_pr...  39.8 us
    ppermute x27, starting transfers between devices, swap(): return lax.ppermute(rows, axis, [(i, i ^ offset) for i in range(count)])  39.5 us
    pallas_call x3, Pallas kernels, list_sums(): pl.pallas_call(body, grid=(1,), in_specs=[pl.BlockSpec((1, 1, rows), lamb...  14.5 us
    all_to_all x6, waiting for transfers between devices, exchange(): return lax.all_to_all(rows, 'list', split_axis=0, concat_axis=0, tiled=True)  12.7 us
    pallas_call x3, Pallas kernels, unpack_rows(): pl.pallas_call(body, grid=(1,), in_specs=in_specs, out_specs=pl.BlockSpec...  11.8 us
    convert_element_type x12, other arithmetic, add(): return total.astype(jnp.bfloat16)  11.2 us
  transfers between devices with their start and end apart: 33, of which 13 were waited for; matrix products, arithmetic and copies ran while one was open for 7% of the time, Pallas kernels for 31%

profile of v2, /device:TPU:2, one launch (start us, length us, event | category | flops | bytes accessed | tf_op | source)
XLA Modules:
  0.0 271.7 jit_solution(13714903427325675117)
XLA Ops:
  4.6 7.6 %all-to-all-start = ((s32[32,1,96]{2,1,0:T(1,128)}), s32[32,1,96]{2,1,0:T(1,128)S(1)}, u32[]{:S(2)}, u32[]{:S(2)}) async-start(s32[32,1,96]{2,1,0:T(1,128)} %bitcast.8), calls=%async_computation | async-start | bytes 32768 | tf_op jit(solution)/shard_map/all_to_all | solution.py:271
  18.2 5.7 %all-to-all-start.1 = ((bf16[32,1,32,1024]{3,2,1,0:T(8,128)(2,1)}), bf16[32,1,32,1024]{3,2,1,0:T(8,128)(2,1)S(1)}, u32[]{:S(2)}, u32[]{:S(2)}) async-start(bf16[32,1,32,1024]{3,2,1,0:T(8,128)(2,1)} %pack_rows.5), calls=%async_computation.1 | async-start | bytes 4194304 | tf_op jit(solution)/shard_map/all_to_all | solution.py:271
  27.3 4.1 %collective-permute-start.2 = (s32[3,1024]{1,0:T(4,128)S(1)}, s32[3,1024]{1,0:T(4,128)S(1)}, u32[]{:S(2)}, u32[]{:S(2)}) collective-permute-start(s32[3,1024]{1,0:T(4,128)S(1)} %convert_reduce_fusion), channel_id=1, source_target_pairs={{0,96},{32,64},{64,32},{96,0},{1,97},{33,65},{65,33},{97,1},{2,98}... | collective-permute-start | bytes 36872 | tf_op jit(solution)/shard_map/ppermute | solution.py:19
  40.9 11.0 %all-to-all-done.1.row_ref = bf16[32,1,32,1024]{3,2,1,0:T(8,128)(2,1)S(1)} async-done(((bf16[32,1,32,1024]{3,2,1,0:T(8,128)(2,1)}), bf16[32,1,32,1024]{3,2,1,0:T(8,128)(2,1)S(1)}, u32[]{:S(2)}, u32[]{:S(2)}) %all-to-all-start.1) | async-done | bytes 2097184 | tf_op jit(solution)/shard_map/all_to_all | solution.py:271
  51.8 6.7 %all-to-all-start.2 = ((bf16[32,1,32,1024]{3,2,1,0:T(8,128)(2,1)}), bf16[32,1,32,1024]{3,2,1,0:T(8,128)(2,1)}, u32[]{:S(2)}, u32[]{:S(2)}) async-start(bf16[32,1,32,1024]{3,2,1,0:T(8,128)(2,1)} %pack_rows.3), calls=%async_computation.2 | async-start | bytes 4194304 | tf_op jit(solution)/shard_map/all_to_all | solution.py:271
  59.3 4.9 %list_sums.3 = (bf16[128,1024]{1,0:T(8,128)(2,1)}, bf16[128,1024]{1,0:T(8,128)(2,1)}, bf16[256,1024]{1,0:T(8,128)(2,1)}, bf16[128,1024]{1,0:T(8,128)(2,1)}, bf16...) custom-call(s32[3,1,1024]{2,1,0:T(1,128)} %compare_select_fusion.1.slot_ref, bf16[32,1,32,1024]{3,2,1,0:T(8,128)(2,1)} %copy-done), custom_call_target="tpu_custom_call" | custom-call | flops 1 | bytes 1 | tf_op jit(solution)/shard_map/list_sums/pallas_call | solution.py:70
  68.6 9.9 %collective-permute-done.3 = bf16[256,1024]{1,0:T(8,128)(2,1)S(1)} collective-permute-done((bf16[256,1024]{1,0:T(8,128)(2,1)}, bf16[256,1024]{1,0:T(8,128)(2,1)S(1)}, u32[]{:S(2)}, u32[]{:S(2)}) %collective-permute-start.3) | collective-permute-done | bytes 524320 | tf_op jit(solution)/shard_map/ppermute | solution.py:19
  79.5 4.0 %collective-permute-start.4 = (bf16[128,1024]{1,0:T(8,128)(2,1)S(1)}, bf16[128,1024]{1,0:T(8,128)(2,1)S(1)}, u32[]{:S(2)}, u32[]{:S(2)}) collective-permute-start(bf16[128,1024]{1,0:T(8,128)(2,1)S(1)} %add_convert_fusion.11), channel_id=1, source_target_pairs={{0,96},{32,64},{64,32},{96,0},{1,97},{33,65},{65,33},{97,1},{2,98}... | collective-permute-start | bytes 786440 | tf_op jit(solution)/shard_map/ppermute | solution.py:19
  85.4 12.0 %residual_rows.3 = bf16[32,2,32,1024]{3,2,1,0:T(8,128)(2,1)} custom-call(s32[2]{0:T(128)} %pad_add_fusion.place_ref, s32[1024,3]{1,0:T(8,128)} %bitcast.31, bf16[32,1,32,1024]{3,2,1,0:T(8,128)(2,1)} %copy-done, f32[1024,1024]{1,0:T(8,128)} %table_ref.7, f32[1024,4]{1,0:T(8,128)} %bitcast.26, ...), custom_call_target="tpu_custom_call", output_to_operand_aliasing={{}: (5, {})} | custom-call | flops 1 | bytes 1 | tf_op jit(solution)/shard_map/residual_rows/pallas_call | solution.py:172
  97.7 7.5 %all-to-all-start.3 = ((bf16[32,2,32,1024]{3,2,1,0:T(8,128)(2,1)}), bf16[32,2,32,1024]{3,2,1,0:T(8,128)(2,1)}, u32[]{:S(2)}, u32[]{:S(2)}) async-start(bf16[32,2,32,1024]{3,2,1,0:T(8,128)(2,1)} %residual_rows.3), calls=%async_computation.3 | async-start | bytes 8388608 | tf_op jit(solution)/shard_map/all_to_all | solution.py:271
  105.3 4.8 %list_sums.4 = (bf16[128,1024]{1,0:T(8,128)(2,1)}, bf16[128,1024]{1,0:T(8,128)(2,1)}, bf16[256,1024]{1,0:T(8,128)(2,1)}, bf16[128,1024]{1,0:T(8,128)(2,1)}, bf16...) custom-call(s32[3,1,1024]{2,1,0:T(1,128)} %compare_select_fusion.1.slot_ref, ...), custom_call_target="tpu_custom_call" | custom-call | flops 1 | bytes 1 | tf_op jit(solution)/shard_map/list_sums/pallas_call | solution.py:70
  115.3 9.2 %collective-permute-done.11 = bf16[256,1024]{1,0:T(8,128)(2,1)S(1)} collective-permute-done((bf16[256,1024]{1,0:T(8,128)(2,1)}, bf16[256,1024]{1,0:T(8,128)(2,1)S(1)}, u32[]{:S(2)}, u32[]{:S(2)}) %collective-permute-start.11) | collective-permute-done | bytes 524320 | tf_op jit(solution)/shard_map/ppermute | solution.py:19
  131.5 6.9 %collective-permute-done.12 = bf16[128,1024]{1,0:T(8,128)(2,1)S(1)} collective-permute-done((bf16[128,1024]{1,0:T(8,128)(2,1)S(1)}, bf16[128,1024]{1,0:T(8,128)(2,1)S(1)}, u32[]{:S(2)}, u32[]{:S(2)}) %collective-permute-start.12) | collective-permute-done | bytes 262176 | tf_op jit(solution)/shard_map/ppermute | solution.py:19
  145.3 4.7 %collective-permute-done.13 = bf16[128,1024]{1,0:T(8,128)(2,1)S(1)} collective-permute-done((bf16[128,1024]{1,0:T(8,128)(2,1)S(1)}, bf16[128,1024]{1,0:T(8,128)(2,1)S(1)}, u32[]{:S(2)}, u32[]{:S(2)}) %collective-permute-start.13) | collective-permute-done | bytes 262176 | tf_op jit(solution)/shard_map/ppermute | solution.py:19
  152.4 8.2 %collective-permute-done.8.rest_1_ = bf16[256,1024]{1,0:T(8,128)(2,1)S(1)} collective-permute-done((bf16[256,1024]{1,0:T(8,128)(2,1)S(1)}, bf16[256,1024]{1,0:T(8,128)(2,1)S(1)}, u32[]{:S(2)}, u32[]{:S(2)}) %collective-permute-start.8) | collective-permute-done | bytes 524320 | tf_op jit(solution)/shard_map/ppermute | solution.py:19
  162.2 13.6 %residual_rows.4 = bf16[32,1,32,1024]{3,2,1,0:T(8,128)(2,1)} custom-call(s32[2]{0:T(128)} %pad_add_fusion.place_ref, s32[1024,3]{1,0:T(8,128)} %bitcast.32, bf16[32,1,32,1024]{3,2,1,0:T(8,128)(2,1)} %all-to-all-done.2.row_ref, f32[1024,1024]{1,0:T(8,128)} %table_ref.7, f32[1024,4]{1,0:T(8,128)} %bitcast.27, bf16[256,1024]{1,0:T(8,128)(2,1)} %copy-done.4, ...), custom_call_target="tpu_custom_call" | custom-call | flops 1 | bytes 1 | tf_op jit(solution)/shard_map/residual_rows/pallas_call | solution.py:172
  175.8 7.4 %all-to-all-start.4 = ((bf16[32,1,32,1024]{3,2,1,0:T(8,128)(2,1)}), bf16[32,1,32,1024]{3,2,1,0:T(8,128)(2,1)S(1)}, u32[]{:S(2)}, u32[]{:S(2)}) async-start(bf16[32,1,32,1024]{3,2,1,0:T(8,128)(2,1)} %residual_rows.4), calls=%async_computation.4 | async-start | bytes 4194304 | tf_op jit(solution)/shard_map/all_to_all | solution.py:271
  183.2 4.8 %list_sums.5 = (bf16[128,1024]{1,0:T(8,128)(2,1)}, bf16[128,1024]{1,0:T(8,128)(2,1)}, bf16[256,1024]{1,0:T(8,128)(2,1)}, bf16[128,1024]{1,0:T(8,128)(2,1)}, bf16...) custom-call(s32[3,1,1024]{2,1,0:T(1,128)} %compare_select_fusion.1.slot_ref, ...), custom_call_target="tpu_custom_call" | custom-call | flops 1 | bytes 1 | tf_op jit(solution)/shard_map/list_sums/pallas_call | solution.py:70
  191.0 11.2 %collective-permute-done.19 = bf16[256,1024]{1,0:T(8,128)(2,1)S(1)} collective-permute-done((bf16[256,1024]{1,0:T(8,128)(2,1)}, bf16[256,1024]{1,0:T(8,128)(2,1)S(1)}, u32[]{:S(2)}, u32[]{:S(2)}) %collective-permute-start.19) | collective-permute-done | bytes 524320 | tf_op jit(solution)/shard_map/ppermute | solution.py:19
  208.0 14.3 %residual_rows.5 = bf16[32,1,32,1024]{3,2,1,0:T(8,128)(2,1)} custom-call(s32[2]{0:T(128)} %pad_add_fusion.place_ref, s32[1024,3]{1,0:T(8,128)} %bitcast.33, bf16[32,2,32,1024]{3,2,1,0:T(8,128)(2,1)} %all-to-all-done.3.row_ref, f32[1024,1024]{1,0:T(8,128)} %table_ref.7, f32[1024,4]{1,0:T(8,128)} %bitcast.28, bf16[256,1024]{1,0:T(8,128)(2,1)} %copy-done.4, ...), custom_call_target="tpu_custom_call" | custom-call | flops 1 | bytes 1 | tf_op jit(solution)/shard_map/residual_rows/pallas_call | solution.py:172
  225.3 7.4 %all-to-all-start.5 = ((bf16[32,1,32,1024]{3,2,1,0:T(8,128)(2,1)}), bf16[32,1,32,1024]{3,2,1,0:T(8,128)(2,1)}, u32[]{:S(2)}, u32[]{:S(2)}) async-start(bf16[32,1,32,1024]{3,2,1,0:T(8,128)(2,1)} %residual_rows.5), calls=%async_computation.5 | async-start | bytes 4194304 | tf_op jit(solution)/shard_map/all_to_all | solution.py:271
  235.9 6.7 %collective-permute-done.23 = bf16[128,1024]{1,0:T(8,128)(2,1)S(1)} collective-permute-done((bf16[128,1024]{1,0:T(8,128)(2,1)}, bf16[128,1024]{1,0:T(8,128)(2,1)S(1)}, u32[]{:S(2)}, u32[]{:S(2)}) %collective-permute-start.23) | collective-permute-done | bytes 262176 | tf_op jit(solution)/shard_map/ppermute | solution.py:19
  257.9 9.8 %new_rows.1 = f32[1024,1024]{1,0:T(8,128)} custom-call(s32[2]{0:T(128)} %pad_add_fusion.place_ref, f32[1024,1024]{1,0:T(8,128)} %table_ref.7, f32[1024,4]{1,0:T(8,128)} %bitcast.29, bf16[256,1024]{1,0:T(8,128)(2,1)} %copy-done.4, bf16[256,1024]{1,0:T(8,128)(2,1)} %copy-done.6, bf16[256,1024]{1,0:T(8,128)(2,1)} %copy-done.5, bf16[256,1024]{1,0:T(8,128)(2,1)} %copy-done.7, ...), custom_call_target="tpu_custom_call" | custom-call | flops 1 | bytes 1 | tf_op jit(solution)/shard_map/new_rows/pallas_call | solution.py:200
  267.7 4.0 %unpack_rows.5 = bf16[3,512,1024]{2,1,0:T(8,128)(2,1)} custom-call(s32[512,3]{1,0:T(8,128)} %bitcast.36, bf16[32,1,32,1024]{3,2,1,0:T(8,128)(2,1)} %all-to-all-done.5.row_ref, bf16[3,512,1024]{2,1,0:T(8,128)(2,1)} %unpack_rows.4.rest_0_), custom_call_target="tpu_custom_call", output_to_operand_aliasing={{}: (2, {})} | custom-call | flops 1 | bytes 1 | tf_op jit(solution)/shard_map/unpack_rows/pallas_call | solution.py:238
  (138 shorter events, 84.1 us)
Async XLA Ops:
  4.6 13.7 %all-to-all-start = ((s32[32,1,96]{2,1,0:T(1,128)}), s32[32,1,96]{2,1,0:T(1,128)S(1)}, u32[]{:S(2)}, u32[]{:S(2)}) async-start(s32[32,1,96]{2,1,0:T(1,128)} %bitcast.8), calls=%async_computation | async-start | bytes 32768 | tf_op jit(solution)/shard_map/all_to_all | solution.py:271
  18.2 33.6 %all-to-all-start.1 = ((bf16[32,1,32,1024]{3,2,1,0:T(8,128)(2,1)}), bf16[32,1,32,1024]{3,2,1,0:T(8,128)(2,1)S(1)}, u32[]{:S(2)}, u32[]{:S(2)}) async-start(bf16[32,1,32,1024]{3,2,1,0:T(8,128)(2,1)} %pack_rows.5), calls=%async_computation.1 | async-start | bytes 4194304 | tf_op jit(solution)/shard_map/all_to_all | solution.py:271
  51.8 45.9 %all-to-all-start.2 = ((bf16[32,1,32,1024]{3,2,1,0:T(8,128)(2,1)}), bf16[32,1,32,1024]{3,2,1,0:T(8,128)(2,1)}, u32[]{:S(2)}, u32[]{:S(2)}) async-start(bf16[32,1,32,1024]{3,2,1,0:T(8,128)(2,1)} %pack_rows.3), calls=%async_computation.2 | async-start | bytes 4194304 | tf_op jit(solution)/shard_map/all_to_all | solution.py:271
  64.2 14.4 %collective-permute-start.3 = (bf16[256,1024]{1,0:T(8,128)(2,1)}, bf16[256,1024]{1,0:T(8,128)(2,1)S(1)}, u32[]{:S(2)}, u32[]{:S(2)}) collective-permute-start(bf16[256,1024]{1,0:T(8,128)(2,1)} %get-tuple-element.48), channel_id=1, source_target_pairs={{0,32},{32,0},{64,96},{96,64},{1,33},{33,1},{65,97},{97,65},{2,34}... | collective-permute-start | bytes 1572872 | tf_op jit(solution)/shard_map/ppermute | solution.py:19
  66.1 17.4 %collective-permute-start.5 = (bf16[256,1024]{1,0:T(8,128)(2,1)}, bf16[256,1024]{1,0:T(8,128)(2,1)S(1)}, u32[]{:S(2)}, u32[]{:S(2)}) collective-permute-start(bf16[256,1024]{1,0:T(8,128)(2,1)} %get-tuple-element.51), channel_id=1, source_target_pairs={{0,96},{32,64},{64,32},{96,0},{1,97},{33,65},{65,33},{97,1},{2,98}... | collective-permute-start | bytes 1572872 | tf_op jit(solution)/shard_map/ppermute | solution.py:19
  79.5 17.9 %collective-permute-start.4 = (bf16[128,1024]{1,0:T(8,128)(2,1)S(1)}, bf16[128,1024]{1,0:T(8,128)(2,1)S(1)}, u32[]{:S(2)}, u32[]{:S(2)}) collective-permute-start(bf16[128,1024]{1,0:T(8,128)(2,1)S(1)} %add_convert_fusion.11), channel_id=1, source_target_pairs={{0,96},{32,64},{64,32},{96,0},{1,97},{33,65},{65,33},{97,1},{2,98}... | collective-permute-start | bytes 786440 | tf_op jit(solution)/shard_map/ppermute | solution.py:19
  84.5 13.0 %collective-permute-start.6 = (bf16[128,1024]{1,0:T(8,128)(2,1)S(1)}, bf16[128,1024]{1,0:T(8,128)(2,1)S(1)}, u32[]{:S(2)}, u32[]{:S(2)}) collective-permute-start(bf16[128,1024]{1,0:T(8,128)(2,1)S(1)} %add_convert_fusion.9), channel_id=1, source_target_pairs={{0,32},{32,0},{64,96},{96,64},{1,33},{33,1},{65,97},{97,65},{2,34}... | collective-permute-start | bytes 786440 | tf_op jit(solution)/shard_map/ppermute | solution.py:19
  97.7 78.1 %all-to-all-start.3 = ((bf16[32,2,32,1024]{3,2,1,0:T(8,128)(2,1)}), bf16[32,2,32,1024]{3,2,1,0:T(8,128)(2,1)}, u32[]{:S(2)}, u32[]{:S(2)}) async-start(bf16[32,2,32,1024]{3,2,1,0:T(8,128)(2,1)} %residual_rows.3), calls=%async_computation.3 | async-start | bytes 8388608 | tf_op jit(solution)/shard_map/all_to_all | solution.py:271
  110.1 14.4 %collective-permute-start.11 = (bf16[256,1024]{1,0:T(8,128)(2,1)}, bf16[256,1024]{1,0:T(8,128)(2,1)S(1)}, u32[]{:S(2)}, u32[]{:S(2)}) collective-permute-start(bf16[256,1024]{1,0:T(8,128)(2,1)} %get-tuple-element.58), channel_id=1, source_target_pairs={{0,32},{32,0},{64,96},{96,64},{1,33},{33,1},{65,97},{97,65},{2,34}... | collective-permute-start | bytes 1572872 | tf_op jit(solution)/shard_map/ppermute | solution.py:19
  112.1 16.2 %collective-permute-start.15 = (bf16[256,1024]{1,0:T(8,128)(2,1)}, bf16[256,1024]{1,0:T(8,128)(2,1)S(1)}, u32[]{:S(2)}, u32[]{:S(2)}) collective-permute-start(bf16[256,1024]{1,0:T(8,128)(2,1)} %get-tuple-element.61), channel_id=1, source_target_pairs={{0,96},{32,64},{64,32},{96,0},{1,97},{33,65},{65,33},{97,1},{2,98}... | collective-permute-start | bytes 1572872 | tf_op jit(solution)/shard_map/ppermute | solution.py:19
  112.3 27.8 %collective-permute-start.7 = (bf16[128,1024]{1,0:T(8,128)(2,1)S(1)}, bf16[128,1024]{1,0:T(8,128)(2,1)S(1)}, u32[]{:S(2)}, u32[]{:S(2)}) collective-permute-start(bf16[128,1024]{1,0:T(8,128)(2,1)S(1)} %add_convert_fusion.10), channel_id=1, source_target_pairs={{0,96},{32,64},{64,32},{96,0},{1,97},{33,65},{65,33},{97,1},{2,98}... | collective-permute-start | bytes 786440 | tf_op jit(solution)/shard_map/ppermute | solution.py:19
  125.6 12.9 %collective-permute-start.12 = (bf16[128,1024]{1,0:T(8,128)(2,1)S(1)}, bf16[128,1024]{1,0:T(8,128)(2,1)S(1)}, u32[]{:S(2)}, u32[]{:S(2)}) collective-permute-start(bf16[128,1024]{1,0:T(8,128)(2,1)S(1)} %add_convert_fusion.7), channel_id=1, source_target_pairs={{0,96},{32,64},{64,32},{96,0},{1,97},{33,65},{65,33},{97,1},{2,98}... | collective-permute-start | bytes 786440 | tf_op jit(solution)/shard_map/ppermute | solution.py:19
  140.2 20.4 %collective-permute-start.8 = (bf16[256,1024]{1,0:T(8,128)(2,1)S(1)}, bf16[256,1024]{1,0:T(8,128)(2,1)S(1)}, u32[]{:S(2)}, u32[]{:S(2)}) collective-permute-start(bf16[256,1024]{1,0:T(8,128)(2,1)S(1)} %constant_dynamic-update-slice_fusion.rest_0_), channel_id=1, source_target_pairs={{0,32},{32,0},{64,96},{96,64},{1,33},{33,1},{65,97},{97,65},{2,34}... | collective-permute-start | bytes 1572872 | tf_op jit(solution)/shard_map/ppermute | solution.py:19
  142.3 19.0 %collective-permute-start.10 = (bf16[256,1024]{1,0:T(8,128)(2,1)S(1)}, bf16[256,1024]{1,0:T(8,128)(2,1)S(1)}, u32[]{:S(2)}, u32[]{:S(2)}) collective-permute-start(bf16[256,1024]{1,0:T(8,128)(2,1)S(1)} %constant_dynamic-update-slice_fusion.2.rest_2_), channel_id=1, source_target_pairs={{0,96},{32,64},{64,32},{96,0},{1,97},{33,65},{65,33},{97,1},{2,98}... | collective-permute-start | bytes 1572872 | tf_op jit(solution)/shard_map/ppermute | solution.py:19
  150.1 25.7 %collective-permute-start.14 = (bf16[256,1024]{1,0:T(8,128)(2,1)S(1)}, bf16[256,1024]{1,0:T(8,128)(2,1)}, u32[]{:S(2)}, u32[]{:S(2)}) collective-permute-start(bf16[256,1024]{1,0:T(8,128)(2,1)S(1)} %pad_maximum_fusion.rest_4_), channel_id=1, source_target_pairs={{0,32},{32,0},{64,96},{96,64},{1,33},{33,1},{65,97},{97,65},{2,34}... | collective-permute-start | bytes 1572872 | tf_op jit(solution)/shard_map/ppermute | solution.py:19
  150.3 25.5 %collective-permute-start.18 = (bf16[256,1024]{1,0:T(8,128)(2,1)S(1)}, bf16[256,1024]{1,0:T(8,128)(2,1)}, u32[]{:S(2)}, u32[]{:S(2)}) collective-permute-start(bf16[256,1024]{1,0:T(8,128)(2,1)S(1)} %pad_maximum_fusion.1.rest_6_), channel_id=1, source_target_pairs={{0,96},{32,64},{64,32},{96,0},{1,97},{33,65},{65,33},{97,1},{2,98}... | collective-permute-start | bytes 1572872 | tf_op jit(solution)/shard_map/ppermute | solution.py:19
  175.8 49.4 %all-to-all-start.4 = ((bf16[32,1,32,1024]{3,2,1,0:T(8,128)(2,1)}), bf16[32,1,32,1024]{3,2,1,0:T(8,128)(2,1)S(1)}, u32[]{:S(2)}, u32[]{:S(2)}) async-start(bf16[32,1,32,1024]{3,2,1,0:T(8,128)(2,1)} %residual_rows.4), calls=%async_computation.4 | async-start | bytes 4194304 | tf_op jit(solution)/shard_map/all_to_all | solution.py:271
  188.0 14.2 %collective-permute-start.19 = (bf16[256,1024]{1,0:T(8,128)(2,1)}, bf16[256,1024]{1,0:T(8,128)(2,1)S(1)}, u32[]{:S(2)}, u32[]{:S(2)}) collective-permute-start(bf16[256,1024]{1,0:T(8,128)(2,1)} %get-tuple-element.70), channel_id=1, source_target_pairs={{0,32},{32,0},{64,96},{96,64},{1,33},{33,1},{65,97},{97,65},{2,34}... | collective-permute-start | bytes 1572872 | tf_op jit(solution)/shard_map/ppermute | solution.py:19
  188.0 18.2 %collective-permute-start.21 = (bf16[256,1024]{1,0:T(8,128)(2,1)}, bf16[256,1024]{1,0:T(8,128)(2,1)S(1)}, u32[]{:S(2)}, u32[]{:S(2)}) collective-permute-start(bf16[256,1024]{1,0:T(8,128)(2,1)} %get-tuple-element.73), channel_id=1, source_target_pairs={{0,96},{32,64},{64,32},{96,0},{1,97},{33,65},{65,33},{97,1},{2,98}... | collective-permute-start | bytes 1572872 | tf_op jit(solution)/shard_map/ppermute | solution.py:19
  203.2 19.0 %collective-permute-start.20 = (bf16[128,1024]{1,0:T(8,128)(2,1)S(1)}, bf16[128,1024]{1,0:T(8,128)(2,1)}, u32[]{:S(2)}, u32[]{:S(2)}) collective-permute-start(bf16[128,1024]{1,0:T(8,128)(2,1)S(1)} %add_convert_fusion.3), channel_id=1, source_target_pairs={{0,96},{32,64},{64,32},{96,0},{1,97},{33,65},{65,33},{97,1},{2,98}... | collective-permute-start | bytes 786440 | tf_op jit(solution)/shard_map/ppermute | solution.py:19
  208.0 16.1 %collective-permute-start.22 = (bf16[128,1024]{1,0:T(8,128)(2,1)}, bf16[128,1024]{1,0:T(8,128)(2,1)}, u32[]{:S(2)}, u32[]{:S(2)}) collective-permute-start(bf16[128,1024]{1,0:T(8,128)(2,1)} %add_convert_fusion.1), channel_id=1, source_target_pairs={{0,32},{32,0},{64,96},{96,64},{1,33},{33,1},{65,97},{97,65},{2,34}... | collective-permute-start | bytes 786440 | tf_op jit(solution)/shard_map/ppermute | solution.py:19
  225.3 42.5 %all-to-all-start.5 = ((bf16[32,1,32,1024]{3,2,1,0:T(8,128)(2,1)}), bf16[32,1,32,1024]{3,2,1,0:T(8,128)(2,1)}, u32[]{:S(2)}, u32[]{:S(2)}) async-start(bf16[32,1,32,1024]{3,2,1,0:T(8,128)(2,1)} %residual_rows.5), calls=%async_computation.5 | async-start | bytes 4194304 | tf_op jit(solution)/shard_map/all_to_all | solution.py:271
  242.6 13.4 %collective-permute-start.24 = (bf16[256,1024]{1,0:T(8,128)(2,1)S(1)}, bf16[256,1024]{1,0:T(8,128)(2,1)}, u32[]{:S(2)}, u32[]{:S(2)}) collective-permute-start(bf16[256,1024]{1,0:T(8,128)(2,1)S(1)} %constant_dynamic-update-slice_fusion.4.rest_8_), channel_id=1, source_target_pairs={{0,32},{32,0},{64,96},{96,64},{1,33},{33,1},{65,97},{97,65},{2,34}... | collective-permute-start | bytes 1572872 | tf_op jit(solution)/shard_map/ppermute | solution.py:19
  243.5 14.4 %collective-permute-start.26 = (bf16[256,1024]{1,0:T(8,128)(2,1)S(1)}, bf16[256,1024]{1,0:T(8,128)(2,1)}, u32[]{:S(2)}, u32[]{:S(2)}) collective-permute-start(bf16[256,1024]{1,0:T(8,128)(2,1)S(1)} %constant_dynamic-update-slice_fusion.6.rest_10_), channel_id=1, source_target_pairs={{0,96},{32,64},{64,32},{96,0},{1,97},{33,65},{65,33},{97,1},{2,98}... | collective-permute-start | bytes 1572872 | tf_op jit(solution)/shard_map/ppermute | solution.py:19
  (25 other events, 309.9 us)

commit v3 on v2

--- a/solution.py
+++ b/solution.py
@@ -85,12 +85,12 @@
     chunk = table_ref.shape[0]
     slab = 16
 
-    def run(piece, base):
+    def run(piece, flip):
         def one(k, carry):
             at = pl.ds(pl.multiple_of(k * slab, slab), slab)
             table = table_ref[at, :]
             if parts:
-                away = pl.ds(pl.multiple_of(base + k * slab, slab), slab)
+                away = pl.ds(pl.multiple_of((k * slab) ^ flip, slab), slab)
                 total = parts[0][piece][away, :].astype(jnp.float32)
                 for four in parts[1:]:
                     total = total + four[piece][away, :].astype(jnp.float32)
@@ -105,11 +105,11 @@
     if not parts:
         run(0, 0)
         return
-    half = index // 4
-    relative = (index % 4) ^ place_ref[half]
-    mine = 2 * half + relative // 2
+    half = index // 2
+    place = place_ref[half]
+    mine = 2 * half + ((index % 2) ^ (place // 2))
     for piece in range(4):
-        pl.when(mine == piece)(lambda piece=piece: run(piece, (relative % 2) * chunk))
+        pl.when(mine == piece)(lambda piece=piece: run(piece, (place % 2) * (chunk // 2)))
 
 
 def part_specs(parts):
@@ -125,7 +125,7 @@
     list_dev = centroids.shape[0]
     group = BLOCK // capacity
     blocks = owners // group
-    chunks = 8
+    chunks = 4
     chunk = list_dev // chunks
     part_count = 4 * len(parts)
 
@@ -187,32 +187,60 @@
     )(places, *args)
 
 
-def new_rows(centroids, weights, parts, places):
+def new_rows(centroids, weights, parts, places, piece, into):
     list_dev, width = centroids.shape
-    chunk = list_dev // 8
+    chunk = list_dev // 4
+    slab = 16
 
     def body(place_ref, table_ref, weight_ref, *rest):
-        def store(first, at, table):
-            rest[-1][at, :] = table
-
-        update(STEPS, pl.program_id(0), place_ref, weight_ref, table_ref, fours(rest[:-1]), store)
-
+        half = pl.program_id(0)
+
+        def run(which):
+            flip = (place_ref[which] % 2) * (chunk // 2)
+
+            def one(k, carry):
+                at = pl.ds(pl.multiple_of(k * slab, slab), slab)
+                away = pl.ds(pl.multiple_of((k * slab) ^ flip, slab), slab)
+                total = rest[which][away, :].astype(jnp.float32)
+                for four in range(1, STEPS):
+                    total = total + rest[2 * four + which][away, :].astype(jnp.float32)
+                block = weight_ref[at, :]
+                share = 1.0 / block[:, STEPS : STEPS + 1]
+                rest[-1][at, :] = (block[:, :1] * table_ref[at, :] + total) * share
+                return carry
+
+            lax.fori_loop(0, chunk // slab, one, 0, unroll=4)
+
+        for which in range(2):
+            pl.when(half == which)(lambda which=which: run(which))
+
+    def chunk_of(i, places):
+        return 2 * i + (piece ^ (places[i] // 2))
+
+    pieces = [four[2 * half + piece] for four in parts for half in range(2)]
+    in_specs = [
+        pl.BlockSpec((chunk, width), lambda i, places: (chunk_of(i, places), 0)),
+        pl.BlockSpec((chunk, STEPS + 1), lambda i, places: (chunk_of(i, places), 0)),
+    ] + [pl.BlockSpec(p.shape, lambda i, places: (0, 0)) for p in pieces]
+    args = [centroids, weights] + pieces
+    aliases = {}
+    if into is not None:
+        in_specs.append(pl.BlockSpec(memory_space=pl.ANY))
+        aliases = {1 + len(args): 0}
+        args.append(into)
     return pl.pallas_call(
         body,
         grid_spec=pltpu.PrefetchScalarGridSpec(
             num_scalar_prefetch=1,
-            grid=(8,),
-            in_specs=[
-                pl.BlockSpec((chunk, width), lambda i, places: (i, 0)),
-                pl.BlockSpec((chunk, STEPS + 1), lambda i, places: (i, 0)),
-            ]
-            + part_specs(parts),
-            out_specs=pl.BlockSpec((chunk, width), lambda i, places: (i, 0)),
+            grid=(2,),
+            in_specs=in_specs,
+            out_specs=pl.BlockSpec((chunk, width), lambda i, places: (chunk_of(i, places), 0)),
         ),
         out_shape=jax.ShapeDtypeStruct((list_dev, width), jnp.float32),
+        input_output_aliases=aliases,
         name="new_rows",
         cost_estimate=CHEAP,
-    )(places, centroids, weights, *[p for four in parts for p in four])
+    )(places, *args)
 
 
 def unpack_rows(back, at, dest, step, into, row_count):
@@ -254,15 +282,21 @@
     return total.astype(jnp.bfloat16)
 
 
-def scatter_sum(parts):
-    got = [swap(parts[2], "grp", 1), swap(parts[5], "grp", 3)]
+def send_far(parts):
+    return [swap(parts[2], "grp", 1), swap(parts[5], "grp", 3)]
+
+
+def send_near(parts, got):
     block = parts[0].shape[0]
     over = [swap(add(parts[3 * h + 1], got[h][block:]), "grp", 3 - 2 * h) for h in range(2)]
     return [add(parts[3 * h], got[h][:block], over[h]) for h in range(2)]
 
 
-def gather_sum(done):
-    own = [jnp.concatenate([done[h], swap(done[h], "grp", 3 - 2 * h)]) for h in range(2)]
+def spread_near(done):
+    return [jnp.concatenate([done[h], swap(done[h], "grp", 3 - 2 * h)]) for h in range(2)]
+
+
+def spread_far(own):
     near = [swap(own[h], "grp", 1 + 2 * h) for h in range(2)]
     return [own[0], near[0], own[1], near[1]]
 
@@ -332,27 +366,37 @@
     second, third, slot_cols, weights, received0 = gate(second, third, slot_cols, weights, received0)
     received1 = exchange(second)
 
-    done = scatter_sum(sums_of(received0, 0))
+    sums = sums_of(received0, 0)
+    got = send_far(sums)
     buffer = residual(received0, 0, [], third, 1, 2)
+    buffer, got = gate(buffer, got)
+    done = send_near(sums, got)
     buffer, done, received1 = gate(buffer, done, received1)
     mixed = exchange(buffer)
 
-    whole = gather_sum(done)
+    own = spread_near(done)
+    received1, own = gate(received1, own)
+    whole = spread_far(own)
+    sums = sums_of(received1, 1)
+    sums, whole = gate(sums, whole)
     parts = [whole]
-    done = scatter_sum(sums_of(received1, 1))
+    got = send_far(sums)
     buffer = residual(received1, 1, parts)
-    whole = gather_sum(done)
-    buffer, whole, mixed = gate(buffer, whole, mixed)
+    buffer, got = gate(buffer, got)
+    own = spread_near(send_near(sums, got))
+    buffer, own, mixed = gate(buffer, own, mixed)
     back1 = exchange(buffer)
 
-    parts = parts + [whole]
-    done = scatter_sum(sums_of(mixed, 2))
+    parts = parts + [spread_far(own)]
+    sums = sums_of(mixed, 2)
+    got = send_far(sums)
     buffer = residual(mixed, 2, parts)
-    buffer, done, back1 = gate(buffer, done, back1)
+    buffer, got, back1 = gate(buffer, got, back1)
     back2 = exchange(buffer)
 
-    parts = parts + [gather_sum(done)]
-    current = new_rows(centroids, weights, parts, places)
+    parts = parts + [spread_far(spread_near(send_near(sums, got)))]
+    current = new_rows(centroids, weights, parts, places, 0, None)
+    current = new_rows(centroids, weights, parts, places, 1, current)
     output = unpack_rows(mixed, 1, dest_cols, 0, None, row_count)
     output = unpack_rows(back1, 0, dest_cols, 1, output, row_count)
     output = unpack_rows(back2, 0, dest_cols, 2, output, row_count)

time: 273 us -> 248 us (0.908)
  waiting for transfers between devices: 78 us -> 66.7 us
  Pallas kernels: 87 us -> 81.9 us
  starting transfers between devices: 81.9 us -> 77.2 us
  other arithmetic: 16.4 us -> 13.1 us
    ppermute x27, waiting for transfers between devices: 65.4 us -> 54 us  [swap(): return lax.ppermute(rows, axis, [(i, i ^ offset) for i in range(count)])]
    ppermute x27, starting transfers between devices: 39.5 us -> 34.5 us  [swap(): return lax.ppermute(rows, axis, [(i, i ^ offset) for i in range(count)])]
    pallas_call x3, Pallas kernels: 39.8 us -> 34.9 us  [residual_rows(): pl.pallas_call(body, grid_spec=pltpu.PrefetchScalarGridSpec(num_scalar_pr...]
    convert_element_type x12, other arithmetic: 11.2 us -> 7.77 us  [add(): return total.astype(jnp.bfloat16)]
    pallas_call x1 -> x2, Pallas kernels: 9.84 us -> 9.68 us  [new_rows(): pl.pallas_call(body, grid_spec=pltpu.PrefetchScalarGridSpec(num_scalar_pr...]
  transfers between devices with their start and end apart: 33 -> 33, of which waited for: 13 -> 18; matrix products, arithmetic and copies ran while one was open for 7% -> 6% of each run, Pallas kernels for 31% -> 32%
where the time goes in v3:
time: 248 us; the launch traced here: 247 us
  Pallas kernels  81.9 us (33%)
  starting transfers between devices  77.2 us (31%)
  waiting for transfers between devices  66.7 us (27%)
  other arithmetic  13.1 us (5%)
  local copies, waits for them, and re-layouts  6.58 us (3%)
    ppermute x27, waiting for transfers between devices, swap(): return lax.ppermute(rows, axis, [(i, i ^ offset) for i in range(count)])  54 us
    all_to_all x6, starting transfers between devices, exchange(): return lax.all_to_all(rows, 'list', split_axis=0, concat_axis=0, tiled=True)  42.7 us
    pallas_call x3, Pallas kernels, residual_rows(): pl.pallas_call(body, grid_spec=pltpu.PrefetchScalarGridSpec(num_scalar_pr...  34.9 us
    ppermute x27, starting transfers between devices, swap(): return lax.ppermute(rows, axis, [(i, i ^ offset) for i in range(count)])  34.5 us
    pallas_call x3, Pallas kernels, list_sums(): pl.pallas_call(body, grid=(1,), in_specs=[pl.BlockSpec((1, 1, rows), lamb...  14.5 us
    all_to_all x6, waiting for transfers between devices, exchange(): return lax.all_to_all(rows, 'list', split_axis=0, concat_axis=0, tiled=True)  12.7 us
    pallas_call x3, Pallas kernels, unpack_rows(): pl.pallas_call(body, grid=(1,), in_specs=in_specs, out_specs=pl.BlockSpec...  11.8 us
    pallas_call x3, Pallas kernels, pack_rows(): pl.pallas_call(body, grid=(owners // group,), in_specs=[pl.BlockSpec((1,...  10.9 us
  transfers between devices with their start and end apart: 33, of which 18 were waited for; matrix products, arithmetic and copies ran while one was open for 6% of the time, Pallas kernels for 32%

profile of v3, /device:TPU:2, one launch (start us, length us, event | category | flops | bytes accessed | tf_op | source)
XLA Modules:
  0.0 247.0 jit_solution(2979690244931700030)
XLA Ops:
  4.5 7.6 %all-to-all-start = ((s32[32,1,96]{2,1,0:T(1,128)}), s32[32,1,96]{2,1,0:T(1,128)S(1)}, u32[]{:S(2)}, u32[]{:S(2)}) async-start(s32[32,1,96]{2,1,0:T(1,128)} %bitcast.8), calls=%async_computation | async-start | bytes 32768 | tf_op jit(solution)/shard_map/all_to_all | solution.py:305
  18.2 5.7 %all-to-all-start.1 = ((bf16[32,1,32,1024]{3,2,1,0:T(8,128)(2,1)}), bf16[32,1,32,1024]{3,2,1,0:T(8,128)(2,1)S(1)}, u32[]{:S(2)}, u32[]{:S(2)}) async-start(bf16[32,1,32,1024]{3,2,1,0:T(8,128)(2,1)} %pack_rows.5), calls=%async_computation.1 | async-start | bytes 4194304 | tf_op jit(solution)/shard_map/all_to_all | solution.py:305
  27.3 4.1 %collective-permute-start.2 = (s32[3,1024]{1,0:T(4,128)S(1)}, s32[3,1024]{1,0:T(4,128)S(1)}, u32[]{:S(2)}, u32[]{:S(2)}) collective-permute-start(s32[3,1024]{1,0:T(4,128)S(1)} %convert_reduce_fusion), channel_id=1, source_target_pairs={{0,96},{32,64},{64,32},{96,0},{1,97},{33,65},{65,33},{97,1},{2,98}... | collective-permute-start | bytes 36872 | tf_op jit(solution)/shard_map/ppermute | solution.py:19
  40.8 11.0 %all-to-all-done.1.row_ref = bf16[32,1,32,1024]{3,2,1,0:T(8,128)(2,1)S(1)} async-done(((bf16[32,1,32,1024]{3,2,1,0:T(8,128)(2,1)}), bf16[32,1,32,1024]{3,2,1,0:T(8,128)(2,1)S(1)}, u32[]{:S(2)}, u32[]{:S(2)}) %all-to-all-start.1) | async-done | bytes 2097184 | tf_op jit(solution)/shard_map/all_to_all | solution.py:305
  51.8 6.7 %all-to-all-start.2 = ((bf16[32,1,32,1024]{3,2,1,0:T(8,128)(2,1)}), bf16[32,1,32,1024]{3,2,1,0:T(8,128)(2,1)}, u32[]{:S(2)}, u32[]{:S(2)}) async-start(bf16[32,1,32,1024]{3,2,1,0:T(8,128)(2,1)} %pack_rows.3), calls=%async_computation.2 | async-start | bytes 4194304 | tf_op jit(solution)/shard_map/all_to_all | solution.py:305
  59.3 4.9 %list_sums.3 = (bf16[128,1024]{1,0:T(8,128)(2,1)}, bf16[128,1024]{1,0:T(8,128)(2,1)}, bf16[256,1024]{1,0:T(8,128)(2,1)}, bf16[128,1024]{1,0:T(8,128)(2,1)}, bf16...) custom-call(s32[3,1,1024]{2,1,0:T(1,128)} %compare_select_fusion.1.slot_ref, bf16[32,1,32,1024]{3,2,1,0:T(8,128)(2,1)} %copy-done), custom_call_target="tpu_custom_call" | custom-call | flops 1 | bytes 1 | tf_op jit(solution)/shard_map/list_sums/pallas_call | solution.py:70
  69.2 10.4 %residual_rows.3 = bf16[32,2,32,1024]{3,2,1,0:T(8,128)(2,1)} custom-call(s32[2]{0:T(128)} %pad_add_fusion.place_ref, s32[1024,3]{1,0:T(8,128)} %bitcast.32, bf16[32,1,32,1024]{3,2,1,0:T(8,128)(2,1)} %copy-done, f32[1024,1024]{1,0:T(8,128)} %table_ref.9, f32[1024,4]{1,0:T(8,128)} %bitcast.26, ...), custom_call_target="tpu_custom_call", output_to_operand_aliasing={{}: (5, {})} | custom-call | flops 1 | bytes 1 | tf_op jit(solution)/shard_map/residual_rows/pallas_call | solution.py:172
  84.6 4.0 %collective-permute-done.6 = bf16[128,1024]{1,0:T(8,128)(2,1)S(1)} collective-permute-done((bf16[128,1024]{1,0:T(8,128)(2,1)S(1)}, bf16[128,1024]{1,0:T(8,128)(2,1)S(1)}, u32[]{:S(2)}, u32[]{:S(2)}) %collective-permute-start.6) | collective-permute-done | bytes 262176 | tf_op jit(solution)/shard_map/ppermute | solution.py:19
  91.0 7.6 %all-to-all-start.3 = ((bf16[32,2,32,1024]{3,2,1,0:T(8,128)(2,1)}), bf16[32,2,32,1024]{3,2,1,0:T(8,128)(2,1)}, u32[]{:S(2)}, u32[]{:S(2)}) async-start(bf16[32,2,32,1024]{3,2,1,0:T(8,128)(2,1)} %residual_rows.3), calls=%async_computation.3 | async-start | bytes 8388608 | tf_op jit(solution)/shard_map/all_to_all | solution.py:305
  100.7 7.5 %collective-permute-done.7 = bf16[128,1024]{1,0:T(8,128)(2,1)S(1)} collective-permute-done((bf16[128,1024]{1,0:T(8,128)(2,1)S(1)}, bf16[128,1024]{1,0:T(8,128)(2,1)S(1)}, u32[]{:S(2)}, u32[]{:S(2)}) %collective-permute-start.7) | collective-permute-done | bytes 262176 | tf_op jit(solution)/shard_map/ppermute | solution.py:19
  110.5 4.9 %list_sums.4 = (bf16[128,1024]{1,0:T(8,128)(2,1)}, bf16[128,1024]{1,0:T(8,128)(2,1)}, bf16[256,1024]{1,0:T(8,128)(2,1)}, bf16[128,1024]{1,0:T(8,128)(2,1)}, bf16...) custom-call(s32[3,1,1024]{2,1,0:T(1,128)} %compare_select_fusion.1.slot_ref, ...), custom_call_target="tpu_custom_call" | custom-call | flops 1 | bytes 1 | tf_op jit(solution)/shard_map/list_sums/pallas_call | solution.py:70
  115.4 6.4 %collective-permute-done.9.rest_1_.rest_0_ = bf16[256,1024]{1,0:T(8,128)(2,1)S(1)} collective-permute-done((bf16[256,1024]{1,0:T(8,128)(2,1)S(1)}, bf16[256,1024]{1,0:T(8,128)(2,1)S(1)}, u32[]{:S(2)}, u32[]{:S(2)}) %collective-permute-start.9) | collective-permute-done | bytes 524320 | tf_op jit(solution)/shard_map/ppermute | solution.py:19
  125.5 12.0 %residual_rows.4 = bf16[32,1,32,1024]{3,2,1,0:T(8,128)(2,1)} custom-call(s32[2]{0:T(128)} %pad_add_fusion.place_ref, s32[1024,3]{1,0:T(8,128)} %bitcast.33, bf16[32,1,32,1024]{3,2,1,0:T(8,128)(2,1)} %all-to-all-done.2.row_ref, f32[1024,1024]{1,0:T(8,128)} %table_ref.9, f32[1024,4]{1,0:T(8,128)} %bitcast.27, bf16[256,1024]{1,0:T(8,128)(2,1)} %copy-done.2, ...), custom_call_target="tpu_custom_call" | custom-call | flops 1 | bytes 1 | tf_op jit(solution)/shard_map/residual_rows/pallas_call | solution.py:172
  156.0 7.4 %all-to-all-start.4 = ((bf16[32,1,32,1024]{3,2,1,0:T(8,128)(2,1)}), bf16[32,1,32,1024]{3,2,1,0:T(8,128)(2,1)S(1)}, u32[]{:S(2)}, u32[]{:S(2)}) async-start(bf16[32,1,32,1024]{3,2,1,0:T(8,128)(2,1)} %residual_rows.4), calls=%async_computation.4 | async-start | bytes 4194304 | tf_op jit(solution)/shard_map/all_to_all | solution.py:305
  165.2 4.8 %list_sums.5 = (bf16[128,1024]{1,0:T(8,128)(2,1)}, bf16[128,1024]{1,0:T(8,128)(2,1)}, bf16[256,1024]{1,0:T(8,128)(2,1)}, bf16[128,1024]{1,0:T(8,128)(2,1)}, bf16...) custom-call(s32[3,1,1024]{2,1,0:T(1,128)} %compare_select_fusion.1.slot_ref, ...), custom_call_target="tpu_custom_call" | custom-call | flops 1 | bytes 1 | tf_op jit(solution)/shard_map/list_sums/pallas_call | solution.py:70
  173.1 5.3 %collective-permute-done.17.rest_5_.rest_2_ = bf16[256,1024]{1,0:T(8,128)(2,1)} collective-permute-done((bf16[256,1024]{1,0:T(8,128)(2,1)S(1)}, bf16[256,1024]{1,0:T(8,128)(2,1)}, u32[]{:S(2)}, u32[]{:S(2)}) %collective-permute-start.17) | collective-permute-done | bytes 524320 | tf_op jit(solution)/shard_map/ppermute | solution.py:19
  179.7 12.6 %residual_rows.5 = bf16[32,1,32,1024]{3,2,1,0:T(8,128)(2,1)} custom-call(s32[2]{0:T(128)} %pad_add_fusion.place_ref, s32[1024,3]{1,0:T(8,128)} %bitcast.34, bf16[32,2,32,1024]{3,2,1,0:T(8,128)(2,1)} %all-to-all-done.3.row_ref, f32[1024,1024]{1,0:T(8,128)} %table_ref.9, f32[1024,4]{1,0:T(8,128)} %bitcast.28, bf16[256,1024]{1,0:T(8,128)(2,1)} %copy-done.2, ...), custom_call_target="tpu_custom_call" | custom-call | flops 1 | bytes 1 | tf_op jit(solution)/shard_map/residual_rows/pallas_call | solution.py:172
  192.4 7.7 %all-to-all-start.5 = ((bf16[32,1,32,1024]{3,2,1,0:T(8,128)(2,1)}), bf16[32,1,32,1024]{3,2,1,0:T(8,128)(2,1)}, u32[]{:S(2)}, u32[]{:S(2)}) async-start(bf16[32,1,32,1024]{3,2,1,0:T(8,128)(2,1)} %residual_rows.5), calls=%async_computation.5 | async-start | bytes 4194304 | tf_op jit(solution)/shard_map/all_to_all | solution.py:305
  204.1 6.7 %collective-permute-done.21 = bf16[128,1024]{1,0:T(8,128)(2,1)S(1)} collective-permute-done((bf16[128,1024]{1,0:T(8,128)(2,1)S(1)}, bf16[128,1024]{1,0:T(8,128)(2,1)S(1)}, u32[]{:S(2)}, u32[]{:S(2)}) %collective-permute-start.21) | collective-permute-done | bytes 262176 | tf_op jit(solution)/shard_map/ppermute | solution.py:19
  214.7 6.1 %collective-permute-done.22 = bf16[128,1024]{1,0:T(8,128)(2,1)S(1)} collective-permute-done((bf16[128,1024]{1,0:T(8,128)(2,1)S(1)}, bf16[128,1024]{1,0:T(8,128)(2,1)S(1)}, u32[]{:S(2)}, u32[]{:S(2)}) %collective-permute-start.22) | collective-permute-done | bytes 262176 | tf_op jit(solution)/shard_map/ppermute | solution.py:19
  223.8 3.9 %unpack_rows.3.rest_0_ = bf16[3,512,1024]{2,1,0:T(8,128)(2,1)} custom-call(s32[512,3]{1,0:T(8,128)} %bitcast.35, bf16[32,2,32,1024]{3,2,1,0:T(8,128)(2,1)} %all-to-all-done.3.row_ref), custom_call_target="tpu_custom_call" | custom-call | flops 1 | bytes 1 | tf_op jit(solution)/shard_map/unpack_rows/pallas_call | solution.py:266
  231.7 4.8 %new_rows.2.rest_6_ = f32[1024,1024]{1,0:T(8,128)} custom-call(s32[2]{0:T(128)} %pad_add_fusion.place_ref, f32[1024,1024]{1,0:T(8,128)} %table_ref.9, f32[1024,4]{1,0:T(8,128)} %bitcast.29, bf16[256,1024]{1,0:T(8,128)(2,1)} %copy-done.2, bf16[256,1024]{1,0:T(8,128)(2,1)} %copy-done.3, bf16[256,1024]{1,0:T(8,128)(2,1)} %copy-done.9, ...), custom_call_target="tpu_custom_call" | custom-call | flops 1 | bytes 1 | tf_op jit(solution)/shard_map/new_rows/pallas_call | solution.py:231
  238.2 4.8 %new_rows.3 = f32[1024,1024]{1,0:T(8,128)} custom-call(s32[2]{0:T(128)} %pad_add_fusion.place_ref, f32[1024,1024]{1,0:T(8,128)} %table_ref.9, f32[1024,4]{1,0:T(8,128)} %bitcast.30, bf16[256,1024]{1,0:T(8,128)(2,1)} %copy-done.6, bf16[256,1024]{1,0:T(8,128)(2,1)} %copy-done.7, ...), custom_call_target="tpu_custom_call", output_to_operand_aliasing={{}: (9, {})} | custom-call | flops 1 | bytes 1 | tf_op jit(solution)/shard_map/new_rows/pallas_call | solution.py:231
  243.0 3.9 %unpack_rows.5 = bf16[3,512,1024]{2,1,0:T(8,128)(2,1)} custom-call(s32[512,3]{1,0:T(8,128)} %bitcast.37, bf16[32,1,32,1024]{3,2,1,0:T(8,128)(2,1)} %all-to-all-done.5.row_ref, bf16[3,512,1024]{2,1,0:T(8,128)(2,1)} %unpack_rows.4.rest_0_), custom_call_target="tpu_custom_call", output_to_operand_aliasing={{}: (2, {})} | custom-call | flops 1 | bytes 1 | tf_op jit(solution)/shard_map/unpack_rows/pallas_call | solution.py:266
  (151 shorter events, 84.8 us)
Async XLA Ops:
  4.5 13.7 %all-to-all-start = ((s32[32,1,96]{2,1,0:T(1,128)}), s32[32,1,96]{2,1,0:T(1,128)S(1)}, u32[]{:S(2)}, u32[]{:S(2)}) async-start(s32[32,1,96]{2,1,0:T(1,128)} %bitcast.8), calls=%async_computation | async-start | bytes 32768 | tf_op jit(solution)/shard_map/all_to_all | solution.py:305
  18.2 33.6 %all-to-all-start.1 = ((bf16[32,1,32,1024]{3,2,1,0:T(8,128)(2,1)}), bf16[32,1,32,1024]{3,2,1,0:T(8,128)(2,1)S(1)}, u32[]{:S(2)}, u32[]{:S(2)}) async-start(bf16[32,1,32,1024]{3,2,1,0:T(8,128)(2,1)} %pack_rows.5), calls=%async_computation.1 | async-start | bytes 4194304 | tf_op jit(solution)/shard_map/all_to_all | solution.py:305
  27.3 12.4 %collective-permute-start.2 = (s32[3,1024]{1,0:T(4,128)S(1)}, s32[3,1024]{1,0:T(4,128)S(1)}, u32[]{:S(2)}, u32[]{:S(2)}) collective-permute-start(s32[3,1024]{1,0:T(4,128)S(1)} %convert_reduce_fusion), channel_id=1, source_target_pairs={{0,96},{32,64},{64,32},{96,0},{1,97},{33,65},{65,33},{97,1},{2,98}... | collective-permute-start | bytes 36872 | tf_op jit(solution)/shard_map/ppermute | solution.py:19
  51.8 39.2 %all-to-all-start.2 = ((bf16[32,1,32,1024]{3,2,1,0:T(8,128)(2,1)}), bf16[32,1,32,1024]{3,2,1,0:T(8,128)(2,1)}, u32[]{:S(2)}, u32[]{:S(2)}) async-start(bf16[32,1,32,1024]{3,2,1,0:T(8,128)(2,1)} %pack_rows.3), calls=%async_computation.2 | async-start | bytes 4194304 | tf_op jit(solution)/shard_map/all_to_all | solution.py:305
  64.2 15.4 %collective-permute-start.3 = (bf16[256,1024]{1,0:T(8,128)(2,1)}, bf16[256,1024]{1,0:T(8,128)(2,1)S(1)}, u32[]{:S(2)}, u32[]{:S(2)}) collective-permute-start(bf16[256,1024]{1,0:T(8,128)(2,1)} %get-tuple-element.64), channel_id=1, source_target_pairs={{0,32},{32,0},{64,96},{96,64},{1,33},{33,1},{65,97},{97,65},{2,34}... | collective-permute-start | bytes 1572872 | tf_op jit(solution)/shard_map/ppermute | solution.py:19
  66.1 15.1 %collective-permute-start.4 = (bf16[256,1024]{1,0:T(8,128)(2,1)}, bf16[256,1024]{1,0:T(8,128)(2,1)S(1)}, u32[]{:S(2)}, u32[]{:S(2)}) collective-permute-start(bf16[256,1024]{1,0:T(8,128)(2,1)} %get-tuple-element.65), channel_id=1, source_target_pairs={{0,96},{32,64},{64,32},{96,0},{1,97},{33,65},{65,33},{97,1},{2,98}... | collective-permute-start | bytes 1572872 | tf_op jit(solution)/shard_map/ppermute | solution.py:19
  82.0 8.8 %collective-permute-start.5 = (bf16[128,1024]{1,0:T(8,128)(2,1)S(1)}, bf16[128,1024]{1,0:T(8,128)(2,1)S(1)}, u32[]{:S(2)}, u32[]{:S(2)}) collective-permute-start(bf16[128,1024]{1,0:T(8,128)(2,1)S(1)} %add_convert_fusion.11), channel_id=1, source_target_pairs={{0,96},{32,64},{64,32},{96,0},{1,97},{33,65},{65,33},{97,1},{2,98}... | collective-permute-start | bytes 786440 | tf_op jit(solution)/shard_map/ppermute | solution.py:19
  91.0 65.0 %all-to-all-start.3 = ((bf16[32,2,32,1024]{3,2,1,0:T(8,128)(2,1)}), bf16[32,2,32,1024]{3,2,1,0:T(8,128)(2,1)}, u32[]{:S(2)}, u32[]{:S(2)}) async-start(bf16[32,2,32,1024]{3,2,1,0:T(8,128)(2,1)} %residual_rows.3), calls=%async_computation.3 | async-start | bytes 8388608 | tf_op jit(solution)/shard_map/all_to_all | solution.py:305
  98.6 9.7 %collective-permute-start.7 = (bf16[128,1024]{1,0:T(8,128)(2,1)S(1)}, bf16[128,1024]{1,0:T(8,128)(2,1)S(1)}, u32[]{:S(2)}, u32[]{:S(2)}) collective-permute-start(bf16[128,1024]{1,0:T(8,128)(2,1)S(1)} %add_convert_fusion.10), channel_id=1, source_target_pairs={{0,96},{32,64},{64,32},{96,0},{1,97},{33,65},{65,33},{97,1},{2,98}... | collective-permute-start | bytes 786440 | tf_op jit(solution)/shard_map/ppermute | solution.py:19
  108.8 13.0 %collective-permute-start.9 = (bf16[256,1024]{1,0:T(8,128)(2,1)S(1)}, bf16[256,1024]{1,0:T(8,128)(2,1)S(1)}, u32[]{:S(2)}, u32[]{:S(2)}) collective-permute-start(bf16[256,1024]{1,0:T(8,128)(2,1)S(1)} %pad_maximum_fusion.rest_0_), channel_id=1, source_target_pairs={{0,32},{32,0},{64,96},{96,64},{1,33},{33,1},{65,97},{97,65},{2,34}... | collective-permute-start | bytes 1572872 | tf_op jit(solution)/shard_map/ppermute | solution.py:19
  109.2 14.2 %collective-permute-start.10 = (bf16[256,1024]{1,0:T(8,128)(2,1)S(1)}, bf16[256,1024]{1,0:T(8,128)(2,1)S(1)}, u32[]{:S(2)}, u32[]{:S(2)}) collective-permute-start(bf16[256,1024]{1,0:T(8,128)(2,1)S(1)} %pad_maximum_fusion.1.rest_2_.rest_1_), channel_id=1, source_target_pairs={{0,96},{32,64},{64,32},{96,0},{1,97},{33,65},{65,33},{97,1},{2,98}... | collective-permute-start | bytes 1572872 | tf_op jit(solution)/shard_map/ppermute | solution.py:19
  123.4 14.1 %collective-permute-start.11 = (bf16[256,1024]{1,0:T(8,128)(2,1)}, bf16[256,1024]{1,0:T(8,128)(2,1)S(1)}, u32[]{:S(2)}, u32[]{:S(2)}) collective-permute-start(bf16[256,1024]{1,0:T(8,128)(2,1)} %get-tuple-element.90), channel_id=1, source_target_pairs={{0,32},{32,0},{64,96},{96,64},{1,33},{33,1},{65,97},{97,65},{2,34}... | collective-permute-start | bytes 1572872 | tf_op jit(solution)/shard_map/ppermute | solution.py:19
  123.6 13.9 %collective-permute-start.12 = (bf16[256,1024]{1,0:T(8,128)(2,1)}, bf16[256,1024]{1,0:T(8,128)(2,1)S(1)}, u32[]{:S(2)}, u32[]{:S(2)}) collective-permute-start(bf16[256,1024]{1,0:T(8,128)(2,1)} %get-tuple-element.91), channel_id=1, source_target_pairs={{0,96},{32,64},{64,32},{96,0},{1,97},{33,65},{65,33},{97,1},{2,98}... | collective-permute-start | bytes 1572872 | tf_op jit(solution)/shard_map/ppermute | solution.py:19
  156.0 36.3 %all-to-all-start.4 = ((bf16[32,1,32,1024]{3,2,1,0:T(8,128)(2,1)}), bf16[32,1,32,1024]{3,2,1,0:T(8,128)(2,1)S(1)}, u32[]{:S(2)}, u32[]{:S(2)}) async-start(bf16[32,1,32,1024]{3,2,1,0:T(8,128)(2,1)} %residual_rows.4), calls=%async_computation.4 | async-start | bytes 4194304 | tf_op jit(solution)/shard_map/all_to_all | solution.py:305
  163.4 15.0 %collective-permute-start.17 = (bf16[256,1024]{1,0:T(8,128)(2,1)S(1)}, bf16[256,1024]{1,0:T(8,128)(2,1)}, u32[]{:S(2)}, u32[]{:S(2)}) collective-permute-start(bf16[256,1024]{1,0:T(8,128)(2,1)S(1)} %pad_maximum_fusion.2.rest_4_.rest_2_), channel_id=1, source_target_pairs={{0,32},{32,0},{64,96},{96,64},{1,33},{33,1},{65,97},{97,65},{2,34}... | collective-permute-start | bytes 1572872 | tf_op jit(solution)/shard_map/ppermute | solution.py:19
  163.5 16.2 %collective-permute-start.18 = (bf16[256,1024]{1,0:T(8,128)(2,1)S(1)}, bf16[256,1024]{1,0:T(8,128)(2,1)}, u32[]{:S(2)}, u32[]{:S(2)}) collective-permute-start(bf16[256,1024]{1,0:T(8,128)(2,1)S(1)} %pad_maximum_fusion.3.rest_6_.rest_3_), channel_id=1, source_target_pairs={{0,96},{32,64},{64,32},{96,0},{1,97},{33,65},{65,33},{97,1},{2,98}... | collective-permute-start | bytes 1572872 | tf_op jit(solution)/shard_map/ppermute | solution.py:19
  170.0 22.3 %collective-permute-start.19 = (bf16[256,1024]{1,0:T(8,128)(2,1)}, bf16[256,1024]{1,0:T(8,128)(2,1)}, u32[]{:S(2)}, u32[]{:S(2)}) collective-permute-start(bf16[256,1024]{1,0:T(8,128)(2,1)} %get-tuple-element.103), channel_id=1, source_target_pairs={{0,32},{32,0},{64,96},{96,64},{1,33},{33,1},{65,97},{97,65},{2,34}... | collective-permute-start | bytes 1572872 | tf_op jit(solution)/shard_map/ppermute | solution.py:19
  171.4 20.9 %collective-permute-start.20 = (bf16[256,1024]{1,0:T(8,128)(2,1)}, bf16[256,1024]{1,0:T(8,128)(2,1)}, u32[]{:S(2)}, u32[]{:S(2)}) collective-permute-start(bf16[256,1024]{1,0:T(8,128)(2,1)} %get-tuple-element.104), channel_id=1, source_target_pairs={{0,96},{32,64},{64,32},{96,0},{1,97},{33,65},{65,33},{97,1},{2,98}... | collective-permute-start | bytes 1572872 | tf_op jit(solution)/shard_map/ppermute | solution.py:19
  192.4 50.6 %all-to-all-start.5 = ((bf16[32,1,32,1024]{3,2,1,0:T(8,128)(2,1)}), bf16[32,1,32,1024]{3,2,1,0:T(8,128)(2,1)}, u32[]{:S(2)}, u32[]{:S(2)}) async-start(bf16[32,1,32,1024]{3,2,1,0:T(8,128)(2,1)} %residual_rows.5), calls=%async_computation.5 | async-start | bytes 4194304 | tf_op jit(solution)/shard_map/all_to_all | solution.py:305
  201.2 9.7 %collective-permute-start.21 = (bf16[128,1024]{1,0:T(8,128)(2,1)S(1)}, bf16[128,1024]{1,0:T(8,128)(2,1)S(1)}, u32[]{:S(2)}, u32[]{:S(2)}) collective-permute-start(bf16[128,1024]{1,0:T(8,128)(2,1)S(1)} %add_convert_fusion.3), channel_id=1, source_target_pairs={{0,96},{32,64},{64,32},{96,0},{1,97},{33,65},{65,33},{97,1},{2,98}... | collective-permute-start | bytes 786440 | tf_op jit(solution)/shard_map/ppermute | solution.py:19
  203.9 9.7 %collective-permute-start.24 = (bf16[128,1024]{1,0:T(8,128)(2,1)S(1)}, bf16[128,1024]{1,0:T(8,128)(2,1)S(1)}, u32[]{:S(2)}, u32[]{:S(2)}) collective-permute-start(bf16[128,1024]{1,0:T(8,128)(2,1)S(1)} %add_convert_fusion.1), channel_id=1, source_target_pairs={{0,32},{32,0},{64,96},{96,64},{1,33},{33,1},{65,97},{97,65},{2,34}... | collective-permute-start | bytes 786440 | tf_op jit(solution)/shard_map/ppermute | solution.py:19
  211.9 8.9 %collective-permute-start.22 = (bf16[128,1024]{1,0:T(8,128)(2,1)S(1)}, bf16[128,1024]{1,0:T(8,128)(2,1)S(1)}, u32[]{:S(2)}, u32[]{:S(2)}) collective-permute-start(bf16[128,1024]{1,0:T(8,128)(2,1)S(1)} %add_convert_fusion.2), channel_id=1, source_target_pairs={{0,96},{32,64},{64,32},{96,0},{1,97},{33,65},{65,33},{97,1},{2,98}... | collective-permute-start | bytes 786440 | tf_op jit(solution)/shard_map/ppermute | solution.py:19
  220.9 15.7 %collective-permute-start.23 = (bf16[256,1024]{1,0:T(8,128)(2,1)S(1)}, bf16[256,1024]{1,0:T(8,128)(2,1)S(1)}, u32[]{:S(2)}, u32[]{:S(2)}) collective-permute-start(bf16[256,1024]{1,0:T(8,128)(2,1)S(1)} %pad_maximum_fusion.4.rest_4_), channel_id=1, source_target_pairs={{0,32},{32,0},{64,96},{96,64},{1,33},{33,1},{65,97},{97,65},{2,34}... | collective-permute-start | bytes 1572872 | tf_op jit(solution)/shard_map/ppermute | solution.py:19
  222.1 14.5 %collective-permute-start.26 = (bf16[256,1024]{1,0:T(8,128)(2,1)S(1)}, bf16[256,1024]{1,0:T(8,128)(2,1)S(1)}, u32[]{:S(2)}, u32[]{:S(2)}) collective-permute-start(bf16[256,1024]{1,0:T(8,128)(2,1)S(1)} %pad_maximum_fusion.5.rest_5_), channel_id=1, source_target_pairs={{0,96},{32,64},{64,32},{96,0},{1,97},{33,65},{65,33},{97,1},{2,98}... | collective-permute-start | bytes 1572872 | tf_op jit(solution)/shard_map/ppermute | solution.py:19
  (33 other events, 366.2 us)

commit v4 on v3

--- a/solution.py
+++ b/solution.py
@@ -391,15 +391,17 @@
     sums = sums_of(mixed, 2)
     got = send_far(sums)
     buffer = residual(mixed, 2, parts)
-    buffer, got, back1 = gate(buffer, got, back1)
+    output = unpack_rows(mixed, 1, dest_cols, 0, None, row_count)
+    buffer, got, output, back1 = gate(buffer, got, output, back1)
     back2 = exchange(buffer)
 
-    parts = parts + [spread_far(spread_near(send_near(sums, got)))]
-    current = new_rows(centroids, weights, parts, places, 0, None)
-    current = new_rows(centroids, weights, parts, places, 1, current)
-    output = unpack_rows(mixed, 1, dest_cols, 0, None, row_count)
+    whole = spread_far(spread_near(send_near(sums, got)))
+    current = new_rows(centroids, weights, parts + [whole], places, 0, None)
     output = unpack_rows(back1, 0, dest_cols, 1, output, row_count)
+    output, current = gate(output, current)
     output = unpack_rows(back2, 0, dest_cols, 2, output, row_count)
+    output, whole[1], whole[3] = gate(output, whole[1], whole[3])
+    current = new_rows(centroids, weights, parts + [whole], places, 1, current)
     return (output, current)
 
 

time: 248 us -> 244 us (0.984)
  waiting for transfers between devices: 66.7 us -> 62.8 us
    ppermute x27, waiting for transfers between devices: 54 us -> 50.1 us  [swap(): return lax.ppermute(rows, axis, [(i, i ^ offset) for i in range(count)])]
where the time goes in v4:
time: 244 us; the launch traced here: 243 us
  Pallas kernels  82 us (34%)
  starting transfers between devices  77.2 us (32%)
  waiting for transfers between devices  62.8 us (26%)
  other arithmetic  13.1 us (5%)
  local copies, waits for them, and re-layouts  6.58 us (3%)
    ppermute x27, waiting for transfers between devices, swap(): return lax.ppermute(rows, axis, [(i, i ^ offset) for i in range(count)])  50.1 us
    all_to_all x6, starting transfers between devices, exchange(): return lax.all_to_all(rows, 'list', split_axis=0, concat_axis=0, tiled=True)  42.7 us
    pallas_call x3, Pallas kernels, residual_rows(): pl.pallas_call(body, grid_spec=pltpu.PrefetchScalarGridSpec(num_scalar_pr...  35 us
    ppermute x27, starting transfers between devices, swap(): return lax.ppermute(rows, axis, [(i, i ^ offset) for i in range(count)])  34.5 us
    pallas_call x3, Pallas kernels, list_sums(): pl.pallas_call(body, grid=(1,), in_specs=[pl.BlockSpec((1, 1, rows), lamb...  14.5 us
    all_to_all x6, waiting for transfers between devices, exchange(): return lax.all_to_all(rows, 'list', split_axis=0, concat_axis=0, tiled=True)  12.7 us
    pallas_call x3, Pallas kernels, unpack_rows(): pl.pallas_call(body, grid=(1,), in_specs=in_specs, out_specs=pl.BlockSpec...  11.8 us
    pallas_call x3, Pallas kernels, pack_rows(): pl.pallas_call(body, grid=(owners // group,), in_specs=[pl.BlockSpec((1,...  10.9 us
  transfers between devices with their start and end apart: 33, of which 18 were waited for; matrix products, arithmetic and copies ran while one was open for 6% of the time, Pallas kernels for 32%

profile of v4, /device:TPU:2, one launch (start us, length us, event | category | flops | bytes accessed | tf_op | source)
XLA Modules:
  0.0 243.1 jit_solution(16569009264301180787)
XLA Ops:
  4.5 7.6 %all-to-all-start = ((s32[32,1,96]{2,1,0:T(1,128)}), s32[32,1,96]{2,1,0:T(1,128)S(1)}, u32[]{:S(2)}, u32[]{:S(2)}) async-start(s32[32,1,96]{2,1,0:T(1,128)} %bitcast.8), calls=%async_computation | async-start | bytes 32768 | tf_op jit(solution)/shard_map/all_to_all | solution.py:305
  18.2 5.7 %all-to-all-start.1 = ((bf16[32,1,32,1024]{3,2,1,0:T(8,128)(2,1)}), bf16[32,1,32,1024]{3,2,1,0:T(8,128)(2,1)S(1)}, u32[]{:S(2)}, u32[]{:S(2)}) async-start(bf16[32,1,32,1024]{3,2,1,0:T(8,128)(2,1)} %pack_rows.5), calls=%async_computation.1 | async-start | bytes 4194304 | tf_op jit(solution)/shard_map/all_to_all | solution.py:305
  27.3 4.1 %collective-permute-start.2 = (s32[3,1024]{1,0:T(4,128)S(1)}, s32[3,1024]{1,0:T(4,128)S(1)}, u32[]{:S(2)}, u32[]{:S(2)}) collective-permute-start(s32[3,1024]{1,0:T(4,128)S(1)} %convert_reduce_fusion), channel_id=1, source_target_pairs={{0,96},{32,64},{64,32},{96,0},{1,97},{33,65},{65,33},{97,1},{2,98}... | collective-permute-start | bytes 36872 | tf_op jit(solution)/shard_map/ppermute | solution.py:19
  40.8 11.0 %all-to-all-done.1.row_ref = bf16[32,1,32,1024]{3,2,1,0:T(8,128)(2,1)S(1)} async-done(((bf16[32,1,32,1024]{3,2,1,0:T(8,128)(2,1)}), bf16[32,1,32,1024]{3,2,1,0:T(8,128)(2,1)S(1)}, u32[]{:S(2)}, u32[]{:S(2)}) %all-to-all-start.1) | async-done | bytes 2097184 | tf_op jit(solution)/shard_map/all_to_all | solution.py:305
  51.8 6.7 %all-to-all-start.2 = ((bf16[32,1,32,1024]{3,2,1,0:T(8,128)(2,1)}), bf16[32,1,32,1024]{3,2,1,0:T(8,128)(2,1)}, u32[]{:S(2)}, u32[]{:S(2)}) async-start(bf16[32,1,32,1024]{3,2,1,0:T(8,128)(2,1)} %pack_rows.3), calls=%async_computation.2 | async-start | bytes 4194304 | tf_op jit(solution)/shard_map/all_to_all | solution.py:305
  59.3 4.8 %list_sums.3 = (bf16[128,1024]{1,0:T(8,128)(2,1)}, bf16[128,1024]{1,0:T(8,128)(2,1)}, bf16[256,1024]{1,0:T(8,128)(2,1)}, bf16[128,1024]{1,0:T(8,128)(2,1)}, bf16...) custom-call(s32[3,1,1024]{2,1,0:T(1,128)} %compare_select_fusion.1.slot_ref, bf16[32,1,32,1024]{3,2,1,0:T(8,128)(2,1)} %copy-done), custom_call_target="tpu_custom_call" | custom-call | flops 1 | bytes 1 | tf_op jit(solution)/shard_map/list_sums/pallas_call | solution.py:70
  69.2 10.4 %residual_rows.3 = bf16[32,2,32,1024]{3,2,1,0:T(8,128)(2,1)} custom-call(s32[2]{0:T(128)} %pad_add_fusion.place_ref, s32[1024,3]{1,0:T(8,128)} %bitcast.32, bf16[32,1,32,1024]{3,2,1,0:T(8,128)(2,1)} %copy-done, f32[1024,1024]{1,0:T(8,128)} %table_ref.9, f32[1024,4]{1,0:T(8,128)} %bitcast.26, ...), custom_call_target="tpu_custom_call", output_to_operand_aliasing={{}: (5, {})} | custom-call | flops 1 | bytes 1 | tf_op jit(solution)/shard_map/residual_rows/pallas_call | solution.py:172
  84.6 4.0 %collective-permute-done.6 = bf16[128,1024]{1,0:T(8,128)(2,1)S(1)} collective-permute-done((bf16[128,1024]{1,0:T(8,128)(2,1)S(1)}, bf16[128,1024]{1,0:T(8,128)(2,1)S(1)}, u32[]{:S(2)}, u32[]{:S(2)}) %collective-permute-start.6) | collective-permute-done | bytes 262176 | tf_op jit(solution)/shard_map/ppermute | solution.py:19
  91.0 7.6 %all-to-all-start.3 = ((bf16[32,2,32,1024]{3,2,1,0:T(8,128)(2,1)}), bf16[32,2,32,1024]{3,2,1,0:T(8,128)(2,1)}, u32[]{:S(2)}, u32[]{:S(2)}) async-start(bf16[32,2,32,1024]{3,2,1,0:T(8,128)(2,1)} %residual_rows.3), calls=%async_computation.3 | async-start | bytes 8388608 | tf_op jit(solution)/shard_map/all_to_all | solution.py:305
  100.7 7.5 %collective-permute-done.7 = bf16[128,1024]{1,0:T(8,128)(2,1)S(1)} collective-permute-done((bf16[128,1024]{1,0:T(8,128)(2,1)S(1)}, bf16[128,1024]{1,0:T(8,128)(2,1)S(1)}, u32[]{:S(2)}, u32[]{:S(2)}) %collective-permute-start.7) | collective-permute-done | bytes 262176 | tf_op jit(solution)/shard_map/ppermute | solution.py:19
  110.5 4.8 %list_sums.4 = (bf16[128,1024]{1,0:T(8,128)(2,1)}, bf16[128,1024]{1,0:T(8,128)(2,1)}, bf16[256,1024]{1,0:T(8,128)(2,1)}, bf16[128,1024]{1,0:T(8,128)(2,1)}, bf16...) custom-call(s32[3,1,1024]{2,1,0:T(1,128)} %compare_select_fusion.1.slot_ref, ...), custom_call_target="tpu_custom_call" | custom-call | flops 1 | bytes 1 | tf_op jit(solution)/shard_map/list_sums/pallas_call | solution.py:70
  115.3 6.5 %collective-permute-done.9.rest_1_.rest_0_ = bf16[256,1024]{1,0:T(8,128)(2,1)S(1)} collective-permute-done((bf16[256,1024]{1,0:T(8,128)(2,1)S(1)}, bf16[256,1024]{1,0:T(8,128)(2,1)S(1)}, u32[]{:S(2)}, u32[]{:S(2)}) %collective-permute-start.9) | collective-permute-done | bytes 524320 | tf_op jit(solution)/shard_map/ppermute | solution.py:19
  125.4 12.0 %residual_rows.4 = bf16[32,1,32,1024]{3,2,1,0:T(8,128)(2,1)} custom-call(s32[2]{0:T(128)} %pad_add_fusion.place_ref, s32[1024,3]{1,0:T(8,128)} %bitcast.33, bf16[32,1,32,1024]{3,2,1,0:T(8,128)(2,1)} %all-to-all-done.2.row_ref, f32[1024,1024]{1,0:T(8,128)} %table_ref.9, f32[1024,4]{1,0:T(8,128)} %bitcast.27, bf16[256,1024]{1,0:T(8,128)(2,1)} %copy-done.2, ...), custom_call_target="tpu_custom_call" | custom-call | flops 1 | bytes 1 | tf_op jit(solution)/shard_map/residual_rows/pallas_call | solution.py:172
  156.1 7.4 %all-to-all-start.4 = ((bf16[32,1,32,1024]{3,2,1,0:T(8,128)(2,1)}), bf16[32,1,32,1024]{3,2,1,0:T(8,128)(2,1)S(1)}, u32[]{:S(2)}, u32[]{:S(2)}) async-start(bf16[32,1,32,1024]{3,2,1,0:T(8,128)(2,1)} %residual_rows.4), calls=%async_computation.4 | async-start | bytes 4194304 | tf_op jit(solution)/shard_map/all_to_all | solution.py:305
  165.3 4.8 %list_sums.5 = (bf16[128,1024]{1,0:T(8,128)(2,1)}, bf16[128,1024]{1,0:T(8,128)(2,1)}, bf16[256,1024]{1,0:T(8,128)(2,1)}, bf16[128,1024]{1,0:T(8,128)(2,1)}, bf16...) custom-call(s32[3,1,1024]{2,1,0:T(1,128)} %compare_select_fusion.1.slot_ref, ...), custom_call_target="tpu_custom_call" | custom-call | flops 1 | bytes 1 | tf_op jit(solution)/shard_map/list_sums/pallas_call | solution.py:70
  173.1 3.9 %unpack_rows.3.rest_0_ = bf16[3,512,1024]{2,1,0:T(8,128)(2,1)} custom-call(s32[512,3]{1,0:T(8,128)} %bitcast.35, bf16[32,2,32,1024]{3,2,1,0:T(8,128)(2,1)} %all-to-all-done.3.row_ref), custom_call_target="tpu_custom_call" | custom-call | flops 1 | bytes 1 | tf_op jit(solution)/shard_map/unpack_rows/pallas_call | solution.py:266
  179.8 12.6 %residual_rows.5 = bf16[32,1,32,1024]{3,2,1,0:T(8,128)(2,1)} custom-call(s32[2]{0:T(128)} %pad_add_fusion.place_ref, s32[1024,3]{1,0:T(8,128)} %bitcast.34, bf16[32,2,32,1024]{3,2,1,0:T(8,128)(2,1)} %all-to-all-done.3.row_ref, f32[1024,1024]{1,0:T(8,128)} %table_ref.9, f32[1024,4]{1,0:T(8,128)} %bitcast.28, bf16[256,1024]{1,0:T(8,128)(2,1)} %copy-done.2, ...), custom_call_target="tpu_custom_call" | custom-call | flops 1 | bytes 1 | tf_op jit(solution)/shard_map/residual_rows/pallas_call | solution.py:172
  192.4 7.7 %all-to-all-start.5 = ((bf16[32,1,32,1024]{3,2,1,0:T(8,128)(2,1)}), bf16[32,1,32,1024]{3,2,1,0:T(8,128)(2,1)}, u32[]{:S(2)}, u32[]{:S(2)}) async-start(bf16[32,1,32,1024]{3,2,1,0:T(8,128)(2,1)} %residual_rows.5), calls=%async_computation.5 | async-start | bytes 4194304 | tf_op jit(solution)/shard_map/all_to_all | solution.py:305
  204.1 6.7 %collective-permute-done.21 = bf16[128,1024]{1,0:T(8,128)(2,1)S(1)} collective-permute-done((bf16[128,1024]{1,0:T(8,128)(2,1)S(1)}, bf16[128,1024]{1,0:T(8,128)(2,1)S(1)}, u32[]{:S(2)}, u32[]{:S(2)}) %collective-permute-start.21) | collective-permute-done | bytes 262176 | tf_op jit(solution)/shard_map/ppermute | solution.py:19
  214.8 6.1 %collective-permute-done.22 = bf16[128,1024]{1,0:T(8,128)(2,1)S(1)} collective-permute-done((bf16[128,1024]{1,0:T(8,128)(2,1)S(1)}, bf16[128,1024]{1,0:T(8,128)(2,1)S(1)}, u32[]{:S(2)}, u32[]{:S(2)}) %collective-permute-start.22) | collective-permute-done | bytes 262176 | tf_op jit(solution)/shard_map/ppermute | solution.py:19
  223.9 4.0 %unpack_rows.4.rest_0_ = bf16[3,512,1024]{2,1,0:T(8,128)(2,1)} custom-call(s32[512,3]{1,0:T(8,128)} %bitcast.36, bf16[32,1,32,1024]{3,2,1,0:T(8,128)(2,1)} %copy-done.4, bf16[3,512,1024]{2,1,0:T(8,128)(2,1)} %unpack_rows.3.rest_0_), custom_call_target="tpu_custom_call", output_to_operand_aliasing={{}: (2, {})} | custom-call | flops 1 | bytes 1 | tf_op jit(solution)/shard_map/unpack_rows/pallas_call | solution.py:266
  227.9 4.8 %new_rows.2.rest_6_ = f32[1024,1024]{1,0:T(8,128)} custom-call(s32[2]{0:T(128)} %pad_add_fusion.place_ref, f32[1024,1024]{1,0:T(8,128)} %table_ref.9, f32[1024,4]{1,0:T(8,128)} %bitcast.29, bf16[256,1024]{1,0:T(8,128)(2,1)} %copy-done.2, bf16[256,1024]{1,0:T(8,128)(2,1)} %copy-done.3, bf16[256,1024]{1,0:T(8,128)(2,1)} %copy-done.9, ...), custom_call_target="tpu_custom_call" | custom-call | flops 1 | bytes 1 | tf_op jit(solution)/shard_map/new_rows/pallas_call | solution.py:231
  232.7 4.0 %unpack_rows.5 = bf16[3,512,1024]{2,1,0:T(8,128)(2,1)} custom-call(s32[512,3]{1,0:T(8,128)} %bitcast.37, bf16[32,1,32,1024]{3,2,1,0:T(8,128)(2,1)} %all-to-all-done.5.row_ref, bf16[3,512,1024]{2,1,0:T(8,128)(2,1)} %unpack_rows.4.rest_0_), custom_call_target="tpu_custom_call", output_to_operand_aliasing={{}: (2, {})} | custom-call | flops 1 | bytes 1 | tf_op jit(solution)/shard_map/unpack_rows/pallas_call | solution.py:266
  238.2 4.8 %new_rows.3 = f32[1024,1024]{1,0:T(8,128)} custom-call(s32[2]{0:T(128)} %pad_add_fusion.place_ref, f32[1024,1024]{1,0:T(8,128)} %table_ref.9, f32[1024,4]{1,0:T(8,128)} %bitcast.30, bf16[256,1024]{1,0:T(8,128)(2,1)} %copy-done.6, bf16[256,1024]{1,0:T(8,128)(2,1)} %copy-done.7, ...), custom_call_target="tpu_custom_call", output_to_operand_aliasing={{}: (9, {})} | custom-call | flops 1 | bytes 1 | tf_op jit(solution)/shard_map/new_rows/pallas_call | solution.py:231
  (151 shorter events, 82.2 us)
Async XLA Ops:
  4.5 13.7 %all-to-all-start = ((s32[32,1,96]{2,1,0:T(1,128)}), s32[32,1,96]{2,1,0:T(1,128)S(1)}, u32[]{:S(2)}, u32[]{:S(2)}) async-start(s32[32,1,96]{2,1,0:T(1,128)} %bitcast.8), calls=%async_computation | async-start | bytes 32768 | tf_op jit(solution)/shard_map/all_to_all | solution.py:305
  18.2 33.6 %all-to-all-start.1 = ((bf16[32,1,32,1024]{3,2,1,0:T(8,128)(2,1)}), bf16[32,1,32,1024]{3,2,1,0:T(8,128)(2,1)S(1)}, u32[]{:S(2)}, u32[]{:S(2)}) async-start(bf16[32,1,32,1024]{3,2,1,0:T(8,128)(2,1)} %pack_rows.5), calls=%async_computation.1 | async-start | bytes 4194304 | tf_op jit(solution)/shard_map/all_to_all | solution.py:305
  27.3 12.4 %collective-permute-start.2 = (s32[3,1024]{1,0:T(4,128)S(1)}, s32[3,1024]{1,0:T(4,128)S(1)}, u32[]{:S(2)}, u32[]{:S(2)}) collective-permute-start(s32[3,1024]{1,0:T(4,128)S(1)} %convert_reduce_fusion), channel_id=1, source_target_pairs={{0,96},{32,64},{64,32},{96,0},{1,97},{33,65},{65,33},{97,1},{2,98}... | collective-permute-start | bytes 36872 | tf_op jit(solution)/shard_map/ppermute | solution.py:19
  51.8 39.1 %all-to-all-start.2 = ((bf16[32,1,32,1024]{3,2,1,0:T(8,128)(2,1)}), bf16[32,1,32,1024]{3,2,1,0:T(8,128)(2,1)}, u32[]{:S(2)}, u32[]{:S(2)}) async-start(bf16[32,1,32,1024]{3,2,1,0:T(8,128)(2,1)} %pack_rows.3), calls=%async_computation.2 | async-start | bytes 4194304 | tf_op jit(solution)/shard_map/all_to_all | solution.py:305
  64.1 15.4 %collective-permute-start.3 = (bf16[256,1024]{1,0:T(8,128)(2,1)}, bf16[256,1024]{1,0:T(8,128)(2,1)S(1)}, u32[]{:S(2)}, u32[]{:S(2)}) collective-permute-start(bf16[256,1024]{1,0:T(8,128)(2,1)} %get-tuple-element.70), channel_id=1, source_target_pairs={{0,32},{32,0},{64,96},{96,64},{1,33},{33,1},{65,97},{97,65},{2,34}... | collective-permute-start | bytes 1572872 | tf_op jit(solution)/shard_map/ppermute | solution.py:19
  66.1 15.1 %collective-permute-start.4 = (bf16[256,1024]{1,0:T(8,128)(2,1)}, bf16[256,1024]{1,0:T(8,128)(2,1)S(1)}, u32[]{:S(2)}, u32[]{:S(2)}) collective-permute-start(bf16[256,1024]{1,0:T(8,128)(2,1)} %get-tuple-element.71), channel_id=1, source_target_pairs={{0,96},{32,64},{64,32},{96,0},{1,97},{33,65},{65,33},{97,1},{2,98}... | collective-permute-start | bytes 1572872 | tf_op jit(solution)/shard_map/ppermute | solution.py:19
  82.0 8.8 %collective-permute-start.5 = (bf16[128,1024]{1,0:T(8,128)(2,1)S(1)}, bf16[128,1024]{1,0:T(8,128)(2,1)S(1)}, u32[]{:S(2)}, u32[]{:S(2)}) collective-permute-start(bf16[128,1024]{1,0:T(8,128)(2,1)S(1)} %add_convert_fusion.11), channel_id=1, source_target_pairs={{0,96},{32,64},{64,32},{96,0},{1,97},{33,65},{65,33},{97,1},{2,98}... | collective-permute-start | bytes 786440 | tf_op jit(solution)/shard_map/ppermute | solution.py:19
  91.0 65.1 %all-to-all-start.3 = ((bf16[32,2,32,1024]{3,2,1,0:T(8,128)(2,1)}), bf16[32,2,32,1024]{3,2,1,0:T(8,128)(2,1)}, u32[]{:S(2)}, u32[]{:S(2)}) async-start(bf16[32,2,32,1024]{3,2,1,0:T(8,128)(2,1)} %residual_rows.3), calls=%async_computation.3 | async-start | bytes 8388608 | tf_op jit(solution)/shard_map/all_to_all | solution.py:305
  98.5 9.7 %collective-permute-start.7 = (bf16[128,1024]{1,0:T(8,128)(2,1)S(1)}, bf16[128,1024]{1,0:T(8,128)(2,1)S(1)}, u32[]{:S(2)}, u32[]{:S(2)}) collective-permute-start(bf16[128,1024]{1,0:T(8,128)(2,1)S(1)} %add_convert_fusion.10), channel_id=1, source_target_pairs={{0,96},{32,64},{64,32},{96,0},{1,97},{33,65},{65,33},{97,1},{2,98}... | collective-permute-start | bytes 786440 | tf_op jit(solution)/shard_map/ppermute | solution.py:19
  108.8 13.0 %collective-permute-start.9 = (bf16[256,1024]{1,0:T(8,128)(2,1)S(1)}, bf16[256,1024]{1,0:T(8,128)(2,1)S(1)}, u32[]{:S(2)}, u32[]{:S(2)}) collective-permute-start(bf16[256,1024]{1,0:T(8,128)(2,1)S(1)} %pad_maximum_fusion.rest_0_), channel_id=1, source_target_pairs={{0,32},{32,0},{64,96},{96,64},{1,33},{33,1},{65,97},{97,65},{2,34}... | collective-permute-start | bytes 1572872 | tf_op jit(solution)/shard_map/ppermute | solution.py:19
  109.1 14.2 %collective-permute-start.10 = (bf16[256,1024]{1,0:T(8,128)(2,1)S(1)}, bf16[256,1024]{1,0:T(8,128)(2,1)S(1)}, u32[]{:S(2)}, u32[]{:S(2)}) collective-permute-start(bf16[256,1024]{1,0:T(8,128)(2,1)S(1)} %pad_maximum_fusion.1.rest_2_.rest_1_), channel_id=1, source_target_pairs={{0,96},{32,64},{64,32},{96,0},{1,97},{33,65},{65,33},{97,1},{2,98}... | collective-permute-start | bytes 1572872 | tf_op jit(solution)/shard_map/ppermute | solution.py:19
  123.3 14.1 %collective-permute-start.11 = (bf16[256,1024]{1,0:T(8,128)(2,1)}, bf16[256,1024]{1,0:T(8,128)(2,1)S(1)}, u32[]{:S(2)}, u32[]{:S(2)}) collective-permute-start(bf16[256,1024]{1,0:T(8,128)(2,1)} %get-tuple-element.96), channel_id=1, source_target_pairs={{0,32},{32,0},{64,96},{96,64},{1,33},{33,1},{65,97},{97,65},{2,34}... | collective-permute-start | bytes 1572872 | tf_op jit(solution)/shard_map/ppermute | solution.py:19
  123.5 13.9 %collective-permute-start.12 = (bf16[256,1024]{1,0:T(8,128)(2,1)}, bf16[256,1024]{1,0:T(8,128)(2,1)S(1)}, u32[]{:S(2)}, u32[]{:S(2)}) collective-permute-start(bf16[256,1024]{1,0:T(8,128)(2,1)} %get-tuple-element.97), channel_id=1, source_target_pairs={{0,96},{32,64},{64,32},{96,0},{1,97},{33,65},{65,33},{97,1},{2,98}... | collective-permute-start | bytes 1572872 | tf_op jit(solution)/shard_map/ppermute | solution.py:19
  156.1 36.3 %all-to-all-start.4 = ((bf16[32,1,32,1024]{3,2,1,0:T(8,128)(2,1)}), bf16[32,1,32,1024]{3,2,1,0:T(8,128)(2,1)S(1)}, u32[]{:S(2)}, u32[]{:S(2)}) async-start(bf16[32,1,32,1024]{3,2,1,0:T(8,128)(2,1)} %residual_rows.4), calls=%async_computation.4 | async-start | bytes 4194304 | tf_op jit(solution)/shard_map/all_to_all | solution.py:305
  163.5 15.0 %collective-permute-start.17 = (bf16[256,1024]{1,0:T(8,128)(2,1)S(1)}, bf16[256,1024]{1,0:T(8,128)(2,1)}, u32[]{:S(2)}, u32[]{:S(2)}) collective-permute-start(bf16[256,1024]{1,0:T(8,128)(2,1)S(1)} %pad_maximum_fusion.2.rest_4_.rest_2_), channel_id=1, source_target_pairs={{0,32},{32,0},{64,96},{96,64},{1,33},{33,1},{65,97},{97,65},{2,34}... | collective-permute-start | bytes 1572872 | tf_op jit(solution)/shard_map/ppermute | solution.py:19
  163.6 16.2 %collective-permute-start.18 = (bf16[256,1024]{1,0:T(8,128)(2,1)S(1)}, bf16[256,1024]{1,0:T(8,128)(2,1)}, u32[]{:S(2)}, u32[]{:S(2)}) collective-permute-start(bf16[256,1024]{1,0:T(8,128)(2,1)S(1)} %pad_maximum_fusion.3.rest_6_.rest_3_), channel_id=1, source_target_pairs={{0,96},{32,64},{64,32},{96,0},{1,97},{33,65},{65,33},{97,1},{2,98}... | collective-permute-start | bytes 1572872 | tf_op jit(solution)/shard_map/ppermute | solution.py:19
  170.1 22.3 %collective-permute-start.19 = (bf16[256,1024]{1,0:T(8,128)(2,1)}, bf16[256,1024]{1,0:T(8,128)(2,1)}, u32[]{:S(2)}, u32[]{:S(2)}) collective-permute-start(bf16[256,1024]{1,0:T(8,128)(2,1)} %get-tuple-element.109), channel_id=1, source_target_pairs={{0,32},{32,0},{64,96},{96,64},{1,33},{33,1},{65,97},{97,65},{2,34}... | collective-permute-start | bytes 1572872 | tf_op jit(solution)/shard_map/ppermute | solution.py:19
  171.5 20.9 %collective-permute-start.20 = (bf16[256,1024]{1,0:T(8,128)(2,1)}, bf16[256,1024]{1,0:T(8,128)(2,1)}, u32[]{:S(2)}, u32[]{:S(2)}) collective-permute-start(bf16[256,1024]{1,0:T(8,128)(2,1)} %get-tuple-element.110), channel_id=1, source_target_pairs={{0,96},{32,64},{64,32},{96,0},{1,97},{33,65},{65,33},{97,1},{2,98}... | collective-permute-start | bytes 1572872 | tf_op jit(solution)/shard_map/ppermute | solution.py:19
  192.4 40.2 %all-to-all-start.5 = ((bf16[32,1,32,1024]{3,2,1,0:T(8,128)(2,1)}), bf16[32,1,32,1024]{3,2,1,0:T(8,128)(2,1)}, u32[]{:S(2)}, u32[]{:S(2)}) async-start(bf16[32,1,32,1024]{3,2,1,0:T(8,128)(2,1)} %residual_rows.5), calls=%async_computation.5 | async-start | bytes 4194304 | tf_op jit(solution)/shard_map/all_to_all | solution.py:305
  201.2 9.7 %collective-permute-start.21 = (bf16[128,1024]{1,0:T(8,128)(2,1)S(1)}, bf16[128,1024]{1,0:T(8,128)(2,1)S(1)}, u32[]{:S(2)}, u32[]{:S(2)}) collective-permute-start(bf16[128,1024]{1,0:T(8,128)(2,1)S(1)} %add_convert_fusion.3), channel_id=1, source_target_pairs={{0,96},{32,64},{64,32},{96,0},{1,97},{33,65},{65,33},{97,1},{2,98}... | collective-permute-start | bytes 786440 | tf_op jit(solution)/shard_map/ppermute | solution.py:19
  203.9 9.7 %collective-permute-start.23 = (bf16[128,1024]{1,0:T(8,128)(2,1)S(1)}, bf16[128,1024]{1,0:T(8,128)(2,1)S(1)}, u32[]{:S(2)}, u32[]{:S(2)}) collective-permute-start(bf16[128,1024]{1,0:T(8,128)(2,1)S(1)} %add_convert_fusion.1), channel_id=1, source_target_pairs={{0,32},{32,0},{64,96},{96,64},{1,33},{33,1},{65,97},{97,65},{2,34}... | collective-permute-start | bytes 786440 | tf_op jit(solution)/shard_map/ppermute | solution.py:19
  211.9 8.9 %collective-permute-start.22 = (bf16[128,1024]{1,0:T(8,128)(2,1)S(1)}, bf16[128,1024]{1,0:T(8,128)(2,1)S(1)}, u32[]{:S(2)}, u32[]{:S(2)}) collective-permute-start(bf16[128,1024]{1,0:T(8,128)(2,1)S(1)} %add_convert_fusion.2), channel_id=1, source_target_pairs={{0,96},{32,64},{64,32},{96,0},{1,97},{33,65},{65,33},{97,1},{2,98}... | collective-permute-start | bytes 786440 | tf_op jit(solution)/shard_map/ppermute | solution.py:19
  220.9 15.7 %collective-permute-start.25 = (bf16[256,1024]{1,0:T(8,128)(2,1)S(1)}, bf16[256,1024]{1,0:T(8,128)(2,1)S(1)}, u32[]{:S(2)}, u32[]{:S(2)}) collective-permute-start(bf16[256,1024]{1,0:T(8,128)(2,1)S(1)} %pad_maximum_fusion.4.rest_4_), channel_id=1, source_target_pairs={{0,32},{32,0},{64,96},{96,64},{1,33},{33,1},{65,97},{97,65},{2,34}... | collective-permute-start | bytes 1572872 | tf_op jit(solution)/shard_map/ppermute | solution.py:19
  222.2 14.5 %collective-permute-start.26 = (bf16[256,1024]{1,0:T(8,128)(2,1)S(1)}, bf16[256,1024]{1,0:T(8,128)(2,1)S(1)}, u32[]{:S(2)}, u32[]{:S(2)}) collective-permute-start(bf16[256,1024]{1,0:T(8,128)(2,1)S(1)} %pad_maximum_fusion.5.rest_5_), channel_id=1, source_target_pairs={{0,96},{32,64},{64,32},{96,0},{1,97},{33,65},{65,33},{97,1},{2,98}... | collective-permute-start | bytes 1572872 | tf_op jit(solution)/shard_map/ppermute | solution.py:19
  (33 other events, 362.4 us)

commit v5 on v4

--- a/solution.py
+++ b/solution.py
@@ -74,8 +74,8 @@
             pl.BlockSpec((1, 1, rows), lambda i: (step, 0, 0)),
             pl.BlockSpec((owners, 1, capacity, width), lambda i: (0, at, 0, 0)),
         ],
-        out_specs=[pl.BlockSpec((size, width), lambda i: (0, 0)) for size in sizes],
-        out_shape=[jax.ShapeDtypeStruct((size, width), jnp.bfloat16) for size in sizes],
+        out_specs=[pl.BlockSpec(memory_space=pltpu.VMEM) for _ in sizes],
+        out_shape=[pltpu.VMEM((size, width), jnp.bfloat16) for size in sizes],
         name="list_sums",
         cost_estimate=CHEAP,
     )(slots, received)

time: 244 us -> 244 us (level)
  Pallas kernels: 82 us -> 79 us
    pallas_call x3, Pallas kernels: 14.5 us -> 11.8 us  [list_sums(): pl.pallas_call(body, grid=(1,), in_specs=[pl.BlockSpec((1, 1, rows), lamb...]
  transfers between devices with their start and end apart: 33 -> 33, of which waited for: 18 -> 18; matrix products, arithmetic and copies ran while one was open for 6% -> 6% of each run, Pallas kernels for 32% -> 31%
where the time goes in v5:
time: 244 us; the launch traced here: 242 us
  Pallas kernels  79 us (32%)
  starting transfers between devices  77 us (32%)
  waiting for transfers between devices  64.7 us (27%)
  other arithmetic  14 us (6%)
  local copies, waits for them, and re-layouts  6.28 us (3%)
    ppermute x27, waiting for transfers between devices, swap(): return lax.ppermute(rows, axis, [(i, i ^ offset) for i in range(count)])  52 us
    all_to_all x6, starting transfers between devices, exchange(): return lax.all_to_all(rows, 'list', split_axis=0, concat_axis=0, tiled=True)  42.4 us
    pallas_call x3, Pallas kernels, residual_rows(): pl.pallas_call(body, grid_spec=pltpu.PrefetchScalarGridSpec(num_scalar_pr...  34.8 us
    ppermute x27, starting transfers between devices, swap(): return lax.ppermute(rows, axis, [(i, i ^ offset) for i in range(count)])  34.5 us
    all_to_all x6, waiting for transfers between devices, exchange(): return lax.all_to_all(rows, 'list', split_axis=0, concat_axis=0, tiled=True)  12.8 us
    pallas_call x3, Pallas kernels, unpack_rows(): pl.pallas_call(body, grid=(1,), in_specs=in_specs, out_specs=pl.BlockSpec...  11.8 us
    pallas_call x3, Pallas kernels, list_sums(): pl.pallas_call(body, grid=(1,), in_specs=[pl.BlockSpec((1, 1, rows), lamb...  11.8 us
    pallas_call x3, Pallas kernels, pack_rows(): pl.pallas_call(body, grid=(owners // group,), in_specs=[pl.BlockSpec((1,...  10.9 us
  transfers between devices with their start and end apart: 33, of which 18 were waited for; matrix products, arithmetic and copies ran while one was open for 6% of the time, Pallas kernels for 31%

profile of v5, /device:TPU:2, one launch (start us, length us, event | category | flops | bytes accessed | tf_op | source)
XLA Modules:
  0.0 242.4 jit_solution(8248981734886821572)
XLA Ops:
  4.5 7.6 %all-to-all-start = ((s32[32,1,96]{2,1,0:T(1,128)}), s32[32,1,96]{2,1,0:T(1,128)S(1)}, u32[]{:S(2)}, u32[]{:S(2)}) async-start(s32[32,1,96]{2,1,0:T(1,128)} %bitcast.8), calls=%async_computation | async-start | bytes 32768 | tf_op jit(solution)/shard_map/all_to_all | solution.py:305
  18.2 5.7 %all-to-all-start.1 = ((bf16[32,1,32,1024]{3,2,1,0:T(8,128)(2,1)}), bf16[32,1,32,1024]{3,2,1,0:T(8,128)(2,1)S(1)}, u32[]{:S(2)}, u32[]{:S(2)}) async-start(bf16[32,1,32,1024]{3,2,1,0:T(8,128)(2,1)} %pack_rows.5), calls=%async_computation.1 | async-start | bytes 4194304 | tf_op jit(solution)/shard_map/all_to_all | solution.py:305
  27.3 4.1 %collective-permute-start.2 = (s32[3,1024]{1,0:T(4,128)S(1)}, s32[3,1024]{1,0:T(4,128)S(1)}, u32[]{:S(2)}, u32[]{:S(2)}) collective-permute-start(s32[3,1024]{1,0:T(4,128)S(1)} %convert_reduce_fusion), channel_id=1, source_target_pairs={{0,96},{32,64},{64,32},{96,0},{1,97},{33,65},{65,33},{97,1},{2,98}... | collective-permute-start | bytes 36872 | tf_op jit(solution)/shard_map/ppermute | solution.py:19
  40.8 11.1 %all-to-all-done.1.row_ref = bf16[32,1,32,1024]{3,2,1,0:T(8,128)(2,1)S(1)} async-done(((bf16[32,1,32,1024]{3,2,1,0:T(8,128)(2,1)}), bf16[32,1,32,1024]{3,2,1,0:T(8,128)(2,1)S(1)}, u32[]{:S(2)}, u32[]{:S(2)}) %all-to-all-start.1) | async-done | bytes 2097184 | tf_op jit(solution)/shard_map/all_to_all | solution.py:305
  51.8 6.7 %all-to-all-start.2 = ((bf16[32,1,32,1024]{3,2,1,0:T(8,128)(2,1)}), bf16[32,1,32,1024]{3,2,1,0:T(8,128)(2,1)}, u32[]{:S(2)}, u32[]{:S(2)}) async-start(bf16[32,1,32,1024]{3,2,1,0:T(8,128)(2,1)} %pack_rows.3), calls=%async_computation.2 | async-start | bytes 4194304 | tf_op jit(solution)/shard_map/all_to_all | solution.py:305
  68.3 10.2 %residual_rows.3 = bf16[32,2,32,1024]{3,2,1,0:T(8,128)(2,1)} custom-call(s32[2]{0:T(128)} %pad_add_fusion.place_ref, s32[1024,3]{1,0:T(8,128)} %bitcast.32, bf16[32,1,32,1024]{3,2,1,0:T(8,128)(2,1)} %copy-done, f32[1024,1024]{1,0:T(8,128)} %table_ref.9, f32[1024,4]{1,0:T(8,128)} %bitcast.26, ...), custom_call_target="tpu_custom_call", output_to_operand_aliasing={{}: (5, {})} | custom-call | flops 1 | bytes 1 | tf_op jit(solution)/shard_map/residual_rows/pallas_call | solution.py:172
  83.5 4.1 %collective-permute-done.6 = bf16[128,1024]{1,0:T(8,128)(2,1)S(1)} collective-permute-done((bf16[128,1024]{1,0:T(8,128)(2,1)S(1)}, bf16[128,1024]{1,0:T(8,128)(2,1)S(1)}, u32[]{:S(2)}, u32[]{:S(2)}) %collective-permute-start.6) | collective-permute-done | bytes 262176 | tf_op jit(solution)/shard_map/ppermute | solution.py:19
  89.9 7.6 %all-to-all-start.3 = ((bf16[32,2,32,1024]{3,2,1,0:T(8,128)(2,1)}), bf16[32,2,32,1024]{3,2,1,0:T(8,128)(2,1)}, u32[]{:S(2)}, u32[]{:S(2)}) async-start(bf16[32,2,32,1024]{3,2,1,0:T(8,128)(2,1)} %residual_rows.3), calls=%async_computation.3 | async-start | bytes 8388608 | tf_op jit(solution)/shard_map/all_to_all | solution.py:305
  99.6 7.5 %collective-permute-done.7 = bf16[128,1024]{1,0:T(8,128)(2,1)S(1)} collective-permute-done((bf16[128,1024]{1,0:T(8,128)(2,1)S(1)}, bf16[128,1024]{1,0:T(8,128)(2,1)S(1)}, u32[]{:S(2)}, u32[]{:S(2)}) %collective-permute-start.7) | collective-permute-done | bytes 262176 | tf_op jit(solution)/shard_map/ppermute | solution.py:19
  109.4 3.9 %list_sums.4 = (bf16[128,1024]{1,0:T(8,128)(2,1)S(1)}, bf16[128,1024]{1,0:T(8,128)(2,1)S(1)}, bf16[256,1024]{1,0:T(8,128)(2,1)S(1)}, bf16[128,1024]{1,0:T(8,128)...) custom-call(s32[3,1,1024]{2,1,0:T(1,128)} %compare_select_fusion.1.slot_ref, ...), custom_call_target="tpu_custom_call" | custom-call | flops 1 | bytes 1 | tf_op jit(solution)/shard_map/list_sums/pallas_call | solution.py:70
  113.4 7.5 %collective-permute-done.9.rest_1_.rest_0_ = bf16[256,1024]{1,0:T(8,128)(2,1)} collective-permute-done((bf16[256,1024]{1,0:T(8,128)(2,1)S(1)}, bf16[256,1024]{1,0:T(8,128)(2,1)}, u32[]{:S(2)}, u32[]{:S(2)}) %collective-permute-start.9) | collective-permute-done | bytes 524320 | tf_op jit(solution)/shard_map/ppermute | solution.py:19
  124.5 12.0 %residual_rows.4 = bf16[32,1,32,1024]{3,2,1,0:T(8,128)(2,1)} custom-call(s32[2]{0:T(128)} %pad_add_fusion.place_ref, s32[1024,3]{1,0:T(8,128)} %bitcast.33, bf16[32,1,32,1024]{3,2,1,0:T(8,128)(2,1)} %all-to-all-done.2.row_ref, f32[1024,1024]{1,0:T(8,128)} %table_ref.9, f32[1024,4]{1,0:T(8,128)} %bitcast.27, bf16[256,1024]{1,0:T(8,128)(2,1)} %copy-done.2, ...), custom_call_target="tpu_custom_call" | custom-call | flops 1 | bytes 1 | tf_op jit(solution)/shard_map/residual_rows/pallas_call | solution.py:172
  151.5 4.4 %collective-permute-done.14 = bf16[128,1024]{1,0:T(8,128)(2,1)S(1)} collective-permute-done((bf16[128,1024]{1,0:T(8,128)(2,1)S(1)}, bf16[128,1024]{1,0:T(8,128)(2,1)S(1)}, u32[]{:S(2)}, u32[]{:S(2)}) %collective-permute-start.14) | collective-permute-done | bytes 262176 | tf_op jit(solution)/shard_map/ppermute | solution.py:19
  156.0 7.4 %all-to-all-start.4 = ((bf16[32,1,32,1024]{3,2,1,0:T(8,128)(2,1)}), bf16[32,1,32,1024]{3,2,1,0:T(8,128)(2,1)}, u32[]{:S(2)}, u32[]{:S(2)}) async-start(bf16[32,1,32,1024]{3,2,1,0:T(8,128)(2,1)} %residual_rows.4), calls=%async_computation.4 | async-start | bytes 4194304 | tf_op jit(solution)/shard_map/all_to_all | solution.py:305
  165.2 3.9 %list_sums.5 = (bf16[128,1024]{1,0:T(8,128)(2,1)S(1)}, bf16[128,1024]{1,0:T(8,128)(2,1)S(1)}, bf16[256,1024]{1,0:T(8,128)(2,1)S(1)}, bf16[128,1024]{1,0:T(8,128)...) custom-call(s32[3,1,1024]{2,1,0:T(1,128)} %compare_select_fusion.1.slot_ref, ...), custom_call_target="tpu_custom_call" | custom-call | flops 1 | bytes 1 | tf_op jit(solution)/shard_map/list_sums/pallas_call | solution.py:70
  172.2 4.0 %unpack_rows.3.rest_0_ = bf16[3,512,1024]{2,1,0:T(8,128)(2,1)} custom-call(s32[512,3]{1,0:T(8,128)} %bitcast.35, bf16[32,2,32,1024]{3,2,1,0:T(8,128)(2,1)} %all-to-all-done.3.row_ref), custom_call_target="tpu_custom_call" | custom-call | flops 1 | bytes 1 | tf_op jit(solution)/shard_map/unpack_rows/pallas_call | solution.py:266
  179.7 12.6 %residual_rows.5 = bf16[32,1,32,1024]{3,2,1,0:T(8,128)(2,1)} custom-call(s32[2]{0:T(128)} %pad_add_fusion.place_ref, s32[1024,3]{1,0:T(8,128)} %bitcast.34, bf16[32,2,32,1024]{3,2,1,0:T(8,128)(2,1)} %all-to-all-done.3.row_ref, f32[1024,1024]{1,0:T(8,128)} %table_ref.9, f32[1024,4]{1,0:T(8,128)} %bitcast.28, bf16[256,1024]{1,0:T(8,128)(2,1)} %copy-done.2, ...), custom_call_target="tpu_custom_call" | custom-call | flops 1 | bytes 1 | tf_op jit(solution)/shard_map/residual_rows/pallas_call | solution.py:172
  192.4 7.4 %all-to-all-start.5 = ((bf16[32,1,32,1024]{3,2,1,0:T(8,128)(2,1)}), bf16[32,1,32,1024]{3,2,1,0:T(8,128)(2,1)S(1)}, u32[]{:S(2)}, u32[]{:S(2)}) async-start(bf16[32,1,32,1024]{3,2,1,0:T(8,128)(2,1)} %residual_rows.5), calls=%async_computation.5 | async-start | bytes 4194304 | tf_op jit(solution)/shard_map/all_to_all | solution.py:305
  203.7 6.7 %collective-permute-done.21 = bf16[128,1024]{1,0:T(8,128)(2,1)S(1)} collective-permute-done((bf16[128,1024]{1,0:T(8,128)(2,1)S(1)}, bf16[128,1024]{1,0:T(8,128)(2,1)S(1)}, u32[]{:S(2)}, u32[]{:S(2)}) %collective-permute-start.21) | collective-permute-done | bytes 262176 | tf_op jit(solution)/shard_map/ppermute | solution.py:19
  214.4 6.0 %collective-permute-done.22 = bf16[128,1024]{1,0:T(8,128)(2,1)S(1)} collective-permute-done((bf16[128,1024]{1,0:T(8,128)(2,1)S(1)}, bf16[128,1024]{1,0:T(8,128)(2,1)S(1)}, u32[]{:S(2)}, u32[]{:S(2)}) %collective-permute-start.22) | collective-permute-done | bytes 262176 | tf_op jit(solution)/shard_map/ppermute | solution.py:19
  223.5 3.9 %unpack_rows.4.rest_0_ = bf16[3,512,1024]{2,1,0:T(8,128)(2,1)} custom-call(s32[512,3]{1,0:T(8,128)} %bitcast.36, bf16[32,1,32,1024]{3,2,1,0:T(8,128)(2,1)} %all-to-all-done.4.row_ref, bf16[3,512,1024]{2,1,0:T(8,128)(2,1)} %unpack_rows.3.rest_0_), custom_call_target="tpu_custom_call", output_to_operand_aliasing={{}: (2, {})} | custom-call | flops 1 | bytes 1 | tf_op jit(solution)/shard_map/unpack_rows/pallas_call | solution.py:266
  227.4 4.8 %new_rows.2.rest_6_ = f32[1024,1024]{1,0:T(8,128)} custom-call(s32[2]{0:T(128)} %pad_add_fusion.place_ref, f32[1024,1024]{1,0:T(8,128)} %table_ref.9, f32[1024,4]{1,0:T(8,128)} %bitcast.29, bf16[256,1024]{1,0:T(8,128)(2,1)} %copy-done.2, bf16[256,1024]{1,0:T(8,128)(2,1)} %copy-done.3, bf16[256,1024]{1,0:T(8,128)(2,1)} %copy-done.7, ...), custom_call_target="tpu_custom_call" | custom-call | flops 1 | bytes 1 | tf_op jit(solution)/shard_map/new_rows/pallas_call | solution.py:231
  233.7 3.9 %unpack_rows.5 = bf16[3,512,1024]{2,1,0:T(8,128)(2,1)} custom-call(s32[512,3]{1,0:T(8,128)} %bitcast.37, bf16[32,1,32,1024]{3,2,1,0:T(8,128)(2,1)} %copy-done.4, bf16[3,512,1024]{2,1,0:T(8,128)(2,1)} %unpack_rows.4.rest_0_), custom_call_target="tpu_custom_call", output_to_operand_aliasing={{}: (2, {})} | custom-call | flops 1 | bytes 1 | tf_op jit(solution)/shard_map/unpack_rows/pallas_call | solution.py:266
  237.6 4.8 %new_rows.3 = f32[1024,1024]{1,0:T(8,128)} custom-call(s32[2]{0:T(128)} %pad_add_fusion.place_ref, f32[1024,1024]{1,0:T(8,128)} %table_ref.9, f32[1024,4]{1,0:T(8,128)} %bitcast.30, bf16[256,1024]{1,0:T(8,128)(2,1)} %collective-permute-done.9.rest_1_.rest_0_, ...), custom_call_target="tpu_custom_call", output_to_operand_aliasing={{}: (9, {})} | custom-call | flops 1 | bytes 1 | tf_op jit(solution)/shard_map/new_rows/pallas_call | solution.py:231
  (125 shorter events, 83.3 us)
Async XLA Ops:
  4.5 13.7 %all-to-all-start = ((s32[32,1,96]{2,1,0:T(1,128)}), s32[32,1,96]{2,1,0:T(1,128)S(1)}, u32[]{:S(2)}, u32[]{:S(2)}) async-start(s32[32,1,96]{2,1,0:T(1,128)} %bitcast.8), calls=%async_computation | async-start | bytes 32768 | tf_op jit(solution)/shard_map/all_to_all | solution.py:305
  18.2 33.6 %all-to-all-start.1 = ((bf16[32,1,32,1024]{3,2,1,0:T(8,128)(2,1)}), bf16[32,1,32,1024]{3,2,1,0:T(8,128)(2,1)S(1)}, u32[]{:S(2)}, u32[]{:S(2)}) async-start(bf16[32,1,32,1024]{3,2,1,0:T(8,128)(2,1)} %pack_rows.5), calls=%async_computation.1 | async-start | bytes 4194304 | tf_op jit(solution)/shard_map/all_to_all | solution.py:305
  27.3 12.4 %collective-permute-start.2 = (s32[3,1024]{1,0:T(4,128)S(1)}, s32[3,1024]{1,0:T(4,128)S(1)}, u32[]{:S(2)}, u32[]{:S(2)}) collective-permute-start(s32[3,1024]{1,0:T(4,128)S(1)} %convert_reduce_fusion), channel_id=1, source_target_pairs={{0,96},{32,64},{64,32},{96,0},{1,97},{33,65},{65,33},{97,1},{2,98}... | collective-permute-start | bytes 36872 | tf_op jit(solution)/shard_map/ppermute | solution.py:19
  51.8 38.1 %all-to-all-start.2 = ((bf16[32,1,32,1024]{3,2,1,0:T(8,128)(2,1)}), bf16[32,1,32,1024]{3,2,1,0:T(8,128)(2,1)}, u32[]{:S(2)}, u32[]{:S(2)}) async-start(bf16[32,1,32,1024]{3,2,1,0:T(8,128)(2,1)} %pack_rows.3), calls=%async_computation.2 | async-start | bytes 4194304 | tf_op jit(solution)/shard_map/all_to_all | solution.py:305
  63.2 15.3 %collective-permute-start.3 = (bf16[256,1024]{1,0:T(8,128)(2,1)S(1)}, bf16[256,1024]{1,0:T(8,128)(2,1)S(1)}, u32[]{:S(2)}, u32[]{:S(2)}) collective-permute-start(bf16[256,1024]{1,0:T(8,128)(2,1)S(1)} %get-tuple-element.70), channel_id=1, source_target_pairs={{0,32},{32,0},{64,96},{96,64},{1,33},{33,1},{65,97},{97,65},{2,34}... | collective-permute-start | bytes 1572872 | tf_op jit(solution)/shard_map/ppermute | solution.py:19
  65.2 14.9 %collective-permute-start.4 = (bf16[256,1024]{1,0:T(8,128)(2,1)S(1)}, bf16[256,1024]{1,0:T(8,128)(2,1)S(1)}, u32[]{:S(2)}, u32[]{:S(2)}) collective-permute-start(bf16[256,1024]{1,0:T(8,128)(2,1)S(1)} %get-tuple-element.71), channel_id=1, source_target_pairs={{0,96},{32,64},{64,32},{96,0},{1,97},{33,65},{65,33},{97,1},{2,98}... | collective-permute-start | bytes 1572872 | tf_op jit(solution)/shard_map/ppermute | solution.py:19
  80.9 8.8 %collective-permute-start.5 = (bf16[128,1024]{1,0:T(8,128)(2,1)S(1)}, bf16[128,1024]{1,0:T(8,128)(2,1)S(1)}, u32[]{:S(2)}, u32[]{:S(2)}) collective-permute-start(bf16[128,1024]{1,0:T(8,128)(2,1)S(1)} %add_convert_fusion.11), channel_id=1, source_target_pairs={{0,96},{32,64},{64,32},{96,0},{1,97},{33,65},{65,33},{97,1},{2,98}... | collective-permute-start | bytes 786440 | tf_op jit(solution)/shard_map/ppermute | solution.py:19
  89.9 66.1 %all-to-all-start.3 = ((bf16[32,2,32,1024]{3,2,1,0:T(8,128)(2,1)}), bf16[32,2,32,1024]{3,2,1,0:T(8,128)(2,1)}, u32[]{:S(2)}, u32[]{:S(2)}) async-start(bf16[32,2,32,1024]{3,2,1,0:T(8,128)(2,1)} %residual_rows.3), calls=%async_computation.3 | async-start | bytes 8388608 | tf_op jit(solution)/shard_map/all_to_all | solution.py:305
  97.5 9.7 %collective-permute-start.7 = (bf16[128,1024]{1,0:T(8,128)(2,1)S(1)}, bf16[128,1024]{1,0:T(8,128)(2,1)S(1)}, u32[]{:S(2)}, u32[]{:S(2)}) collective-permute-start(bf16[128,1024]{1,0:T(8,128)(2,1)S(1)} %add_convert_fusion.10), channel_id=1, source_target_pairs={{0,96},{32,64},{64,32},{96,0},{1,97},{33,65},{65,33},{97,1},{2,98}... | collective-permute-start | bytes 786440 | tf_op jit(solution)/shard_map/ppermute | solution.py:19
  107.7 13.1 %collective-permute-start.9 = (bf16[256,1024]{1,0:T(8,128)(2,1)S(1)}, bf16[256,1024]{1,0:T(8,128)(2,1)}, u32[]{:S(2)}, u32[]{:S(2)}) collective-permute-start(bf16[256,1024]{1,0:T(8,128)(2,1)S(1)} %pad_maximum_fusion.rest_0_), channel_id=1, source_target_pairs={{0,32},{32,0},{64,96},{96,64},{1,33},{33,1},{65,97},{97,65},{2,34}... | collective-permute-start | bytes 1572872 | tf_op jit(solution)/shard_map/ppermute | solution.py:19
  108.1 14.3 %collective-permute-start.10 = (bf16[256,1024]{1,0:T(8,128)(2,1)S(1)}, bf16[256,1024]{1,0:T(8,128)(2,1)}, u32[]{:S(2)}, u32[]{:S(2)}) collective-permute-start(bf16[256,1024]{1,0:T(8,128)(2,1)S(1)} %pad_maximum_fusion.1.rest_2_.rest_1_), channel_id=1, source_target_pairs={{0,96},{32,64},{64,32},{96,0},{1,97},{33,65},{65,33},{97,1},{2,98}... | collective-permute-start | bytes 1572872 | tf_op jit(solution)/shard_map/ppermute | solution.py:19
  122.4 14.1 %collective-permute-start.11 = (bf16[256,1024]{1,0:T(8,128)(2,1)S(1)}, bf16[256,1024]{1,0:T(8,128)(2,1)}, u32[]{:S(2)}, u32[]{:S(2)}) collective-permute-start(bf16[256,1024]{1,0:T(8,128)(2,1)S(1)} %get-tuple-element.96), channel_id=1, source_target_pairs={{0,32},{32,0},{64,96},{96,64},{1,33},{33,1},{65,97},{97,65},{2,34}... | collective-permute-start | bytes 1572872 | tf_op jit(solution)/shard_map/ppermute | solution.py:19
  122.6 13.8 %collective-permute-start.12 = (bf16[256,1024]{1,0:T(8,128)(2,1)S(1)}, bf16[256,1024]{1,0:T(8,128)(2,1)}, u32[]{:S(2)}, u32[]{:S(2)}) collective-permute-start(bf16[256,1024]{1,0:T(8,128)(2,1)S(1)} %get-tuple-element.97), channel_id=1, source_target_pairs={{0,96},{32,64},{64,32},{96,0},{1,97},{33,65},{65,33},{97,1},{2,98}... | collective-permute-start | bytes 1572872 | tf_op jit(solution)/shard_map/ppermute | solution.py:19
  156.0 36.4 %all-to-all-start.4 = ((bf16[32,1,32,1024]{3,2,1,0:T(8,128)(2,1)}), bf16[32,1,32,1024]{3,2,1,0:T(8,128)(2,1)}, u32[]{:S(2)}, u32[]{:S(2)}) async-start(bf16[32,1,32,1024]{3,2,1,0:T(8,128)(2,1)} %residual_rows.4), calls=%async_computation.4 | async-start | bytes 4194304 | tf_op jit(solution)/shard_map/all_to_all | solution.py:305
  163.4 15.0 %collective-permute-start.17 = (bf16[256,1024]{1,0:T(8,128)(2,1)S(1)}, bf16[256,1024]{1,0:T(8,128)(2,1)}, u32[]{:S(2)}, u32[]{:S(2)}) collective-permute-start(bf16[256,1024]{1,0:T(8,128)(2,1)S(1)} %pad_maximum_fusion.2.rest_4_.rest_2_), channel_id=1, source_target_pairs={{0,32},{32,0},{64,96},{96,64},{1,33},{33,1},{65,97},{97,65},{2,34}... | collective-permute-start | bytes 1572872 | tf_op jit(solution)/shard_map/ppermute | solution.py:19
  163.5 16.2 %collective-permute-start.18 = (bf16[256,1024]{1,0:T(8,128)(2,1)S(1)}, bf16[256,1024]{1,0:T(8,128)(2,1)}, u32[]{:S(2)}, u32[]{:S(2)}) collective-permute-start(bf16[256,1024]{1,0:T(8,128)(2,1)S(1)} %pad_maximum_fusion.3.rest_6_.rest_3_), channel_id=1, source_target_pairs={{0,96},{32,64},{64,32},{96,0},{1,97},{33,65},{65,33},{97,1},{2,98}... | collective-permute-start | bytes 1572872 | tf_op jit(solution)/shard_map/ppermute | solution.py:19
  169.2 23.2 %collective-permute-start.19 = (bf16[256,1024]{1,0:T(8,128)(2,1)S(1)}, bf16[256,1024]{1,0:T(8,128)(2,1)}, u32[]{:S(2)}, u32[]{:S(2)}) collective-permute-start(bf16[256,1024]{1,0:T(8,128)(2,1)S(1)} %get-tuple-element.109), channel_id=1, source_target_pairs={{0,32},{32,0},{64,96},{96,64},{1,33},{33,1},{65,97},{97,65},{2,34}... | collective-permute-start | bytes 1572872 | tf_op jit(solution)/shard_map/ppermute | solution.py:19
  170.6 21.8 %collective-permute-start.20 = (bf16[256,1024]{1,0:T(8,128)(2,1)S(1)}, bf16[256,1024]{1,0:T(8,128)(2,1)}, u32[]{:S(2)}, u32[]{:S(2)}) collective-permute-start(bf16[256,1024]{1,0:T(8,128)(2,1)S(1)} %get-tuple-element.110), channel_id=1, source_target_pairs={{0,96},{32,64},{64,32},{96,0},{1,97},{33,65},{65,33},{97,1},{2,98}... | collective-permute-start | bytes 1572872 | tf_op jit(solution)/shard_map/ppermute | solution.py:19
  192.4 39.9 %all-to-all-start.5 = ((bf16[32,1,32,1024]{3,2,1,0:T(8,128)(2,1)}), bf16[32,1,32,1024]{3,2,1,0:T(8,128)(2,1)S(1)}, u32[]{:S(2)}, u32[]{:S(2)}) async-start(bf16[32,1,32,1024]{3,2,1,0:T(8,128)(2,1)} %residual_rows.5), calls=%async_computation.5 | async-start | bytes 4194304 | tf_op jit(solution)/shard_map/all_to_all | solution.py:305
  200.8 9.7 %collective-permute-start.21 = (bf16[128,1024]{1,0:T(8,128)(2,1)S(1)}, bf16[128,1024]{1,0:T(8,128)(2,1)S(1)}, u32[]{:S(2)}, u32[]{:S(2)}) collective-permute-start(bf16[128,1024]{1,0:T(8,128)(2,1)S(1)} %add_convert_fusion.3), channel_id=1, source_target_pairs={{0,96},{32,64},{64,32},{96,0},{1,97},{33,65},{65,33},{97,1},{2,98}... | collective-permute-start | bytes 786440 | tf_op jit(solution)/shard_map/ppermute | solution.py:19
  203.5 9.7 %collective-permute-start.23 = (bf16[128,1024]{1,0:T(8,128)(2,1)S(1)}, bf16[128,1024]{1,0:T(8,128)(2,1)S(1)}, u32[]{:S(2)}, u32[]{:S(2)}) collective-permute-start(bf16[128,1024]{1,0:T(8,128)(2,1)S(1)} %add_convert_fusion.1), channel_id=1, source_target_pairs={{0,32},{32,0},{64,96},{96,64},{1,33},{33,1},{65,97},{97,65},{2,34}... | collective-permute-start | bytes 786440 | tf_op jit(solution)/shard_map/ppermute | solution.py:19
  211.5 8.8 %collective-permute-start.22 = (bf16[128,1024]{1,0:T(8,128)(2,1)S(1)}, bf16[128,1024]{1,0:T(8,128)(2,1)S(1)}, u32[]{:S(2)}, u32[]{:S(2)}) collective-permute-start(bf16[128,1024]{1,0:T(8,128)(2,1)S(1)} %add_convert_fusion.2), channel_id=1, source_target_pairs={{0,96},{32,64},{64,32},{96,0},{1,97},{33,65},{65,33},{97,1},{2,98}... | collective-permute-start | bytes 786440 | tf_op jit(solution)/shard_map/ppermute | solution.py:19
  220.4 17.2 %collective-permute-start.25 = (bf16[256,1024]{1,0:T(8,128)(2,1)S(1)}, bf16[256,1024]{1,0:T(8,128)(2,1)}, u32[]{:S(2)}, u32[]{:S(2)}) collective-permute-start(bf16[256,1024]{1,0:T(8,128)(2,1)S(1)} %pad_maximum_fusion.4.rest_4_), channel_id=1, source_target_pairs={{0,32},{32,0},{64,96},{96,64},{1,33},{33,1},{65,97},{97,65},{2,34}... | collective-permute-start | bytes 1572872 | tf_op jit(solution)/shard_map/ppermute | solution.py:19
  221.7 15.9 %collective-permute-start.26 = (bf16[256,1024]{1,0:T(8,128)(2,1)S(1)}, bf16[256,1024]{1,0:T(8,128)(2,1)}, u32[]{:S(2)}, u32[]{:S(2)}) collective-permute-start(bf16[256,1024]{1,0:T(8,128)(2,1)S(1)} %pad_maximum_fusion.5.rest_5_), channel_id=1, source_target_pairs={{0,96},{32,64},{64,32},{96,0},{1,97},{33,65},{65,33},{97,1},{2,98}... | collective-permute-start | bytes 1572872 | tf_op jit(solution)/shard_map/ppermute | solution.py:19
  (20 other events, 186.9 us)
